TPU v7x, 32 devices: a whole 2x2x4 slice. The times are simulated.
32 devices in a mesh: net: 8 (over z, x), mem: 4 (over y, core).
Axes of the slice: x: 2, y: 2, z: 4, core: 2. Of those that a mesh axis runs over, the one named last changes fastest.
Arguments:
- stored_reach_flows: bfloat16 [5, 128, 32768], P(None, 'mem', 'net'), may hold values from 0.19921875 to 5
- lateral: bfloat16 [4, 128, 32768], P(None, 'mem', 'net'), may hold values from 0.049804688 to 1
- cotangent: bfloat16 [4, 128, 32768], P(None, 'mem', 'net'), may hold values from -3 to 3
- roughness: float32 [32768], P('net'), may hold values from 0.02 to 0.1
- travel_factor: float32 [32768], P('net'), may hold values from 0.2 to 5
- inverse_block_matrix: float32 [256, 128, 128], P('net'), may hold values from 0 to 1, as said below
- down_in_block: int32 [32768], P('net'), may hold values from 1 to 128, as said below
- exit_slot: int32 [32768], P('net'), may hold values from -1 to 127, as said below
- inlet_reach: int32 [8, 128], P('net'), may hold values from 1 to 3999, as said below
Outputs:
- grad_lateral: bfloat16 [4, 128, 32768], P(None, 'mem', 'net')
- grad_rough: float32 [32768], P(('net', 'mem'))
Inputs may be any that keep to these rules, and one draw needn't show every extreme that they name: Within a block a reach feeds a later position: down_in_block[r] > r % 128 where it is under 128. exit_slot[r] >= 0 only where down_in_block[r] == 128 and r is not in the last partition; every reach of the last partition has -1. `inlet_reach`: each entry is a reach at positions 1 to 31 of some block of that partition; several slots may name the same reach. inverse_block_matrix[k][i, j] is 1 where i = j, the product of weight_new over the reaches after j up to and including i where i lies on the in-block path of next reaches from j, and 0 elsewhere.
All inputs are finite; a program needn't handle non-finite values.
Results may differ from a plain program's by a relative error of at most 0.001.
Values sent between devices are 32-bit elements; how exact they have to be, the bound alone decides.
No kernel may reach another device: no remote copies, remote signals or barrier semaphores. Data moves between devices by JAX's collectives and lax.ppermute only.
A program may use at most 64 MiB of HBM per device.

v0:
```python
import jax
import jax.numpy as jnp
from jax import lax
from jax.sharding import PartitionSpec as P

skew_weight = 0.2


def from_behind(value, axis, by):
    count = lax.axis_size(axis)
    pairs = [(i, i + by) for i in range(count) if 0 <= i + by < count]
    return lax.ppermute(value, axis, pairs)


def coefficients(roughness, travel_factor):
    travel = roughness * travel_factor
    divisor = travel * (1.0 - skew_weight) + 0.5
    weight_new = (0.5 - travel * skew_weight) / divisor
    weight_old = (0.5 + travel * skew_weight) / divisor
    weight_stay = (travel * (1.0 - skew_weight) - 0.5) / divisor
    weight_side = 1.0 / divisor
    square = divisor * divisor
    updated_slope = -0.5 / square
    slope_old = (skew_weight - 0.5) / square
    slope_stay = (1.0 - skew_weight) / square
    slope_side = (skew_weight - 1.0) / square
    return (
        (weight_new, weight_old, weight_stay, weight_side),
        (updated_slope, slope_old, slope_stay, slope_side),
    )


def solve_blocks(right_side, inverse_block_matrix):
    members, reaches = right_side.shape
    reshaped_values = right_side.reshape(members, reaches // 128, 128)
    solved_adjoint = jnp.einsum(
        "acj,cjv->acv", reshaped_values, inverse_block_matrix, precision=lax.Precision.HIGHEST
    )
    return solved_adjoint.reshape(members, reaches)


def body(
    stored_reach_flows,
    lateral,
    cotangent,
    roughness,
    travel_factor,
    inverse_block_matrix,
    down_in_block,
    exit_slot,
    inlet_reach,
):
    step_count = cotangent.shape[0]
    members = stored_reach_flows.shape[1]
    reaches = stored_reach_flows.shape[2]
    blocks = reaches // 128
    slot_count = inlet_reach.shape[1]
    weights, slopes = coefficients(roughness, travel_factor)
    weight_new, weight_old, weight_stay, weight_side = weights
    updated_slope, slope_old, slope_stay, slope_side = slopes
    positions = jnp.arange(128, dtype=jnp.int32)
    within_table = down_in_block.reshape(blocks, 128)[:, :, None] == positions[None, None, :]
    within = within_table.astype(jnp.bfloat16)
    exact_within_partition = within_table.astype(jnp.float32)
    local_in = jnp.einsum(
        "lmbu,bur->lmbr",
        stored_reach_flows.reshape(step_count + 1, members, blocks, 128),
        within,
        preferred_element_type=jnp.float32,
    ).reshape(step_count + 1, members, reaches)
    slot_table = exit_slot[:, None] == jnp.arange(slot_count, dtype=jnp.int32)[None, :]
    leaving_flow = slot_table.astype(jnp.bfloat16)
    leaving_exact = slot_table.astype(jnp.float32).T
    reach_outflow = jnp.einsum(
        "gcq,qj->gcj", stored_reach_flows, leaving_flow, preferred_element_type=jnp.float32
    )
    arriving_flow = from_behind(reach_outflow, "net", 1)
    inlets = inlet_reach[0]
    placement_rows = (inlets[:, None] == jnp.arange(reaches, dtype=jnp.int32)[None, :]).astype(
        jnp.float32
    )
    inflow = local_in + jnp.einsum(
        "dqe,ej->dqj", arriving_flow, placement_rows, precision=lax.Precision.HIGHEST
    )
    weight_new_in = weight_new[inlets]
    weight_old_in = weight_old[inlets]

    def from_below(values):
        return jnp.dot(
            values,
            leaving_exact,
            precision=lax.Precision.HIGHEST,
            preferred_element_type=jnp.float32,
        )

    def inlet_rows(adjoint):
        adjoint_inlet = jnp.einsum(
            "mr,er->me", adjoint, placement_rows, precision=lax.Precision.HIGHEST
        )
        return jnp.stack([weight_new_in * adjoint_inlet, weight_old_in * adjoint_inlet])

    zero_slots = jnp.zeros((members, slot_count), jnp.float32)
    running = jnp.zeros((reaches,), jnp.float32)
    adjoint_next = jnp.zeros((members, reaches), jnp.float32)
    remote_prior = zero_slots
    outputs = [None] * step_count
    for counter in range(step_count):
        current_instant = step_count - counter
        weighted_flows = (weight_old * adjoint_next).reshape(members, blocks, 128)
        interior_reaches = jnp.einsum(
            "qvt,vzt->qvz", weighted_flows, exact_within_partition, precision=lax.Precision.HIGHEST
        )
        source = (
            cotangent[current_instant - 1].astype(jnp.float32)
            + weight_stay * adjoint_next
            + (interior_reaches.reshape(members, reaches) + from_below(remote_prior))
        )

        def one_section(section_id, carry):
            adjoint, remote_new, remote_old = carry
            adjoint = solve_blocks(source + from_below(remote_new), inverse_block_matrix)
            received = from_behind(inlet_rows(adjoint), "net", -1)
            return (adjoint, received[0], received[1])

        adjoint, remote_new, remote_old = lax.fori_loop(
            0,
            lax.axis_size("net"),
            one_section,
            (jnp.zeros_like(adjoint_next), zero_slots, zero_slots),
        )
        inflow_now = lax.dynamic_index_in_dim(inflow, current_instant, 0, False)
        inflow_prior = lax.dynamic_index_in_dim(inflow, current_instant - 1, 0, False)
        flows_prior = lax.dynamic_index_in_dim(
            stored_reach_flows, current_instant - 1, 0, False
        ).astype(jnp.float32)
        forcing = lax.dynamic_index_in_dim(lateral, current_instant - 1, 0, False).astype(
            jnp.float32
        )
        factor = (
            updated_slope * inflow_now
            + slope_old * inflow_prior
            + slope_stay * flows_prior
            + slope_side * forcing
        )
        part_sum = jnp.sum(adjoint * factor, axis=0)
        lateral_grad = (weight_side * adjoint).astype(jnp.bfloat16)
        running = running + part_sum
        outputs[current_instant - 1] = lateral_grad
        adjoint_next = adjoint
        remote_prior = remote_old
    grad_lateral = jnp.stack(outputs)
    grad_rough = lax.psum_scatter(travel_factor * running, "mem", scatter_dimension=0, tiled=True)
    return (grad_lateral, grad_rough)


def solution(mesh):
    in_specs = (
        P(None, "mem", "net"),
        P(None, "mem", "net"),
        P(None, "mem", "net"),
        P("net"),
        P("net"),
        P("net", None, None),
        P("net"),
        P("net"),
        P("net", None),
    )
    out_specs = (P(None, "mem", "net"), P(("net", "mem")))
    return jax.shard_map(body, mesh=mesh, in_specs=in_specs, out_specs=out_specs, check_vma=False)
```

profile of v0, /device:TPU:0, one launch (start us, length us, event | category | flops | bytes accessed | tf_op | source)
XLA Modules:
  0.0 499.4 jit_solution(17685390303827762844)
XLA Ops:
  27.0 107.4 %while.58 = (s32[]{:T(128)}, f32[32,4096]{1,0:T(8,128)}, f32[32,128]{1,0:T(8,128)S(1)}, f32[32,128]{1,0:T(8,128)}, f32[32,4096]{1,0:T(8,128)S(1)}, /*index=5*/f3...) while((s32[]{:T(128)}, f32[32,4096]{1,0:T(8,128)}, ...), condition=%wide.region_1.0_spmd.clone, body=%wide.region_0.0_spmd.clone.sunk | while | flops 606224384 | bytes 8193713 | solution.py:125
  60.4 5.4 %collective-permute-done = f32[2,32,128]{2,1,0:T(8,128)S(1)} collective-permute-done((f32[2,32,128]{2,1,0:T(8,128)S(1)}, f32[2,32,128]{2,1,0:T(8,128)S(1)}, u32[]{:S(2)}, u32[]{:S(2)}) %collective-permute-start) | collective-permute-done | bytes 32800 | tf_op jit(solution)/shard_map/while/body/eval_jaxpr/ppermute | solution.py:12
  74.0 5.4 %collective-permute-done = f32[2,32,128]{2,1,0:T(8,128)S(1)} collective-permute-done((f32[2,32,128]{2,1,0:T(8,128)S(1)}, f32[2,32,128]{2,1,0:T(8,128)S(1)}, u32[]{:S(2)}, u32[]{:S(2)}) %collective-permute-start) | collective-permute-done | bytes 32800 | tf_op jit(solution)/shard_map/while/body/eval_jaxpr/ppermute | solution.py:12
  87.6 5.4 %collective-permute-done = f32[2,32,128]{2,1,0:T(8,128)S(1)} collective-permute-done((f32[2,32,128]{2,1,0:T(8,128)S(1)}, f32[2,32,128]{2,1,0:T(8,128)S(1)}, u32[]{:S(2)}, u32[]{:S(2)}) %collective-permute-start) | collective-permute-done | bytes 32800 | tf_op jit(solution)/shard_map/while/body/eval_jaxpr/ppermute | solution.py:12
  101.2 5.4 %collective-permute-done = f32[2,32,128]{2,1,0:T(8,128)S(1)} collective-permute-done((f32[2,32,128]{2,1,0:T(8,128)S(1)}, f32[2,32,128]{2,1,0:T(8,128)S(1)}, u32[]{:S(2)}, u32[]{:S(2)}) %collective-permute-start) | collective-permute-done | bytes 32800 | tf_op jit(solution)/shard_map/while/body/eval_jaxpr/ppermute | solution.py:12
  114.7 5.4 %collective-permute-done = f32[2,32,128]{2,1,0:T(8,128)S(1)} collective-permute-done((f32[2,32,128]{2,1,0:T(8,128)S(1)}, f32[2,32,128]{2,1,0:T(8,128)S(1)}, u32[]{:S(2)}, u32[]{:S(2)}) %collective-permute-start) | collective-permute-done | bytes 32800 | tf_op jit(solution)/shard_map/while/body/eval_jaxpr/ppermute | solution.py:12
  128.3 5.4 %collective-permute-done = f32[2,32,128]{2,1,0:T(8,128)S(1)} collective-permute-done((f32[2,32,128]{2,1,0:T(8,128)S(1)}, f32[2,32,128]{2,1,0:T(8,128)S(1)}, u32[]{:S(2)}, u32[]{:S(2)}) %collective-permute-start) | collective-permute-done | bytes 32800 | tf_op jit(solution)/shard_map/while/body/eval_jaxpr/ppermute | solution.py:12
  143.2 108.7 %while.59 = (s32[]{:T(128)}, f32[32,4096]{1,0:T(8,128)}, f32[32,128]{1,0:T(8,128)S(1)}, f32[32,128]{1,0:T(8,128)}, f32[32,4096]{1,0:T(8,128)S(1)}, /*index=5*/f3...) while((s32[]{:T(128)}, f32[32,4096]{1,0:T(8,128)}, ...), condition=%wide.region_3.4_spmd.clone, body=%wide.region_2.3_spmd.clone.sunk | while | flops 606224384 | bytes 8193713 | solution.py:125
  150.8 5.4 %collective-permute-done.1 = f32[2,32,128]{2,1,0:T(8,128)S(1)} collective-permute-done((f32[2,32,128]{2,1,0:T(8,128)S(1)}, f32[2,32,128]{2,1,0:T(8,128)S(1)}, u32[]{:S(2)}, u32[]{:S(2)}) %collective-permute-start.1) | collective-permute-done | bytes 32800 | tf_op jit(solution)/shard_map/while/body/eval_jaxpr/ppermute | solution.py:12
  164.4 5.4 %collective-permute-done.1 = f32[2,32,128]{2,1,0:T(8,128)S(1)} collective-permute-done((f32[2,32,128]{2,1,0:T(8,128)S(1)}, f32[2,32,128]{2,1,0:T(8,128)S(1)}, u32[]{:S(2)}, u32[]{:S(2)}) %collective-permute-start.1) | collective-permute-done | bytes 32800 | tf_op jit(solution)/shard_map/while/body/eval_jaxpr/ppermute | solution.py:12
  178.0 5.6 %collective-permute-done.1 = f32[2,32,128]{2,1,0:T(8,128)S(1)} collective-permute-done((f32[2,32,128]{2,1,0:T(8,128)S(1)}, f32[2,32,128]{2,1,0:T(8,128)S(1)}, u32[]{:S(2)}, u32[]{:S(2)}) %collective-permute-start.1) | collective-permute-done | bytes 32800 | tf_op jit(solution)/shard_map/while/body/eval_jaxpr/ppermute | solution.py:12
  205.2 5.4 %collective-permute-done.1 = f32[2,32,128]{2,1,0:T(8,128)S(1)} collective-permute-done((f32[2,32,128]{2,1,0:T(8,128)S(1)}, f32[2,32,128]{2,1,0:T(8,128)S(1)}, u32[]{:S(2)}, u32[]{:S(2)}) %collective-permute-start.1) | collective-permute-done | bytes 32800 | tf_op jit(solution)/shard_map/while/body/eval_jaxpr/ppermute | solution.py:12
  218.8 5.4 %collective-permute-done.1 = f32[2,32,128]{2,1,0:T(8,128)S(1)} collective-permute-done((f32[2,32,128]{2,1,0:T(8,128)S(1)}, f32[2,32,128]{2,1,0:T(8,128)S(1)}, u32[]{:S(2)}, u32[]{:S(2)}) %collective-permute-start.1) | collective-permute-done | bytes 32800 | tf_op jit(solution)/shard_map/while/body/eval_jaxpr/ppermute | solution.py:12
  232.4 5.4 %collective-permute-done.1 = f32[2,32,128]{2,1,0:T(8,128)S(1)} collective-permute-done((f32[2,32,128]{2,1,0:T(8,128)S(1)}, f32[2,32,128]{2,1,0:T(8,128)S(1)}, u32[]{:S(2)}, u32[]{:S(2)}) %collective-permute-start.1) | collective-permute-done | bytes 32800 | tf_op jit(solution)/shard_map/while/body/eval_jaxpr/ppermute | solution.py:12
  246.0 5.4 %collective-permute-done.1 = f32[2,32,128]{2,1,0:T(8,128)S(1)} collective-permute-done((f32[2,32,128]{2,1,0:T(8,128)S(1)}, f32[2,32,128]{2,1,0:T(8,128)S(1)}, u32[]{:S(2)}, u32[]{:S(2)}) %collective-permute-start.1) | collective-permute-done | bytes 32800 | tf_op jit(solution)/shard_map/while/body/eval_jaxpr/ppermute | solution.py:12
  259.1 108.7 %while.60 = (s32[]{:T(128)}, f32[32,4096]{1,0:T(8,128)}, f32[32,128]{1,0:T(8,128)S(1)}, f32[32,128]{1,0:T(8,128)}, f32[32,4096]{1,0:T(8,128)S(1)}, /*index=5*/f3...) while((s32[]{:T(128)}, f32[32,4096]{1,0:T(8,128)}, ...), condition=%wide.region_5.6_spmd.clone, body=%wide.region_4.5_spmd.clone.sunk | while | flops 606224384 | bytes 8193713 | solution.py:125
  266.7 5.4 %collective-permute-done.2 = f32[2,32,128]{2,1,0:T(8,128)S(1)} collective-permute-done((f32[2,32,128]{2,1,0:T(8,128)S(1)}, f32[2,32,128]{2,1,0:T(8,128)S(1)}, u32[]{:S(2)}, u32[]{:S(2)}) %collective-permute-start.2) | collective-permute-done | bytes 32800 | tf_op jit(solution)/shard_map/while/body/eval_jaxpr/ppermute | solution.py:12
  280.3 5.4 %collective-permute-done.2 = f32[2,32,128]{2,1,0:T(8,128)S(1)} collective-permute-done((f32[2,32,128]{2,1,0:T(8,128)S(1)}, f32[2,32,128]{2,1,0:T(8,128)S(1)}, u32[]{:S(2)}, u32[]{:S(2)}) %collective-permute-start.2) | collective-permute-done | bytes 32800 | tf_op jit(solution)/shard_map/while/body/eval_jaxpr/ppermute | solution.py:12
  293.9 5.4 %collective-permute-done.2 = f32[2,32,128]{2,1,0:T(8,128)S(1)} collective-permute-done((f32[2,32,128]{2,1,0:T(8,128)S(1)}, f32[2,32,128]{2,1,0:T(8,128)S(1)}, u32[]{:S(2)}, u32[]{:S(2)}) %collective-permute-start.2) | collective-permute-done | bytes 32800 | tf_op jit(solution)/shard_map/while/body/eval_jaxpr/ppermute | solution.py:12
  307.4 5.4 %collective-permute-done.2 = f32[2,32,128]{2,1,0:T(8,128)S(1)} collective-permute-done((f32[2,32,128]{2,1,0:T(8,128)S(1)}, f32[2,32,128]{2,1,0:T(8,128)S(1)}, u32[]{:S(2)}, u32[]{:S(2)}) %collective-permute-start.2) | collective-permute-done | bytes 32800 | tf_op jit(solution)/shard_map/while/body/eval_jaxpr/ppermute | solution.py:12
  321.0 5.4 %collective-permute-done.2 = f32[2,32,128]{2,1,0:T(8,128)S(1)} collective-permute-done((f32[2,32,128]{2,1,0:T(8,128)S(1)}, f32[2,32,128]{2,1,0:T(8,128)S(1)}, u32[]{:S(2)}, u32[]{:S(2)}) %collective-permute-start.2) | collective-permute-done | bytes 32800 | tf_op jit(solution)/shard_map/while/body/eval_jaxpr/ppermute | solution.py:12
  334.6 5.4 %collective-permute-done.2 = f32[2,32,128]{2,1,0:T(8,128)S(1)} collective-permute-done((f32[2,32,128]{2,1,0:T(8,128)S(1)}, f32[2,32,128]{2,1,0:T(8,128)S(1)}, u32[]{:S(2)}, u32[]{:S(2)}) %collective-permute-start.2) | collective-permute-done | bytes 32800 | tf_op jit(solution)/shard_map/while/body/eval_jaxpr/ppermute | solution.py:12
  348.2 5.4 %collective-permute-done.2 = f32[2,32,128]{2,1,0:T(8,128)S(1)} collective-permute-done((f32[2,32,128]{2,1,0:T(8,128)S(1)}, f32[2,32,128]{2,1,0:T(8,128)S(1)}, u32[]{:S(2)}, u32[]{:S(2)}) %collective-permute-start.2) | collective-permute-done | bytes 32800 | tf_op jit(solution)/shard_map/while/body/eval_jaxpr/ppermute | solution.py:12
  361.8 5.4 %collective-permute-done.2 = f32[2,32,128]{2,1,0:T(8,128)S(1)} collective-permute-done((f32[2,32,128]{2,1,0:T(8,128)S(1)}, f32[2,32,128]{2,1,0:T(8,128)S(1)}, u32[]{:S(2)}, u32[]{:S(2)}) %collective-permute-start.2) | collective-permute-done | bytes 32800 | tf_op jit(solution)/shard_map/while/body/eval_jaxpr/ppermute | solution.py:12
  374.6 109.9 %while.61 = (s32[]{:T(128)}, f32[32,4096]{1,0:T(8,128)}, f32[32,128]{1,0:T(8,128)S(1)}, f32[32,4096]{1,0:T(8,128)S(1)}, f32[32,128,128]{2,1,0:T(8,128)S(1)}, /*i...) while((s32[]{:T(128)}, f32[32,4096]{1,0:T(8,128)}, ...), condition=%wide.region_7.8_spmd.clone, body=%wide.region_6.7_spmd.clone.sunk | while | flops 606224384 | bytes 8160937 | solution.py:125
  382.9 5.4 %collective-permute-done.3 = f32[2,32,128]{2,1,0:T(8,128)S(1)} collective-permute-done((f32[2,32,128]{2,1,0:T(8,128)S(1)}, f32[2,32,128]{2,1,0:T(8,128)S(1)}, u32[]{:S(2)}, u32[]{:S(2)}) %collective-permute-start.3) | collective-permute-done | bytes 32800 | tf_op jit(solution)/shard_map/while/body/eval_jaxpr/ppermute | solution.py:12
  396.6 5.4 %collective-permute-done.3 = f32[2,32,128]{2,1,0:T(8,128)S(1)} collective-permute-done((f32[2,32,128]{2,1,0:T(8,128)S(1)}, f32[2,32,128]{2,1,0:T(8,128)S(1)}, u32[]{:S(2)}, u32[]{:S(2)}) %collective-permute-start.3) | collective-permute-done | bytes 32800 | tf_op jit(solution)/shard_map/while/body/eval_jaxpr/ppermute | solution.py:12
  410.4 5.4 %collective-permute-done.3 = f32[2,32,128]{2,1,0:T(8,128)S(1)} collective-permute-done((f32[2,32,128]{2,1,0:T(8,128)S(1)}, f32[2,32,128]{2,1,0:T(8,128)S(1)}, u32[]{:S(2)}, u32[]{:S(2)}) %collective-permute-start.3) | collective-permute-done | bytes 32800 | tf_op jit(solution)/shard_map/while/body/eval_jaxpr/ppermute | solution.py:12
  424.1 5.4 %collective-permute-done.3 = f32[2,32,128]{2,1,0:T(8,128)S(1)} collective-permute-done((f32[2,32,128]{2,1,0:T(8,128)S(1)}, f32[2,32,128]{2,1,0:T(8,128)S(1)}, u32[]{:S(2)}, u32[]{:S(2)}) %collective-permute-start.3) | collective-permute-done | bytes 32800 | tf_op jit(solution)/shard_map/while/body/eval_jaxpr/ppermute | solution.py:12
  451.6 5.4 %collective-permute-done.3 = f32[2,32,128]{2,1,0:T(8,128)S(1)} collective-permute-done((f32[2,32,128]{2,1,0:T(8,128)S(1)}, f32[2,32,128]{2,1,0:T(8,128)S(1)}, u32[]{:S(2)}, u32[]{:S(2)}) %collective-permute-start.3) | collective-permute-done | bytes 32800 | tf_op jit(solution)/shard_map/while/body/eval_jaxpr/ppermute | solution.py:12
  465.3 5.4 %collective-permute-done.3 = f32[2,32,128]{2,1,0:T(8,128)S(1)} collective-permute-done((f32[2,32,128]{2,1,0:T(8,128)S(1)}, f32[2,32,128]{2,1,0:T(8,128)S(1)}, u32[]{:S(2)}, u32[]{:S(2)}) %collective-permute-start.3) | collective-permute-done | bytes 32800 | tf_op jit(solution)/shard_map/while/body/eval_jaxpr/ppermute | solution.py:12
  487.6 10.1 %all-reduce = f32[4096]{0:T(1024)S(1)} all-reduce(f32[4096]{0:T(1024)S(1)} %add_multiply_fusion), channel_id=2, replica_groups=mesh['net'=8,'mem'=4] {'mem'}, use_global_device_ids=true, to_apply=%region_12.13.clone | all-reduce | flops 4096 | bytes 32768
  (368 shorter events, 339.9 us)
Async XLA Ops:
  3.0 17.8 %collective-permute-start.4 = (f32[5,32,128]{2,1,0:T(8,128)S(1)}, f32[5,32,128]{2,1,0:T(8,128)S(1)}, u32[]{:S(2)}, u32[]{:S(2)}) collective-permute-start(f32[5,32,128]{2,1,0:T(8,128)S(1)} %fusion.74), channel_id=1, source_target_pairs={{0,4},{4,8},{8,12},{12,16},{16,20},{20,24},{24,28},{1,5},{5,9},{9,... | collective-permute-start | bytes 245768 | tf_op jit(solution)/shard_map/ppermute | solution.py:12
  46.0 6.2 %collective-permute-start = (f32[2,32,128]{2,1,0:T(8,128)S(1)}, f32[2,32,128]{2,1,0:T(8,128)S(1)}, u32[]{:S(2)}, u32[]{:S(2)}) collective-permute-start(f32[2,32,128]{2,1,0:T(8,128)S(1)} %pad_maximum_fusion.9), channel_id=1, source_target_pairs={{4,0},{8,4},{12,8},{16,12},{20,16},{24,20},{28,24},{5,1},{9,5},{13... | collective-permute-start | bytes 98312 | tf_op jit(solution)/shard_map/while/body/eval_jaxpr/ppermute | solution.py:12
  59.1 6.7 %collective-permute-start = (f32[2,32,128]{2,1,0:T(8,128)S(1)}, f32[2,32,128]{2,1,0:T(8,128)S(1)}, u32[]{:S(2)}, u32[]{:S(2)}) collective-permute-start(f32[2,32,128]{2,1,0:T(8,128)S(1)} %pad_maximum_fusion.9), channel_id=1, source_target_pairs={{4,0},{8,4},{12,8},{16,12},{20,16},{24,20},{28,24},{5,1},{9,5},{13... | collective-permute-start | bytes 98312 | tf_op jit(solution)/shard_map/while/body/eval_jaxpr/ppermute | solution.py:12
  72.7 6.7 %collective-permute-start = (f32[2,32,128]{2,1,0:T(8,128)S(1)}, f32[2,32,128]{2,1,0:T(8,128)S(1)}, u32[]{:S(2)}, u32[]{:S(2)}) collective-permute-start(f32[2,32,128]{2,1,0:T(8,128)S(1)} %pad_maximum_fusion.9), channel_id=1, source_target_pairs={{4,0},{8,4},{12,8},{16,12},{20,16},{24,20},{28,24},{5,1},{9,5},{13... | collective-permute-start | bytes 98312 | tf_op jit(solution)/shard_map/while/body/eval_jaxpr/ppermute | solution.py:12
  86.3 6.7 %collective-permute-start = (f32[2,32,128]{2,1,0:T(8,128)S(1)}, f32[2,32,128]{2,1,0:T(8,128)S(1)}, u32[]{:S(2)}, u32[]{:S(2)}) collective-permute-start(f32[2,32,128]{2,1,0:T(8,128)S(1)} %pad_maximum_fusion.9), channel_id=1, source_target_pairs={{4,0},{8,4},{12,8},{16,12},{20,16},{24,20},{28,24},{5,1},{9,5},{13... | collective-permute-start | bytes 98312 | tf_op jit(solution)/shard_map/while/body/eval_jaxpr/ppermute | solution.py:12
  99.9 6.7 %collective-permute-start = (f32[2,32,128]{2,1,0:T(8,128)S(1)}, f32[2,32,128]{2,1,0:T(8,128)S(1)}, u32[]{:S(2)}, u32[]{:S(2)}) collective-permute-start(f32[2,32,128]{2,1,0:T(8,128)S(1)} %pad_maximum_fusion.9), channel_id=1, source_target_pairs={{4,0},{8,4},{12,8},{16,12},{20,16},{24,20},{28,24},{5,1},{9,5},{13... | collective-permute-start | bytes 98312 | tf_op jit(solution)/shard_map/while/body/eval_jaxpr/ppermute | solution.py:12
  113.4 6.7 %collective-permute-start = (f32[2,32,128]{2,1,0:T(8,128)S(1)}, f32[2,32,128]{2,1,0:T(8,128)S(1)}, u32[]{:S(2)}, u32[]{:S(2)}) collective-permute-start(f32[2,32,128]{2,1,0:T(8,128)S(1)} %pad_maximum_fusion.9), channel_id=1, source_target_pairs={{4,0},{8,4},{12,8},{16,12},{20,16},{24,20},{28,24},{5,1},{9,5},{13... | collective-permute-start | bytes 98312 | tf_op jit(solution)/shard_map/while/body/eval_jaxpr/ppermute | solution.py:12
  127.0 6.7 %collective-permute-start = (f32[2,32,128]{2,1,0:T(8,128)S(1)}, f32[2,32,128]{2,1,0:T(8,128)S(1)}, u32[]{:S(2)}, u32[]{:S(2)}) collective-permute-start(f32[2,32,128]{2,1,0:T(8,128)S(1)} %pad_maximum_fusion.9), channel_id=1, source_target_pairs={{4,0},{8,4},{12,8},{16,12},{20,16},{24,20},{28,24},{5,1},{9,5},{13... | collective-permute-start | bytes 98312 | tf_op jit(solution)/shard_map/while/body/eval_jaxpr/ppermute | solution.py:12
  149.5 6.7 %collective-permute-start.1 = (f32[2,32,128]{2,1,0:T(8,128)S(1)}, f32[2,32,128]{2,1,0:T(8,128)S(1)}, u32[]{:S(2)}, u32[]{:S(2)}) collective-permute-start(f32[2,32,128]{2,1,0:T(8,128)S(1)} %pad_maximum_fusion.10), channel_id=1, source_target_pairs={{4,0},{8,4},{12,8},{16,12},{20,16},{24,20},{28,24},{5,1},{9,5},{13... | collective-permute-start | bytes 98312 | tf_op jit(solution)/shard_map/while/body/eval_jaxpr/ppermute | solution.py:12
  163.1 6.7 %collective-permute-start.1 = (f32[2,32,128]{2,1,0:T(8,128)S(1)}, f32[2,32,128]{2,1,0:T(8,128)S(1)}, u32[]{:S(2)}, u32[]{:S(2)}) collective-permute-start(f32[2,32,128]{2,1,0:T(8,128)S(1)} %pad_maximum_fusion.10), channel_id=1, source_target_pairs={{4,0},{8,4},{12,8},{16,12},{20,16},{24,20},{28,24},{5,1},{9,5},{13... | collective-permute-start | bytes 98312 | tf_op jit(solution)/shard_map/while/body/eval_jaxpr/ppermute | solution.py:12
  176.7 6.9 %collective-permute-start.1 = (f32[2,32,128]{2,1,0:T(8,128)S(1)}, f32[2,32,128]{2,1,0:T(8,128)S(1)}, u32[]{:S(2)}, u32[]{:S(2)}) collective-permute-start(f32[2,32,128]{2,1,0:T(8,128)S(1)} %pad_maximum_fusion.10), channel_id=1, source_target_pairs={{4,0},{8,4},{12,8},{16,12},{20,16},{24,20},{28,24},{5,1},{9,5},{13... | collective-permute-start | bytes 98312 | tf_op jit(solution)/shard_map/while/body/eval_jaxpr/ppermute | solution.py:12
  190.5 6.5 %collective-permute-start.1 = (f32[2,32,128]{2,1,0:T(8,128)S(1)}, f32[2,32,128]{2,1,0:T(8,128)S(1)}, u32[]{:S(2)}, u32[]{:S(2)}) collective-permute-start(f32[2,32,128]{2,1,0:T(8,128)S(1)} %pad_maximum_fusion.10), channel_id=1, source_target_pairs={{4,0},{8,4},{12,8},{16,12},{20,16},{24,20},{28,24},{5,1},{9,5},{13... | collective-permute-start | bytes 98312 | tf_op jit(solution)/shard_map/while/body/eval_jaxpr/ppermute | solution.py:12
  203.9 6.7 %collective-permute-start.1 = (f32[2,32,128]{2,1,0:T(8,128)S(1)}, f32[2,32,128]{2,1,0:T(8,128)S(1)}, u32[]{:S(2)}, u32[]{:S(2)}) collective-permute-start(f32[2,32,128]{2,1,0:T(8,128)S(1)} %pad_maximum_fusion.10), channel_id=1, source_target_pairs={{4,0},{8,4},{12,8},{16,12},{20,16},{24,20},{28,24},{5,1},{9,5},{13... | collective-permute-start | bytes 98312 | tf_op jit(solution)/shard_map/while/body/eval_jaxpr/ppermute | solution.py:12
  217.5 6.7 %collective-permute-start.1 = (f32[2,32,128]{2,1,0:T(8,128)S(1)}, f32[2,32,128]{2,1,0:T(8,128)S(1)}, u32[]{:S(2)}, u32[]{:S(2)}) collective-permute-start(f32[2,32,128]{2,1,0:T(8,128)S(1)} %pad_maximum_fusion.10), channel_id=1, source_target_pairs={{4,0},{8,4},{12,8},{16,12},{20,16},{24,20},{28,24},{5,1},{9,5},{13... | collective-permute-start | bytes 98312 | tf_op jit(solution)/shard_map/while/body/eval_jaxpr/ppermute | solution.py:12
  231.1 6.7 %collective-permute-start.1 = (f32[2,32,128]{2,1,0:T(8,128)S(1)}, f32[2,32,128]{2,1,0:T(8,128)S(1)}, u32[]{:S(2)}, u32[]{:S(2)}) collective-permute-start(f32[2,32,128]{2,1,0:T(8,128)S(1)} %pad_maximum_fusion.10), channel_id=1, source_target_pairs={{4,0},{8,4},{12,8},{16,12},{20,16},{24,20},{28,24},{5,1},{9,5},{13... | collective-permute-start | bytes 98312 | tf_op jit(solution)/shard_map/while/body/eval_jaxpr/ppermute | solution.py:12
  244.7 6.7 %collective-permute-start.1 = (f32[2,32,128]{2,1,0:T(8,128)S(1)}, f32[2,32,128]{2,1,0:T(8,128)S(1)}, u32[]{:S(2)}, u32[]{:S(2)}) collective-permute-start(f32[2,32,128]{2,1,0:T(8,128)S(1)} %pad_maximum_fusion.10), channel_id=1, source_target_pairs={{4,0},{8,4},{12,8},{16,12},{20,16},{24,20},{28,24},{5,1},{9,5},{13... | collective-permute-start | bytes 98312 | tf_op jit(solution)/shard_map/while/body/eval_jaxpr/ppermute | solution.py:12
  265.4 6.7 %collective-permute-start.2 = (f32[2,32,128]{2,1,0:T(8,128)S(1)}, f32[2,32,128]{2,1,0:T(8,128)S(1)}, u32[]{:S(2)}, u32[]{:S(2)}) collective-permute-start(f32[2,32,128]{2,1,0:T(8,128)S(1)} %pad_maximum_fusion.11), channel_id=1, source_target_pairs={{4,0},{8,4},{12,8},{16,12},{20,16},{24,20},{28,24},{5,1},{9,5},{13... | collective-permute-start | bytes 98312 | tf_op jit(solution)/shard_map/while/body/eval_jaxpr/ppermute | solution.py:12
  279.0 6.7 %collective-permute-start.2 = (f32[2,32,128]{2,1,0:T(8,128)S(1)}, f32[2,32,128]{2,1,0:T(8,128)S(1)}, u32[]{:S(2)}, u32[]{:S(2)}) collective-permute-start(f32[2,32,128]{2,1,0:T(8,128)S(1)} %pad_maximum_fusion.11), channel_id=1, source_target_pairs={{4,0},{8,4},{12,8},{16,12},{20,16},{24,20},{28,24},{5,1},{9,5},{13... | collective-permute-start | bytes 98312 | tf_op jit(solution)/shard_map/while/body/eval_jaxpr/ppermute | solution.py:12
  292.6 6.7 %collective-permute-start.2 = (f32[2,32,128]{2,1,0:T(8,128)S(1)}, f32[2,32,128]{2,1,0:T(8,128)S(1)}, u32[]{:S(2)}, u32[]{:S(2)}) collective-permute-start(f32[2,32,128]{2,1,0:T(8,128)S(1)} %pad_maximum_fusion.11), channel_id=1, source_target_pairs={{4,0},{8,4},{12,8},{16,12},{20,16},{24,20},{28,24},{5,1},{9,5},{13... | collective-permute-start | bytes 98312 | tf_op jit(solution)/shard_map/while/body/eval_jaxpr/ppermute | solution.py:12
  306.1 6.7 %collective-permute-start.2 = (f32[2,32,128]{2,1,0:T(8,128)S(1)}, f32[2,32,128]{2,1,0:T(8,128)S(1)}, u32[]{:S(2)}, u32[]{:S(2)}) collective-permute-start(f32[2,32,128]{2,1,0:T(8,128)S(1)} %pad_maximum_fusion.11), channel_id=1, source_target_pairs={{4,0},{8,4},{12,8},{16,12},{20,16},{24,20},{28,24},{5,1},{9,5},{13... | collective-permute-start | bytes 98312 | tf_op jit(solution)/shard_map/while/body/eval_jaxpr/ppermute | solution.py:12
  319.7 6.7 %collective-permute-start.2 = (f32[2,32,128]{2,1,0:T(8,128)S(1)}, f32[2,32,128]{2,1,0:T(8,128)S(1)}, u32[]{:S(2)}, u32[]{:S(2)}) collective-permute-start(f32[2,32,128]{2,1,0:T(8,128)S(1)} %pad_maximum_fusion.11), channel_id=1, source_target_pairs={{4,0},{8,4},{12,8},{16,12},{20,16},{24,20},{28,24},{5,1},{9,5},{13... | collective-permute-start | bytes 98312 | tf_op jit(solution)/shard_map/while/body/eval_jaxpr/ppermute | solution.py:12
  333.3 6.7 %collective-permute-start.2 = (f32[2,32,128]{2,1,0:T(8,128)S(1)}, f32[2,32,128]{2,1,0:T(8,128)S(1)}, u32[]{:S(2)}, u32[]{:S(2)}) collective-permute-start(f32[2,32,128]{2,1,0:T(8,128)S(1)} %pad_maximum_fusion.11), channel_id=1, source_target_pairs={{4,0},{8,4},{12,8},{16,12},{20,16},{24,20},{28,24},{5,1},{9,5},{13... | collective-permute-start | bytes 98312 | tf_op jit(solution)/shard_map/while/body/eval_jaxpr/ppermute | solution.py:12
  346.9 6.7 %collective-permute-start.2 = (f32[2,32,128]{2,1,0:T(8,128)S(1)}, f32[2,32,128]{2,1,0:T(8,128)S(1)}, u32[]{:S(2)}, u32[]{:S(2)}) collective-permute-start(f32[2,32,128]{2,1,0:T(8,128)S(1)} %pad_maximum_fusion.11), channel_id=1, source_target_pairs={{4,0},{8,4},{12,8},{16,12},{20,16},{24,20},{28,24},{5,1},{9,5},{13... | collective-permute-start | bytes 98312 | tf_op jit(solution)/shard_map/while/body/eval_jaxpr/ppermute | solution.py:12
  360.5 6.7 %collective-permute-start.2 = (f32[2,32,128]{2,1,0:T(8,128)S(1)}, f32[2,32,128]{2,1,0:T(8,128)S(1)}, u32[]{:S(2)}, u32[]{:S(2)}) collective-permute-start(f32[2,32,128]{2,1,0:T(8,128)S(1)} %pad_maximum_fusion.11), channel_id=1, source_target_pairs={{4,0},{8,4},{12,8},{16,12},{20,16},{24,20},{28,24},{5,1},{9,5},{13... | collective-permute-start | bytes 98312 | tf_op jit(solution)/shard_map/while/body/eval_jaxpr/ppermute | solution.py:12
  381.6 6.7 %collective-permute-start.3 = (f32[2,32,128]{2,1,0:T(8,128)S(1)}, f32[2,32,128]{2,1,0:T(8,128)S(1)}, u32[]{:S(2)}, u32[]{:S(2)}) collective-permute-start(f32[2,32,128]{2,1,0:T(8,128)S(1)} %pad_maximum_fusion.12), channel_id=1, source_target_pairs={{4,0},{8,4},{12,8},{16,12},{20,16},{24,20},{28,24},{5,1},{9,5},{13... | collective-permute-start | bytes 98312 | tf_op jit(solution)/shard_map/while/body/eval_jaxpr/ppermute | solution.py:12
  395.3 6.7 %collective-permute-start.3 = (f32[2,32,128]{2,1,0:T(8,128)S(1)}, f32[2,32,128]{2,1,0:T(8,128)S(1)}, u32[]{:S(2)}, u32[]{:S(2)}) collective-permute-start(f32[2,32,128]{2,1,0:T(8,128)S(1)} %pad_maximum_fusion.12), channel_id=1, source_target_pairs={{4,0},{8,4},{12,8},{16,12},{20,16},{24,20},{28,24},{5,1},{9,5},{13... | collective-permute-start | bytes 98312 | tf_op jit(solution)/shard_map/while/body/eval_jaxpr/ppermute | solution.py:12
  409.1 6.7 %collective-permute-start.3 = (f32[2,32,128]{2,1,0:T(8,128)S(1)}, f32[2,32,128]{2,1,0:T(8,128)S(1)}, u32[]{:S(2)}, u32[]{:S(2)}) collective-permute-start(f32[2,32,128]{2,1,0:T(8,128)S(1)} %pad_maximum_fusion.12), channel_id=1, source_target_pairs={{4,0},{8,4},{12,8},{16,12},{20,16},{24,20},{28,24},{5,1},{9,5},{13... | collective-permute-start | bytes 98312 | tf_op jit(solution)/shard_map/while/body/eval_jaxpr/ppermute | solution.py:12
  422.8 6.7 %collective-permute-start.3 = (f32[2,32,128]{2,1,0:T(8,128)S(1)}, f32[2,32,128]{2,1,0:T(8,128)S(1)}, u32[]{:S(2)}, u32[]{:S(2)}) collective-permute-start(f32[2,32,128]{2,1,0:T(8,128)S(1)} %pad_maximum_fusion.12), channel_id=1, source_target_pairs={{4,0},{8,4},{12,8},{16,12},{20,16},{24,20},{28,24},{5,1},{9,5},{13... | collective-permute-start | bytes 98312 | tf_op jit(solution)/shard_map/while/body/eval_jaxpr/ppermute | solution.py:12
  436.6 6.7 %collective-permute-start.3 = (f32[2,32,128]{2,1,0:T(8,128)S(1)}, f32[2,32,128]{2,1,0:T(8,128)S(1)}, u32[]{:S(2)}, u32[]{:S(2)}) collective-permute-start(f32[2,32,128]{2,1,0:T(8,128)S(1)} %pad_maximum_fusion.12), channel_id=1, source_target_pairs={{4,0},{8,4},{12,8},{16,12},{20,16},{24,20},{28,24},{5,1},{9,5},{13... | collective-permute-start | bytes 98312 | tf_op jit(solution)/shard_map/while/body/eval_jaxpr/ppermute | solution.py:12
  450.3 6.7 %collective-permute-start.3 = (f32[2,32,128]{2,1,0:T(8,128)S(1)}, f32[2,32,128]{2,1,0:T(8,128)S(1)}, u32[]{:S(2)}, u32[]{:S(2)}) collective-permute-start(f32[2,32,128]{2,1,0:T(8,128)S(1)} %pad_maximum_fusion.12), channel_id=1, source_target_pairs={{4,0},{8,4},{12,8},{16,12},{20,16},{24,20},{28,24},{5,1},{9,5},{13... | collective-permute-start | bytes 98312 | tf_op jit(solution)/shard_map/while/body/eval_jaxpr/ppermute | solution.py:12
  464.0 6.7 %collective-permute-start.3 = (f32[2,32,128]{2,1,0:T(8,128)S(1)}, f32[2,32,128]{2,1,0:T(8,128)S(1)}, u32[]{:S(2)}, u32[]{:S(2)}) collective-permute-start(f32[2,32,128]{2,1,0:T(8,128)S(1)} %pad_maximum_fusion.12), channel_id=1, source_target_pairs={{4,0},{8,4},{12,8},{16,12},{20,16},{24,20},{28,24},{5,1},{9,5},{13... | collective-permute-start | bytes 98312 | tf_op jit(solution)/shard_map/while/body/eval_jaxpr/ppermute | solution.py:12
  477.8 6.7 %collective-permute-start.3 = (f32[2,32,128]{2,1,0:T(8,128)S(1)}, f32[2,32,128]{2,1,0:T(8,128)S(1)}, u32[]{:S(2)}, u32[]{:S(2)}) collective-permute-start(f32[2,32,128]{2,1,0:T(8,128)S(1)} %pad_maximum_fusion.12), channel_id=1, source_target_pairs={{4,0},{8,4},{12,8},{16,12},{20,16},{24,20},{28,24},{5,1},{9,5},{13... | collective-permute-start | bytes 98312 | tf_op jit(solution)/shard_map/while/body/eval_jaxpr/ppermute | solution.py:12
  (52 other events, 1154.4 us)
where the time goes:
time: 501 us; the launch traced here: 499 us
  matrix products  229 us (46%)
  waiting for transfers between devices  172 us (34%)
  starting transfers between devices  46.2 us (9%)
  local copies, waits for them, and re-layouts  32.1 us (6%)
  blocking collectives  10.1 us (2%)
  other arithmetic  7.44 us (1%)
    ppermute x33, waiting for transfers between devices, from_behind(): return lax.ppermute(value, axis, pairs)  172 us
    dot_general x32, matrix products, inlet_rows(): jnp.einsum('mr,er->me', adjoint, placement_rows, precision=lax.Precision....  92.2 us
    dot_general x32, matrix products, solve_blocks(): jnp.einsum('acj,cjv->acv', reshaped_values, inverse_block_matrix, precisi...  60.9 us
    dot_general x36, matrix products, from_below(): jnp.dot(values, leaving_exact, precision=lax.Precision.HIGHEST, preferred...  55.6 us
    ppermute x33, starting transfers between devices, from_behind(): return lax.ppermute(value, axis, pairs)  46.2 us
    squeeze x32, local copies, waits for them, and re-layouts, one_section(): return (adjoint, received[0], received[1])  14.4 us
    dot_general x4, matrix products, body(): jnp.einsum('qvt,vzt->qvz', weighted_flows, exact_within_partition, precis...  10.7 us
    unnamed x1, blocking collectives  10.1 us
  transfers between devices with their start and end apart: 33, of which 32 were waited for; matrix products, arithmetic and copies ran while one was open for 2% of the time, Pallas kernels for 0%

commit v1 on v0

v1 whole, which is shorter than its diff:
```python
import functools

import jax
import jax.numpy as jnp
from jax import lax
from jax.experimental import pallas as pl
from jax.experimental.pallas import tpu as pltpu
from jax.sharding import PartitionSpec as P

skew_weight = 0.2
LANES = 128
EXTRA = 8
F32 = jnp.float32


def take(values, index):
    return jnp.take_along_axis(values, index, axis=1, mode="promise_in_bounds")


def weights_of(travel):
    divisor = travel * (1.0 - skew_weight) + 0.5
    weight_new = (0.5 - travel * skew_weight) / divisor
    weight_old = (0.5 + travel * skew_weight) / divisor
    weight_stay = (travel * (1.0 - skew_weight) - 0.5) / divisor
    return weight_new, weight_old, weight_stay


def slopes_of(travel):
    divisor = travel * (1.0 - skew_weight) + 0.5
    square = divisor * divisor
    return (
        -0.5 / square,
        (skew_weight - 0.5) / square,
        (1.0 - skew_weight) / square,
        (skew_weight - 1.0) / square,
    )


def levels_of(lanes):
    count = 0
    while (1 << count) < lanes:
        count += 1
    return count


def local_kernel(
    steps, members, blocks,
    cot_ref, rough_ref, factor_ref, down_ref, exit_ref, inlet_ref,
    own_ref, message_ref, response_ref, slot_ref, inlet_values_ref, inlet_rows_ref,
    pointer_ref, gain_ref, stay_ref, ratio_ref,
):
    levels = levels_of(LANES)
    travel = rough_ref[...] * factor_ref[...]
    weight_new, weight_old, weight_stay = weights_of(travel)
    down = down_ref[...]
    lane = lax.broadcasted_iota(jnp.int32, down.shape, 1)
    interior = down < LANES
    pointer = jnp.where(interior, down, lane)
    next_new = take(weight_new, pointer)
    next_old = take(weight_old, pointer)
    gain = jnp.where(interior, next_new, 0.0)
    ratio = jnp.where(interior, next_old / next_new, 0.0)
    stay_ref[...] = weight_stay
    ratio_ref[...] = ratio
    pointers, gains = [], []
    for level in range(levels):
        pointers.append(pointer)
        gains.append(gain)
        pointer_ref[level] = pointer
        gain_ref[level] = gain
        gain = gain * take(gain, pointer)
        pointer = take(pointer, pointer)
    slot = take(exit_ref[...], pointer)
    reached = slot >= 0
    slot = jnp.maximum(slot, 0)
    slot_ref[...] = slot
    right = jnp.where(exit_ref[...] >= 0, 1.0, 0.0).astype(F32)
    responses = []
    for lag in range(steps):
        value = right
        for level in range(levels):
            value = value + gains[level] * take(value, pointers[level])
        responses.append(value)
        response_ref[lag] = value
        right = weight_stay * value + ratio * (value - right)

    inlet = inlet_ref[...]
    inlet_block = inlet // LANES
    inlet_lane = inlet - inlet_block * LANES
    lane_rows = jnp.broadcast_to(inlet_lane, (blocks, LANES))
    block_rows = lax.broadcasted_iota(jnp.int32, (blocks, LANES), 0)
    chosen = block_rows == jnp.broadcast_to(inlet_block, (blocks, LANES))

    def at_inlets(rows):
        return jnp.sum(jnp.where(chosen, take(rows, lane_rows), 0.0), axis=0, keepdims=True)

    travel_in = at_inlets(travel)
    slot_in = at_inlets(jnp.where(reached, slot, 0).astype(F32))
    response_in = [at_inlets(value) for value in responses]
    new_in, old_in, _ = weights_of(travel_in)

    member_lane = jnp.broadcast_to(inlet_lane, (members, LANES))
    member_block = jnp.broadcast_to(inlet_block, (members, LANES))
    inlet_values_ref[...] = jnp.zeros_like(inlet_values_ref)

    def one_block(block, carry):
        place = pl.ds(pl.multiple_of(block * LANES, LANES), LANES)
        row = pl.ds(block, 1)
        shape = (members, LANES)
        stay = jnp.broadcast_to(stay_ref[row, :], shape)
        rate = jnp.broadcast_to(ratio_ref[row, :], shape)
        here = member_block == block
        right = None
        value = None
        for step in reversed(range(steps)):
            source = cot_ref[step, :, place].astype(F32)
            right = source if value is None else source + stay * value + rate * (value - right)
            value = right
            for level in range(levels):
                index = jnp.broadcast_to(pointer_ref[level, row, :], shape)
                gain = jnp.broadcast_to(gain_ref[level, row, :], shape)
                value = value + gain * take(value, index)
            own_ref[step, :, place] = value
            rows = pl.ds(step * members, members)
            inlet_values_ref[rows, :] = jnp.where(
                here, take(value, member_lane), inlet_values_ref[rows, :]
            )
        return carry

    lax.fori_loop(0, blocks, one_block, 0, unroll=2)

    for step in range(steps):
        rows = pl.ds(step * members, members)
        outgoing = new_in * inlet_values_ref[rows, :]
        if step + 1 < steps:
            outgoing = outgoing + old_in * inlet_values_ref[pl.ds((step + 1) * members, members), :]
        message_ref[rows, :] = outgoing
    tail = []
    for lag in range(steps):
        coefficient = new_in * response_in[lag]
        if lag > 0:
            coefficient = coefficient + old_in * response_in[lag - 1]
        tail.append(coefficient)
    tail.append(slot_in)
    while len(tail) < EXTRA:
        tail.append(jnp.zeros_like(slot_in))
    message_ref[pl.ds(steps * members, EXTRA), :] = jnp.concatenate(tail, axis=0)
    aside = list(response_in) + [travel_in, slot_in]
    while len(aside) < EXTRA:
        aside.append(jnp.zeros_like(slot_in))
    inlet_rows_ref[...] = jnp.concatenate(aside, axis=0)


def compose(steps, members, upper, lower):
    values, coefficients, slot = upper
    below, below_coefficients, below_slot = lower
    index = jnp.broadcast_to(slot, (members, LANES)).astype(jnp.int32)
    pulled = [take(value, index) for value in below]
    result = []
    for step in range(steps):
        total = values[step]
        for lag in range(steps - step):
            total = total + coefficients[lag] * pulled[step + lag]
        result.append(total)
    if below_coefficients is None:
        return result, None, None
    table = jnp.concatenate(list(below_coefficients) + [below_slot], axis=0)
    pad = (-table.shape[0]) % 8
    if pad:
        table = jnp.concatenate([table, jnp.zeros((pad, LANES), F32)], axis=0)
    table = take(table, jnp.broadcast_to(slot, table.shape).astype(jnp.int32))
    combined = []
    for lag in range(steps):
        total = coefficients[0] * table[lag:lag + 1]
        for first in range(1, lag + 1):
            total = total + coefficients[first] * table[lag - first:lag - first + 1]
        combined.append(total)
    return result, combined, table[steps:steps + 1]


def read_message(steps, members, ref):
    values = [ref[pl.ds(step * members, members), :] for step in range(steps)]
    tail = ref[pl.ds(steps * members, EXTRA), :]
    return values, [tail[lag:lag + 1] for lag in range(steps)], tail[steps:steps + 1]


def write_message(steps, members, ref, message):
    values, coefficients, slot = message
    for step in range(steps):
        ref[pl.ds(step * members, members), :] = values[step]
    rows = list(coefficients) + [slot]
    while len(rows) < EXTRA:
        rows.append(jnp.zeros_like(slot))
    ref[pl.ds(steps * members, EXTRA), :] = jnp.concatenate(rows, axis=0)


def identity_message(steps, members):
    zero = jnp.zeros((members, LANES), F32)
    row = jnp.zeros((1, LANES), F32)
    lane = lax.broadcasted_iota(jnp.int32, (8, LANES), 1).astype(F32)[0:1]
    return [zero] * steps, [row + 1.0] + [row] * (steps - 1), lane


def digit_of(axis, stride, radix):
    return (lax.axis_index(axis) // stride) % radix


def group_kernel(steps, members, axis, stride, radix, final, has_inner, *refs):
    messages = refs[:radix]
    rest = refs[radix:]
    inner = rest[0] if has_inner else None
    outs = rest[1:] if has_inner else rest
    digit = digit_of(axis, stride, radix)
    for mine in range(radix):
        @pl.when(digit == mine)
        def _(mine=mine):
            def message(other):
                return read_message(steps, members, messages[source_of(mine, other, radix)])

            if final:
                value = [jnp.zeros((members, LANES), F32)] * steps
                for other in reversed(range(mine + 1, radix)):
                    if other == radix - 1:
                        value = message(other)[0]
                    else:
                        value = compose(steps, members, message(other), (value, None, None))[0]
                if has_inner and mine < radix - 1:
                    within = read_message(steps, members, inner)
                    value = compose(steps, members, within, (value, None, None))[0]
                elif has_inner:
                    value = read_message(steps, members, inner)[0]
                for step in range(steps):
                    outs[0][pl.ds(step * members, members), :] = value[step]
                return
            total = None
            later = None
            for other in reversed(range(radix)):
                total = message(other) if total is None else compose(steps, members, message(other), total)
                if other == mine + 1:
                    later = total
            if later is None:
                later = identity_message(steps, members)
            if has_inner:
                later = compose(steps, members, read_message(steps, members, inner), later)
            write_message(steps, members, outs[0], later)
            write_message(steps, members, outs[1], total)


def is_power(number):
    return number & (number - 1) == 0


def source_of(mine, other, radix):
    return mine ^ other if is_power(radix) else (other - mine) % radix


def exchange(value, axis, stride, radix, offset):
    pairs = []
    for device in range(lax.axis_size(axis)):
        digit = (device // stride) % radix
        source = digit ^ offset if is_power(radix) else (digit + offset) % radix
        pairs.append((device + (source - digit) * stride, device))
    return lax.ppermute(value, axis, pairs)


def radices_of(count):
    radices = []
    while count > 1:
        radix = next(r for r in (4, 2, 3, 5, 7, count) if count % r == 0)
        radices.append(radix)
        count //= radix
    return radices


def flow_kernel(
    steps, members, blocks,
    flow_ref, lateral_ref, rough_ref, factor_ref, down_ref, exit_ref,
    weight_ref, leaving_ref, slopes_ref,
):
    slopes = slopes_of(rough_ref[...] * factor_ref[...])
    for i in range(4):
        slopes_ref[i] = slopes[i]
    leaving_ref[...] = jnp.zeros_like(leaving_ref)
    sub = lax.broadcasted_iota(jnp.int32, (LANES, LANES), 0)

    def one_block(block, carry):
        place = pl.ds(pl.multiple_of(block * LANES, LANES), LANES)
        row = pl.ds(block, 1)
        into = (sub == jnp.broadcast_to(down_ref[row, :], (LANES, LANES)))
        leave = (sub == jnp.broadcast_to(exit_ref[row, :], (LANES, LANES)))
        table = jnp.concatenate([into, leave], axis=0).astype(F32).astype(jnp.bfloat16)
        flows = flow_ref[:, :, place].reshape((steps + 1) * members, LANES)
        summed = lax.dot_general(
            flows, table, (((1,), (1,)), ((), ())), preferred_element_type=F32
        )
        leaving_ref[...] += summed[:, LANES:]
        inflow = summed[:, :LANES]
        new, old, stay, side = (slopes_ref[i, row, :] for i in range(4))
        for step in range(steps):
            now = inflow[(step + 1) * members:(step + 2) * members]
            prior = inflow[step * members:(step + 1) * members]
            weight_ref[step, :, place] = (
                new * now
                + old * prior
                + stay * flow_ref[step, :, place].astype(F32)
                + side * lateral_ref[step, :, place].astype(F32)
            )
        return carry

    lax.fori_loop(0, blocks, one_block, 0, unroll=2)


def final_kernel(
    steps, members, blocks, ranks,
    incoming_ref, own_ref, response_ref, slot_ref, weight_ref, rough_ref, factor_ref,
    inlet_values_ref, inlet_rows_ref, arriving_ref, inlet_ref,
    grad_ref, *rest,
):
    pieces, (part_ref, side_ref) = rest[:ranks], rest[ranks:]
    travel = rough_ref[...] * factor_ref[...]
    side_ref[...] = 1.0 / (travel * (1.0 - skew_weight) + 0.5)
    shape = (members, LANES)

    def one_block(block, carry):
        place = pl.ds(pl.multiple_of(block * LANES, LANES), LANES)
        row = pl.ds(block, 1)
        index = jnp.broadcast_to(slot_ref[row, :], shape)
        response = [response_ref[lag, row, :] for lag in range(steps)]
        side = side_ref[row, :]
        pulled = [
            take(incoming_ref[pl.ds(step * members, members), :], index) for step in range(steps)
        ]
        total = jnp.zeros(shape, F32)
        for step in range(steps):
            value = own_ref[step, :, place]
            for lag in range(steps - step):
                value = value + response[lag] * pulled[step + lag]
            grad_ref[step, :, place] = (side * value).astype(jnp.bfloat16)
            total = total + value * weight_ref[step, :, place]
        part_ref[row, :] = jnp.sum(total, axis=0, keepdims=True)
        return carry

    lax.fori_loop(0, blocks, one_block, 0, unroll=2)

    rows = inlet_rows_ref[...]
    slope_new, slope_old, _, _ = slopes_of(rows[steps:steps + 1])
    index = jnp.broadcast_to(rows[steps + 1:steps + 2], shape).astype(jnp.int32)
    pulled = [
        take(incoming_ref[pl.ds(step * members, members), :], index) for step in range(steps)
    ]
    total = jnp.zeros(shape, F32)
    for step in range(steps):
        value = inlet_values_ref[pl.ds(step * members, members), :]
        for lag in range(steps - step):
            value = value + rows[lag:lag + 1] * pulled[step + lag]
        total = total + value * (
            slope_new * arriving_ref[pl.ds((step + 1) * members, members), :]
            + slope_old * arriving_ref[pl.ds(step * members, members), :]
        )
    at_inlet = jnp.sum(total, axis=0, keepdims=True)
    inlet = inlet_ref[...]
    inlet_block = inlet // LANES
    inlet_lane = inlet - inlet_block * LANES
    block_rows = lax.broadcasted_iota(jnp.int32, (blocks, LANES), 0)
    spread = jnp.where(block_rows == inlet_block, at_inlet, 0.0)
    lane_table = (
        lax.broadcasted_iota(jnp.int32, (LANES, LANES), 0)
        == jnp.broadcast_to(inlet_lane, (LANES, LANES))
    ).astype(F32)
    placed = lax.dot_general(
        spread, lane_table, (((1,), (1,)), ((), ())),
        precision=lax.Precision.HIGHEST, preferred_element_type=F32,
    )
    part_ref[...] = factor_ref[...] * (part_ref[...] + placed)
    mine = lax.axis_index("mem")
    piece = blocks // ranks
    for offset in range(ranks):
        target = mine ^ offset if is_power(ranks) else (mine + offset) % ranks
        pieces[offset][...] = part_ref[pl.ds(pl.multiple_of(target * piece, piece), piece), :]


def call(kernel, out_shape, scratch=(), flops=0, size=0, name=None):
    return pl.pallas_call(
        kernel,
        out_shape=out_shape,
        scratch_shapes=scratch,
        cost_estimate=pl.CostEstimate(flops=flops, bytes_accessed=size, transcendentals=0),
        name=name,
    )


def body(
    stored_reach_flows, lateral, cotangent, roughness, travel_factor,
    inverse_block_matrix, down_in_block, exit_slot, inlet_reach,
):
    steps, members, reaches = cotangent.shape
    blocks = reaches // LANES
    count = lax.axis_size("net")
    ranks = lax.axis_size("mem")
    rough = roughness.reshape(blocks, LANES)
    factor = travel_factor.reshape(blocks, LANES)
    down = down_in_block.reshape(blocks, LANES)
    leave = exit_slot.reshape(blocks, LANES)
    rows = steps * members + EXTRA
    shape = jax.ShapeDtypeStruct

    own, message, response, slot, inlet_values, inlet_rows = call(
        functools.partial(local_kernel, steps, members, blocks),
        (
            shape((steps, members, reaches), F32),
            shape((rows, LANES), F32),
            shape((steps, blocks, LANES), F32),
            shape((blocks, LANES), jnp.int32),
            shape((steps * members, LANES), F32),
            shape((EXTRA, LANES), F32),
        ),
        scratch=[
            pltpu.VMEM((levels_of(LANES), blocks, LANES), jnp.int32),
            pltpu.VMEM((levels_of(LANES), blocks, LANES), F32),
            pltpu.VMEM((blocks, LANES), F32),
            pltpu.VMEM((blocks, LANES), F32),
        ],
        flops=2 * 7 * steps * members * reaches,
        size=6 * steps * members * reaches,
        name="local",
    )(cotangent, rough, factor, down, leave, inlet_reach)

    weight, leaving = pl.pallas_call(
        functools.partial(flow_kernel, steps, members, blocks),
        out_shape=(
            shape((steps, members, reaches), F32),
            shape(((steps + 1) * members, LANES), F32),
        ),
        scratch_shapes=[pltpu.VMEM((4, blocks, LANES), F32)],
        cost_estimate=pl.CostEstimate(
            flops=4 * 128 * (steps + 1) * members * reaches,
            bytes_accessed=8 * steps * members * reaches, transcendentals=0,
        ),
        name="flows",
    )(stored_reach_flows, lateral, rough, factor, down, leave)
    arriving = lax.ppermute(leaving, "net", [(i, i + 1) for i in range(count - 1)])

    stride = 1
    inner = None
    radices = radices_of(count)
    incoming = None
    for turn, radix in enumerate(radices):
        final = turn == len(radices) - 1
        received = [message] + [
            exchange(message, "net", stride, radix, offset) for offset in range(1, radix)
        ]
        has_inner = inner is not None
        args = received + ([inner] if has_inner else [])
        out = shape((steps * members, LANES), F32) if final else (shape((rows, LANES), F32),) * 2
        result = call(
            functools.partial(group_kernel, steps, members, "net", stride, radix, final, has_inner),
            out, flops=20 * radix * rows * LANES, size=4 * radix * rows * LANES, name="compose",
        )(*args)
        if final:
            incoming = result
        else:
            inner, message = result
        stride *= radix
    if incoming is None:
        incoming = jnp.zeros((steps * members, LANES), F32)

    piece = shape((blocks // ranks, LANES), F32)
    grad_lateral, *pieces = call(
        functools.partial(final_kernel, steps, members, blocks, ranks),
        (shape((steps, members, reaches), jnp.bfloat16),) + (piece,) * ranks,
        scratch=[pltpu.VMEM((blocks, LANES), F32), pltpu.VMEM((blocks, LANES), F32)],
        flops=30 * steps * members * reaches,
        size=10 * steps * members * reaches,
        name="finish",
    )(
        incoming, own, response, slot, weight, rough, factor,
        inlet_values, inlet_rows, arriving, inlet_reach,
    )
    total = pieces[0]
    for offset in range(1, ranks):
        total = total + exchange(pieces[offset], "mem", 1, ranks, (ranks - offset) % ranks if not is_power(ranks) else offset)
    return grad_lateral, total.reshape(-1)


def solution(mesh):
    in_specs = (
        P(None, "mem", "net"),
        P(None, "mem", "net"),
        P(None, "mem", "net"),
        P("net"),
        P("net"),
        P("net", None, None),
        P("net"),
        P("net"),
        P("net", None),
    )
    out_specs = (P(None, "mem", "net"), P(("net", "mem")))
    return jax.shard_map(body, mesh=mesh, in_specs=in_specs, out_specs=out_specs, check_vma=False)
```

time: 501 us -> 76.5 us (0.15)
  matrix products: 229 us -> 0 us
  waiting for transfers between devices: 172 us -> 5.8 us
  Pallas kernels: 0 us -> 53.1 us
  starting transfers between devices: 46.2 us -> 12.8 us
  local copies, waits for them, and re-layouts: 32.1 us -> 2.52 us
  blocking collectives: 10.1 us -> 0 us
  other arithmetic: 7.44 us -> 1.28 us
    dot_general x106 -> x0, matrix products: 226 us -> none  [the longest x32 92.2 us: inlet_rows(): jnp.einsum('mr,er->me', adjoint, placement_rows, precision=lax.Precision....]
    ppermute x33 -> x8, waiting for transfers between devices: 172 us -> 5.8 us  [the longest x7 5.8 us: exchange(): return lax.ppermute(value, axis, pairs)]
    pallas_call x0 -> x5, Pallas kernels: none -> 53.1 us  [the longest x1 37.4 us: body(): call(functools.partial(local_kernel, steps, members, blocks), (shape((ste...]
    ppermute x33 -> x8, starting transfers between devices: 46.2 us -> 12.8 us  [the longest x7 9.07 us: exchange(): return lax.ppermute(value, axis, pairs)]
    squeeze x32 -> x0, local copies, waits for them, and re-layouts: 14.4 us -> none  [one_section(): return (adjoint, received[0], received[1])]
    unnamed x1 -> x0, blocking collectives: 10.1 us -> none
    while x64 -> x0, local copies, waits for them, and re-layouts: 6.55 us -> none
    reduce_sum x2 -> x0, other arithmetic: 5.47 us -> none  [body(): part_sum = jnp.sum(adjoint * factor, axis=0)]
  transfers between devices with their start and end apart: 33 -> 8, of which waited for: 32 -> 3; matrix products, arithmetic and copies ran while one was open for 2% -> 0% of each run, Pallas kernels for 0% -> 13%
where the time goes in v1:
time: 76.5 us; the launch traced here: 76.2 us
  Pallas kernels  53.1 us (69%)
  starting transfers between devices  12.8 us (17%)
  waiting for transfers between devices  5.8 us (8%)
  local copies, waits for them, and re-layouts  2.52 us (3%)
  other arithmetic  1.28 us (2%)
    pallas_call x1, Pallas kernels, body(): call(functools.partial(local_kernel, steps, members, blocks), (shape((ste...  37.4 us
    ppermute x7, starting transfers between devices, exchange(): return lax.ppermute(value, axis, pairs)  9.07 us
    pallas_call x1, Pallas kernels, body(): pl.pallas_call(functools.partial(flow_kernel, steps, members, blocks), ou...  6.46 us
    ppermute x7, waiting for transfers between devices, exchange(): return lax.ppermute(value, axis, pairs)  5.8 us
    pallas_call x1, Pallas kernels, body(): call(functools.partial(final_kernel, steps, members, blocks, ranks), (sha...  5.61 us
    ppermute x1, starting transfers between devices, body(): lax.ppermute(leaving, 'net', [(i, i + 1) for i in range(count - 1)])  3.74 us
    pallas_call x2, Pallas kernels, body(): call(functools.partial(group_kernel, steps, members, 'net', stride, radix...  3.6 us
    unnamed x10, local copies, waits for them, and re-layouts  2.52 us
  transfers between devices with their start and end apart: 8, of which 3 were waited for; matrix products, arithmetic and copies ran while one was open for 0% of the time, Pallas kernels for 13%

profile of v1, /device:TPU:0, one launch (start us, length us, event | category | flops | bytes accessed | tf_op | source)
XLA Modules:
  0.0 76.2 jit_solution(5941244864492956213)
XLA Ops:
  0.6 37.4 %local.1 = (f32[4,32,4096]{2,1,0:T(8,128)}, f32[136,128]{1,0:T(8,128)}, f32[4,32,128]{2,1,0:T(8,128)}, s32[32,128]{1,0:T(8,128)}, f32[128,128]{1,0:T(8,128)}, /*index=5*/f32[8,128]{1,0:T(8,128)}) custom-call(bf16[4,32,4096]{2,1,0:T(8,128)(2,1)} %cot_ref.1, f32[32,128]{1,0:T(8,128)} %bitcast.6, f32[32,128]{1,0:T(8,128)} %bitcast.9, s32[32,128]{1,0:T(8,128)} %bitcast.12, ...), custom_call_target="tpu_custom_call" | custom-call | flops 7340032 | bytes 3145728 | tf_op jit(solution)/shard_map/local/pallas_call | solution.py:407
  38.0 4.0 %collective-permute-start.2 = (f32[136,128]{1,0:T(8,128)}, f32[136,128]{1,0:T(8,128)S(1)}, u32[]{:S(2)}, u32[]{:S(2)}) collective-permute-start(f32[136,128]{1,0:T(8,128)} %get-tuple-element.17.refs_0_), channel_id=1, source_target_pairs={{12,0},{8,4},{4,8},{0,12},{28,16},{24,20},{20,24},{16,28},{13,1},{... | collective-permute-start | bytes 208904 | tf_op jit(solution)/shard_map/ppermute | solution.py:263
  42.0 0.4 collective-permute-start.1
  42.5 0.2 collective-permute-start
  42.6 6.5 %flows.1 = (f32[4,32,4096]{2,1,0:T(8,128)}, f32[160,128]{1,0:T(8,128)}) custom-call(bf16[5,32,4096]{2,1,0:T(8,128)(2,1)} %flow_ref.1, bf16[4,32,4096]{2,1,0:T(8,128)(2,1)} %lateral_ref.1, f32[32,128]{1,0:T(8,128)} %bitcast.7, f32[32,128]{1,0:T(8,128)} %bitcast.10, s32[32,128]{1,0:T(8,128)} %bitcast.13, s32[32,128]{1,0:T(8,128)} %bitcast.15), custom_call_target="tpu_custom_call" | custom-call | flops 335544320 | bytes 4194304 | tf_op jit(solution)/shard_map/flows/pallas_call | solution.py:428
  49.1 3.7 %collective-permute-start.4 = (f32[160,128]{1,0:T(8,128)}, f32[160,128]{1,0:T(8,128)S(1)}, u32[]{:S(2)}, u32[]{:S(2)}) collective-permute-start(f32[160,128]{1,0:T(8,128)} %get-tuple-element.26), channel_id=1, source_target_pairs={{0,4},{4,8},{8,12},{12,16},{16,20},{20,24},{24,28},{1,5},{5,9},{9,... | collective-permute-start | bytes 245768 | tf_op jit(solution)/shard_map/ppermute | solution.py:441
  52.8 0.0 collective-permute-done.2.refs_3_
  52.9 0.0 copy-start.1
  52.9 0.0 collective-permute-done.1.refs_2_
  52.9 0.0 copy-start.2
  52.9 0.0 collective-permute-done.refs_1_
  52.9 0.6 copy-done.1
  53.5 0.0 copy-done.2
  53.5 0.0 copy-start.3
  53.5 0.6 copy-done.3
  54.2 1.9 %compose.2 = (f32[136,128]{1,0:T(8,128)}, f32[136,128]{1,0:T(8,128)}) custom-call(f32[136,128]{1,0:T(8,128)} %get-tuple-element.17.refs_0_, f32[136,128]{1,0:T(8,128)} %copy-done.3, f32[136,128]{1,0:T(8,128)} %copy-done.2, f32[136,128]{1,0:T(8,128)} %copy-done.1), custom_call_target="tpu_custom_call" | custom-call | flops 1392640 | bytes 278528 | tf_op jit(solution)/shard_map/compose/pallas_call | solution.py:455
  56.1 2.6 %collective-permute-start.3 = (f32[136,128]{1,0:T(8,128)}, f32[136,128]{1,0:T(8,128)S(1)}, u32[]{:S(2)}, u32[]{:S(2)}) collective-permute-start(f32[136,128]{1,0:T(8,128)} %get-tuple-element.18.refs_0_), channel_id=1, source_target_pairs={{16,0},{20,4},{24,8},{28,12},{0,16},{4,20},{8,24},{12,28},{17,1},{... | collective-permute-start | bytes 208904 | tf_op jit(solution)/shard_map/ppermute | solution.py:263
  58.7 2.8 %collective-permute-done.3.refs_1_ = f32[136,128]{1,0:T(8,128)S(1)} collective-permute-done((f32[136,128]{1,0:T(8,128)}, f32[136,128]{1,0:T(8,128)S(1)}, u32[]{:S(2)}, u32[]{:S(2)}) %collective-permute-start.3) | collective-permute-done | bytes 69664 | tf_op jit(solution)/shard_map/ppermute | solution.py:263
  61.5 0.0 copy-start.4
  61.5 0.6 copy-done.4
  62.1 1.7 %compose.3.incoming_ref = f32[128,128]{1,0:T(8,128)} custom-call(f32[136,128]{1,0:T(8,128)} %get-tuple-element.18.refs_0_, f32[136,128]{1,0:T(8,128)} %copy-done.4, f32[136,128]{1,0:T(8,128)} %get-tuple-element.19.refs_2_), custom_call_target="tpu_custom_call" | custom-call | flops 696320 | bytes 139264 | tf_op jit(solution)/shard_map/compose/pallas_call | solution.py:455
  63.8 0.0 collective-permute-done.4.arriving_ref
  63.8 0.0 copy-start
  63.8 0.6 copy-done
  64.4 5.6 %finish.1 = (bf16[4,32,4096]{2,1,0:T(8,128)(2,1)}, f32[8,128]{1,0:T(8,128)}, f32[8,128]{1,0:T(8,128)}, f32[8,128]{1,0:T(8,128)}, f32[8,128]{1,0:T(8,128)}) custom-call(f32[128,128]{1,0:T(8,128)} %compose.3.incoming_ref, f32[4,32,4096]{2,1,0:T(8,128)} %get-tuple-element.20.own_ref, f32[4,32,128]{2,1,0:T(8,128)} %get-tuple-element.21.response_ref, ...), custom_call_target="tpu_custom_call" | custom-call | flops 15728640 | bytes 5242880 | tf_op jit(solution)/shard_map/finish/pallas_call | solution.py:468
  70.1 0.0 collective-permute-start.5
  70.1 1.6 %collective-permute-start.6 = (f32[8,128]{1,0:T(8,128)}, f32[8,128]{1,0:T(8,128)S(1)}, u32[]{:S(2)}, u32[]{:S(2)}) collective-permute-start(f32[8,128]{1,0:T(8,128)} %get-tuple-element.30), channel_id=1, source_target_pairs={{2,0},{3,1},{0,2},{1,3},{6,4},{7,5},{4,6},{5,7},{10,8},{11,9},{8,1... | collective-permute-start | bytes 12296 | tf_op jit(solution)/shard_map/ppermute | solution.py:263
  71.6 0.3 collective-permute-start.7
  71.9 0.0 collective-permute-done.5
  71.9 2.0 %collective-permute-done.6 = f32[8,128]{1,0:T(8,128)S(1)} collective-permute-done((f32[8,128]{1,0:T(8,128)}, f32[8,128]{1,0:T(8,128)S(1)}, u32[]{:S(2)}, u32[]{:S(2)}) %collective-permute-start.6) | collective-permute-done | bytes 4128 | tf_op jit(solution)/shard_map/ppermute | solution.py:263
  73.9 0.9 %collective-permute-done.7 = f32[8,128]{1,0:T(8,128)S(1)} collective-permute-done((f32[8,128]{1,0:T(8,128)}, f32[8,128]{1,0:T(8,128)S(1)}, u32[]{:S(2)}, u32[]{:S(2)}) %collective-permute-start.7) | collective-permute-done | bytes 4128 | tf_op jit(solution)/shard_map/ppermute | solution.py:263
  74.9 1.3 %add_bitcast_fusion = f32[1024]{0:T(1024)} fusion(f32[8,128]{1,0:T(8,128)S(1)} %collective-permute-done.7, f32[8,128]{1,0:T(8,128)S(1)} %collective-permute-done.6, f32[8,128]{1,0:T(8,128)} %get-tuple-element.28, f32[8,128]{1,0:T(8,128)S(1)} %collective-permute-done.5), kind=kLoop, calls=%fused_computation | loop fusion | flops 3072 | bytes 20480 | tf_op jit(solution)/shard_map/reshape | solution.py:482
Async XLA Ops:
  38.0 14.8 %collective-permute-start.2 = (f32[136,128]{1,0:T(8,128)}, f32[136,128]{1,0:T(8,128)S(1)}, u32[]{:S(2)}, u32[]{:S(2)}) collective-permute-start(f32[136,128]{1,0:T(8,128)} %get-tuple-element.17.refs_0_), channel_id=1, source_target_pairs={{12,0},{8,4},{4,8},{0,12},{28,16},{24,20},{20,24},{16,28},{13,1},{... | collective-permute-start | bytes 208904 | tf_op jit(solution)/shard_map/ppermute | solution.py:263
  42.0 10.9 %collective-permute-start.1 = (f32[136,128]{1,0:T(8,128)}, f32[136,128]{1,0:T(8,128)S(1)}, u32[]{:S(2)}, u32[]{:S(2)}) collective-permute-start(f32[136,128]{1,0:T(8,128)} %get-tuple-element.17.refs_0_), channel_id=1, source_target_pairs={{8,0},{12,4},{0,8},{4,12},{24,16},{28,20},{16,24},{20,28},{9,1},{1... | collective-permute-start | bytes 208904 | tf_op jit(solution)/shard_map/ppermute | solution.py:263
  42.5 10.4 %collective-permute-start = (f32[136,128]{1,0:T(8,128)}, f32[136,128]{1,0:T(8,128)S(1)}, u32[]{:S(2)}, u32[]{:S(2)}) collective-permute-start(f32[136,128]{1,0:T(8,128)} %get-tuple-element.17.refs_0_), channel_id=1, source_target_pairs={{4,0},{0,4},{12,8},{8,12},{20,16},{16,20},{28,24},{24,28},{5,1},{1... | collective-permute-start | bytes 208904 | tf_op jit(solution)/shard_map/ppermute | solution.py:263
  49.1 14.7 %collective-permute-start.4 = (f32[160,128]{1,0:T(8,128)}, f32[160,128]{1,0:T(8,128)S(1)}, u32[]{:S(2)}, u32[]{:S(2)}) collective-permute-start(f32[160,128]{1,0:T(8,128)} %get-tuple-element.26), channel_id=1, source_target_pairs={{0,4},{4,8},{8,12},{12,16},{16,20},{20,24},{24,28},{1,5},{5,9},{9,... | collective-permute-start | bytes 245768 | tf_op jit(solution)/shard_map/ppermute | solution.py:441
  52.9 0.6 copy-start.1
  52.9 0.6 copy-start.2
  53.5 0.6 copy-start.3
  56.1 5.4 %collective-permute-start.3 = (f32[136,128]{1,0:T(8,128)}, f32[136,128]{1,0:T(8,128)S(1)}, u32[]{:S(2)}, u32[]{:S(2)}) collective-permute-start(f32[136,128]{1,0:T(8,128)} %get-tuple-element.18.refs_0_), channel_id=1, source_target_pairs={{16,0},{20,4},{24,8},{28,12},{0,16},{4,20},{8,24},{12,28},{17,1},{... | collective-permute-start | bytes 208904 | tf_op jit(solution)/shard_map/ppermute | solution.py:263
  61.5 0.6 copy-start.4
  63.8 0.6 copy-start
  70.1 1.9 %collective-permute-start.5 = (f32[8,128]{1,0:T(8,128)}, f32[8,128]{1,0:T(8,128)S(1)}, u32[]{:S(2)}, u32[]{:S(2)}) collective-permute-start(f32[8,128]{1,0:T(8,128)} %get-tuple-element.29), channel_id=1, source_target_pairs={{1,0},{0,1},{3,2},{2,3},{5,4},{4,5},{7,6},{6,7},{9,8},{8,9},{11,10... | collective-permute-start | bytes 12296 | tf_op jit(solution)/shard_map/ppermute | solution.py:263
  70.1 3.9 %collective-permute-start.6 = (f32[8,128]{1,0:T(8,128)}, f32[8,128]{1,0:T(8,128)S(1)}, u32[]{:S(2)}, u32[]{:S(2)}) collective-permute-start(f32[8,128]{1,0:T(8,128)} %get-tuple-element.30), channel_id=1, source_target_pairs={{2,0},{3,1},{0,2},{1,3},{6,4},{7,5},{4,6},{5,7},{10,8},{11,9},{8,1... | collective-permute-start | bytes 12296 | tf_op jit(solution)/shard_map/ppermute | solution.py:263
  71.6 3.2 %collective-permute-start.7 = (f32[8,128]{1,0:T(8,128)}, f32[8,128]{1,0:T(8,128)S(1)}, u32[]{:S(2)}, u32[]{:S(2)}) collective-permute-start(f32[8,128]{1,0:T(8,128)} %get-tuple-element.31), channel_id=1, source_target_pairs={{3,0},{2,1},{1,2},{0,3},{7,4},{6,5},{5,6},{4,7},{11,8},{10,9},{9,1... | collective-permute-start | bytes 12296 | tf_op jit(solution)/shard_map/ppermute | solution.py:263

commit v2 on v1

v2 whole, which is shorter than its diff:
```python
import functools

import jax
import jax.numpy as jnp
from jax import lax
from jax.experimental import pallas as pl
from jax.experimental.pallas import tpu as pltpu
from jax.sharding import PartitionSpec as P

skew_weight = 0.2
LANES = 128
EXTRA = 8
F32 = jnp.float32


ROW_GATHER = lax.GatherDimensionNumbers(
    offset_dims=(), collapsed_slice_dims=(1,), start_index_map=(1,),
    operand_batching_dims=(0,), start_indices_batching_dims=(0,),
)
VMEM_BYTES = 20 << 20
GROUP = 8


def take(values, index):
    return lax.gather(
        values, index[..., None], ROW_GATHER, (1, 1),
        mode=lax.GatherScatterMode.PROMISE_IN_BOUNDS,
    )


def weights_of(travel):
    divisor = travel * (1.0 - skew_weight) + 0.5
    weight_new = (0.5 - travel * skew_weight) / divisor
    weight_old = (0.5 + travel * skew_weight) / divisor
    weight_stay = (travel * (1.0 - skew_weight) - 0.5) / divisor
    return weight_new, weight_old, weight_stay


def slopes_of(travel):
    divisor = travel * (1.0 - skew_weight) + 0.5
    square = divisor * divisor
    return (
        -0.5 / square,
        (skew_weight - 0.5) / square,
        (1.0 - skew_weight) / square,
        (skew_weight - 1.0) / square,
    )


def levels_of(lanes):
    count = 0
    while (1 << count) < lanes:
        count += 1
    return count


def split(value):
    high = value.astype(jnp.bfloat16)
    return high, (value - high.astype(F32)).astype(jnp.bfloat16)


def multiply_series(steps, left, right):
    result = []
    for lag in range(steps):
        total = left[0] * right[lag]
        for first in range(1, lag + 1):
            total = total + left[first] * right[lag - first]
        result.append(total)
    return result


def local_kernel(
    steps, members, blocks,
    cot_ref, matrix_ref, rough_ref, factor_ref, down_ref, exit_ref, inlet_ref,
    own_ref, message_ref, response_ref, slot_ref, inlet_values_ref, inlet_rows_ref,
    stay_ref, ratio_ref,
):
    travel = rough_ref[...] * factor_ref[...]
    weight_new, weight_old, weight_stay = weights_of(travel)
    down = down_ref[...]
    lane = lax.broadcasted_iota(jnp.int32, down.shape, 1)
    interior = down < LANES
    pointer = jnp.where(interior, down, lane)
    next_new = take(weight_new, pointer)
    next_old = take(weight_old, pointer)
    ratio = jnp.where(interior, next_old / next_new, 0.0)
    stay_ref[...] = weight_stay
    ratio_ref[...] = ratio

    inlet = inlet_ref[...]
    inlet_block = inlet // LANES
    inlet_lane = inlet - inlet_block * LANES
    member_lane = jnp.broadcast_to(inlet_lane, (members, LANES))
    member_block = jnp.broadcast_to(inlet_block, (members, LANES))
    at_inlet = [jnp.zeros((members, LANES), F32)] * steps

    def solve_group(first, at_inlet):
        places = range(first, min(first + GROUP, blocks))
        tables = {
            block: jnp.concatenate(split(matrix_ref[block]), axis=1) for block in places
        }
        right, value = {}, {}
        for step in reversed(range(steps)):
            for block in places:
                lanes = pl.ds(block * LANES, LANES)
                row = pl.ds(block, 1)
                source = cot_ref[step, :, lanes]
                if step == steps - 1:
                    right[block] = source.astype(F32)
                    product = jnp.dot(source, tables[block], preferred_element_type=F32)
                    value[block] = product[:, :LANES] + product[:, LANES:]
                else:
                    right[block] = (
                        source.astype(F32)
                        + stay_ref[row, :] * value[block]
                        + ratio_ref[row, :] * (value[block] - right[block])
                    )
                    product = jnp.dot(
                        jnp.concatenate(split(right[block]), axis=0), tables[block],
                        preferred_element_type=F32,
                    )
                    value[block] = product[:members, :LANES] + (
                        product[members:, :LANES] + product[:members, LANES:]
                    )
                own_ref[step, :, lanes] = value[block]
                at_inlet[step] = jnp.where(
                    member_block == block, take(value[block], member_lane), at_inlet[step]
                )
        return at_inlet

    groups = list(range(0, blocks, GROUP))
    for first in groups[:1]:
        at_inlet = solve_group(first, list(at_inlet))

    unit = jnp.where(exit_ref[...] >= 0, 1.0, 0.0).astype(F32)
    response = [unit]
    gain = [jnp.where(interior, next_new, 0.0)]
    base = jnp.where(interior, next_new * weight_stay + next_old, 0.0)
    for lag in range(1, steps):
        response.append(response[-1] * weight_stay)
        gain.append(base)
        base = base * weight_stay
    for level in range(levels_of(LANES)):
        pulled = [take(value, pointer) for value in response]
        added = multiply_series(steps, gain, pulled)
        response = [value + more for value, more in zip(response, added)]
        if level + 1 < levels_of(LANES):
            gain = multiply_series(steps, gain, [take(value, pointer) for value in gain])
        pointer = take(pointer, pointer)
    slot = take(exit_ref[...], pointer)
    slot = jnp.maximum(slot, 0)
    slot_ref[...] = slot
    for lag in range(steps):
        response_ref[lag] = response[lag]

    lane_rows = jnp.broadcast_to(inlet_lane, (blocks, LANES))
    block_rows = lax.broadcasted_iota(jnp.int32, (blocks, LANES), 0)
    chosen = block_rows == jnp.broadcast_to(inlet_block, (blocks, LANES))

    def at_inlets(rows):
        return jnp.sum(jnp.where(chosen, take(rows, lane_rows), 0.0), axis=0, keepdims=True)

    travel_in = at_inlets(travel)
    slot_in = at_inlets(slot.astype(F32))
    response_in = [at_inlets(value) for value in response]
    new_in, old_in, _ = weights_of(travel_in)

    for first in groups[1:]:
        at_inlet = solve_group(first, list(at_inlet))

    for step in range(steps):
        rows = pl.ds(step * members, members)
        inlet_values_ref[rows, :] = at_inlet[step]
        outgoing = new_in * at_inlet[step]
        if step + 1 < steps:
            outgoing = outgoing + old_in * at_inlet[step + 1]
        message_ref[rows, :] = outgoing
    tail = []
    for lag in range(steps):
        coefficient = new_in * response_in[lag]
        if lag > 0:
            coefficient = coefficient + old_in * response_in[lag - 1]
        tail.append(coefficient)
    message_ref[pl.ds(steps * members, EXTRA), :] = eight_rows(tail + [slot_in])
    inlet_rows_ref[...] = eight_rows(response_in + [travel_in, slot_in])


def eight_rows(rows):
    rows = list(rows)
    while len(rows) % EXTRA:
        rows.append(jnp.zeros_like(rows[0]))
    return jnp.concatenate(rows, axis=0)


def compose(steps, members, upper, lower):
    values, coefficients, slot = upper
    below, below_coefficients, below_slot = lower
    index = jnp.broadcast_to(slot, (members, LANES)).astype(jnp.int32)
    pulled = [take(value, index) for value in below]
    result = []
    for step in range(steps):
        total = values[step]
        for lag in range(steps - step):
            total = total + coefficients[lag] * pulled[step + lag]
        result.append(total)
    if below_coefficients is None:
        return result, None, None
    table = eight_rows(list(below_coefficients) + [below_slot])
    table = take(table, jnp.broadcast_to(slot, table.shape).astype(jnp.int32))
    combined = multiply_series(
        steps, coefficients, [table[lag:lag + 1] for lag in range(steps)]
    )
    return result, combined, table[steps:steps + 1]


def read_message(steps, members, ref):
    values = [ref[pl.ds(step * members, members), :] for step in range(steps)]
    tail = ref[pl.ds(steps * members, EXTRA), :]
    return values, [tail[lag:lag + 1] for lag in range(steps)], tail[steps:steps + 1]


def write_message(steps, members, ref, message):
    values, coefficients, slot = message
    for step in range(steps):
        ref[pl.ds(step * members, members), :] = values[step]
    ref[pl.ds(steps * members, EXTRA), :] = eight_rows(list(coefficients) + [slot])


def identity_message(steps, members):
    zero = jnp.zeros((members, LANES), F32)
    row = jnp.zeros((1, LANES), F32)
    lane = lax.broadcasted_iota(jnp.int32, (8, LANES), 1).astype(F32)[0:1]
    return [zero] * steps, [row + 1.0] + [row] * (steps - 1), lane


def digit_of(axis, stride, radix):
    return (lax.axis_index(axis) // stride) % radix


def group_kernel(steps, members, axis, stride, radix, has_inner, *refs):
    messages = refs[:radix]
    inner = refs[radix] if has_inner else None
    outs = refs[radix + has_inner:]
    digit = digit_of(axis, stride, radix)
    for mine in range(radix):
        @pl.when(digit == mine)
        def _(mine=mine):
            total = None
            later = None
            for other in reversed(range(radix)):
                message = read_message(steps, members, messages[source_of(mine, other, radix)])
                total = message if total is None else compose(steps, members, message, total)
                if other == mine + 1:
                    later = total
            if later is None:
                later = identity_message(steps, members)
            if has_inner:
                later = compose(steps, members, read_message(steps, members, inner), later)
            write_message(steps, members, outs[0], later)
            write_message(steps, members, outs[1], total)


def last_round(steps, members, axis, stride, radix, messages, inner, out):
    digit = digit_of(axis, stride, radix)
    for mine in range(radix):
        @pl.when(digit == mine)
        def _(mine=mine):
            value = [jnp.zeros((members, LANES), F32)] * steps
            for other in reversed(range(mine + 1, radix)):
                message = read_message(steps, members, messages[source_of(mine, other, radix)])
                if other == radix - 1:
                    value = message[0]
                else:
                    value = compose(steps, members, message, (value, None, None))[0]
            if inner is not None:
                within = read_message(steps, members, inner)
                if mine == radix - 1:
                    value = within[0]
                else:
                    value = compose(steps, members, within, (value, None, None))[0]
            for step in range(steps):
                out[pl.ds(step * members, members), :] = value[step]


def is_power(number):
    return number & (number - 1) == 0


def source_of(mine, other, radix):
    return mine ^ other if is_power(radix) else (other - mine) % radix


def exchange(value, axis, stride, radix, offset):
    pairs = []
    for device in range(lax.axis_size(axis)):
        digit = (device // stride) % radix
        source = digit ^ offset if is_power(radix) else (digit + offset) % radix
        pairs.append((device + (source - digit) * stride, device))
    return lax.ppermute(value, axis, pairs)


def radices_of(count):
    radices = []
    while count > 1:
        radix = next(r for r in (4, 2, 3, 5, 7, count) if count % r == 0)
        radices.append(radix)
        count //= radix
    return radices or [1]


def leaving_kernel(steps, members, blocks, flow_ref, exit_ref, leaving_ref):
    sub = lax.broadcasted_iota(jnp.int32, (LANES, LANES), 0)
    total = None
    for block in range(blocks):
        lanes = pl.ds(block * LANES, LANES)
        table = (sub == exit_ref[pl.ds(block, 1), :]).astype(F32).astype(jnp.bfloat16)
        flows = flow_ref[:, :, lanes].reshape((steps + 1) * members, LANES)
        part = lax.dot_general(
            flows, table, (((1,), (1,)), ((), ())), preferred_element_type=F32
        )
        total = part if total is None else total + part
    leaving_ref[...] = total


def weight_kernel(
    steps, members, blocks,
    flow_ref, lateral_ref, rough_ref, factor_ref, down_ref, weight_ref, slopes_ref,
):
    slopes = slopes_of(rough_ref[...] * factor_ref[...])
    for i in range(4):
        slopes_ref[i] = slopes[i]
    sub = lax.broadcasted_iota(jnp.int32, (LANES, LANES), 0)

    def one_block(block, carry):
        lanes = pl.ds(pl.multiple_of(block * LANES, LANES), LANES)
        row = pl.ds(block, 1)
        table = (sub == down_ref[row, :]).astype(F32).astype(jnp.bfloat16)
        flows = flow_ref[:, :, lanes].reshape((steps + 1) * members, LANES)
        inflow = lax.dot_general(
            flows, table, (((1,), (1,)), ((), ())), preferred_element_type=F32
        )
        new, old, stay, side = (slopes_ref[i, row, :] for i in range(4))
        for step in range(steps):
            now = inflow[(step + 1) * members:(step + 2) * members]
            prior = inflow[step * members:(step + 1) * members]
            weight_ref[step, :, lanes] = (
                new * now
                + old * prior
                + stay * flow_ref[step, :, lanes].astype(F32)
                + side * lateral_ref[step, :, lanes].astype(F32)
            )
        return carry

    lax.fori_loop(0, blocks, one_block, 0, unroll=4)


def final_kernel(steps, members, blocks, ranks, stride, radix, has_inner, *refs):
    messages, refs = refs[:radix], refs[radix:]
    inner, refs = (refs[0], refs[1:]) if has_inner else (None, refs)
    (
        own_ref, response_ref, slot_ref, weight_ref, rough_ref, factor_ref,
        inlet_values_ref, inlet_rows_ref, arriving_ref, inlet_ref,
    ) = refs[:10]
    grad_ref = refs[10]
    pieces = refs[11:11 + ranks]
    part_ref, side_ref, incoming_ref = refs[11 + ranks:]
    last_round(steps, members, "net", stride, radix, messages, inner, incoming_ref)
    travel = rough_ref[...] * factor_ref[...]
    side_ref[...] = 1.0 / (travel * (1.0 - skew_weight) + 0.5)
    shape = (members, LANES)

    def one_block(block, carry):
        place = pl.ds(pl.multiple_of(block * LANES, LANES), LANES)
        row = pl.ds(block, 1)
        index = jnp.broadcast_to(slot_ref[row, :], shape)
        response = [response_ref[lag, row, :] for lag in range(steps)]
        side = side_ref[row, :]
        pulled = [
            take(incoming_ref[pl.ds(step * members, members), :], index) for step in range(steps)
        ]
        total = jnp.zeros(shape, F32)
        for step in range(steps):
            value = own_ref[step, :, place]
            for lag in range(steps - step):
                value = value + response[lag] * pulled[step + lag]
            grad_ref[step, :, place] = (side * value).astype(jnp.bfloat16)
            total = total + value * weight_ref[step, :, place]
        part_ref[row, :] = jnp.sum(total, axis=0, keepdims=True)
        return carry

    lax.fori_loop(0, blocks, one_block, 0, unroll=4)

    rows = inlet_rows_ref[...]
    slope_new, slope_old, _, _ = slopes_of(rows[steps:steps + 1])
    index = jnp.broadcast_to(rows[steps + 1:steps + 2], shape).astype(jnp.int32)
    pulled = [
        take(incoming_ref[pl.ds(step * members, members), :], index) for step in range(steps)
    ]
    total = jnp.zeros(shape, F32)
    for step in range(steps):
        value = inlet_values_ref[pl.ds(step * members, members), :]
        for lag in range(steps - step):
            value = value + rows[lag:lag + 1] * pulled[step + lag]
        total = total + value * (
            slope_new * arriving_ref[pl.ds((step + 1) * members, members), :]
            + slope_old * arriving_ref[pl.ds(step * members, members), :]
        )
    at_inlet = jnp.sum(total, axis=0, keepdims=True)
    inlet = inlet_ref[...]
    inlet_block = inlet // LANES
    inlet_lane = inlet - inlet_block * LANES
    block_rows = lax.broadcasted_iota(jnp.int32, (blocks, LANES), 0)
    spread = jnp.where(block_rows == inlet_block, at_inlet, 0.0)
    lane_table = (
        lax.broadcasted_iota(jnp.int32, (LANES, LANES), 0)
        == jnp.broadcast_to(inlet_lane, (LANES, LANES))
    ).astype(F32)
    placed = lax.dot_general(
        spread, lane_table, (((1,), (1,)), ((), ())),
        precision=lax.Precision.HIGHEST, preferred_element_type=F32,
    )
    part_ref[...] = factor_ref[...] * (part_ref[...] + placed)
    mine = lax.axis_index("mem")
    piece = blocks // ranks
    for offset in range(ranks):
        target = mine ^ offset if is_power(ranks) else (mine + offset) % ranks
        pieces[offset][...] = part_ref[pl.ds(pl.multiple_of(target * piece, piece), piece), :]


def call(kernel, name, out_shape, scratch=(), flops=0, size=0):
    return pl.pallas_call(
        kernel,
        out_shape=out_shape,
        scratch_shapes=scratch,
        compiler_params=pltpu.CompilerParams(vmem_limit_bytes=VMEM_BYTES),
        cost_estimate=pl.CostEstimate(flops=flops, bytes_accessed=size, transcendentals=0),
        name=name,
    )


def body(
    stored_reach_flows, lateral, cotangent, roughness, travel_factor,
    inverse_block_matrix, down_in_block, exit_slot, inlet_reach,
):
    steps, members, reaches = cotangent.shape
    blocks = reaches // LANES
    count = lax.axis_size("net")
    ranks = lax.axis_size("mem")
    rough = roughness.reshape(blocks, LANES)
    factor = travel_factor.reshape(blocks, LANES)
    down = down_in_block.reshape(blocks, LANES)
    leave = exit_slot.reshape(blocks, LANES)
    rows = steps * members + EXTRA
    shape = jax.ShapeDtypeStruct
    work = steps * members * reaches

    own, message, response, slot, inlet_values, inlet_rows = call(
        functools.partial(local_kernel, steps, members, blocks),
        "local",
        (
            shape((steps, members, reaches), F32),
            shape((rows, LANES), F32),
            shape((steps, blocks, LANES), F32),
            shape((blocks, LANES), jnp.int32),
            shape((steps * members, LANES), F32),
            shape((EXTRA, LANES), F32),
        ),
        scratch=[pltpu.VMEM((blocks, LANES), F32)] * 2,
        flops=8 * LANES * work,
        size=6 * work,
    )(cotangent, inverse_block_matrix, rough, factor, down, leave, inlet_reach)

    leaving = call(
        functools.partial(leaving_kernel, steps, members, blocks),
        "leaving",
        shape(((steps + 1) * members, LANES), F32),
        flops=2 * LANES * work,
        size=2 * work,
    )(stored_reach_flows, leave)
    weight = call(
        functools.partial(weight_kernel, steps, members, blocks),
        "weight",
        shape((steps, members, reaches), F32),
        scratch=[pltpu.VMEM((4, blocks, LANES), F32)],
        flops=2 * LANES * work,
        size=8 * work,
    )(stored_reach_flows, lateral, rough, factor, down)
    arriving = lax.ppermute(leaving, "net", [(i, i + 1) for i in range(count - 1)])

    stride = 1
    inner = ()
    radices = radices_of(count)
    for radix in radices[:-1]:
        received = [message] + [
            exchange(message, "net", stride, radix, offset) for offset in range(1, radix)
        ]
        later, message = call(
            functools.partial(group_kernel, steps, members, "net", stride, radix, len(inner)),
            "compose",
            (shape((rows, LANES), F32),) * 2,
            flops=20 * radix * rows * LANES,
            size=4 * radix * rows * LANES,
        )(*received, *inner)
        inner = (later,)
        stride *= radix
    radix = radices[-1]
    received = [message] + [
        exchange(message, "net", stride, radix, offset) for offset in range(1, radix)
    ]

    piece = shape((blocks // ranks, LANES), F32)
    grad_lateral, *pieces = call(
        functools.partial(
            final_kernel, steps, members, blocks, ranks, stride, radix, len(inner)
        ),
        "finish",
        (shape((steps, members, reaches), jnp.bfloat16),) + (piece,) * ranks,
        scratch=[
            pltpu.VMEM((blocks, LANES), F32),
            pltpu.VMEM((blocks, LANES), F32),
            pltpu.VMEM((steps * members, LANES), F32),
        ],
        flops=30 * work,
        size=10 * work,
    )(
        *received, *inner, own, response, slot, weight, rough, factor,
        inlet_values, inlet_rows, arriving, inlet_reach,
    )
    total = pieces[0]
    for offset in range(1, ranks):
        back = offset if is_power(ranks) else ranks - offset
        total = total + exchange(pieces[offset], "mem", 1, ranks, back)
    return grad_lateral, total.reshape(-1)


def solution(mesh):
    in_specs = (
        P(None, "mem", "net"),
        P(None, "mem", "net"),
        P(None, "mem", "net"),
        P("net"),
        P("net"),
        P("net", None, None),
        P("net"),
        P("net"),
        P("net", None),
    )
    out_specs = (P(None, "mem", "net"), P(("net", "mem")))
    return jax.shard_map(body, mesh=mesh, in_specs=in_specs, out_specs=out_specs, check_vma=False)
```

time: 76.5 us -> 32.6 us (0.43)
  Pallas kernels: 53.1 us -> 8.01 us
  local copies, waits for them, and re-layouts: 2.52 us -> 6.46 us
  waiting for transfers between devices: 5.8 us -> 3.33 us
    pallas_call x3 -> x4, Pallas kernels: 49.5 us -> 7.72 us  [the longest x1 2.61 us: body(): call(functools.partial(final_kernel, steps, members, blocks, ranks, strid...]
    unnamed x10 -> x26, local copies, waits for them, and re-layouts: 2.52 us -> 6.46 us
    pallas_call x2 -> x1, Pallas kernels: 3.6 us -> 0.29 us  [body(): call(functools.partial(group_kernel, steps, members, 'net', stride, radix...]
    ppermute x7, waiting for transfers between devices: 5.8 us -> 3.33 us  [exchange(): return lax.ppermute(value, axis, pairs)]
  transfers between devices with their start and end apart: 8 -> 8, of which waited for: 3 -> 3; matrix products, arithmetic and copies ran while one was open for 0% -> 0% of each run, Pallas kernels for 13% -> 10%
where the time goes in v2:
time: 32.6 us; the launch traced here: 32.1 us
  starting transfers between devices  12.9 us (40%)
  Pallas kernels  8.01 us (25%)
  local copies, waits for them, and re-layouts  6.46 us (20%)
  waiting for transfers between devices  3.33 us (10%)
  between operations  0.74 us (2%)
  other arithmetic  0.6 us (2%)
    ppermute x7, starting transfers between devices, exchange(): return lax.ppermute(value, axis, pairs)  9.21 us
    unnamed x26, local copies, waits for them, and re-layouts  6.46 us
    ppermute x1, starting transfers between devices, body(): lax.ppermute(leaving, 'net', [(i, i + 1) for i in range(count - 1)])  3.74 us
    ppermute x7, waiting for transfers between devices, exchange(): return lax.ppermute(value, axis, pairs)  3.33 us
    pallas_call x1, Pallas kernels, body(): call(functools.partial(final_kernel, steps, members, blocks, ranks, strid...  2.61 us
    pallas_call x1, Pallas kernels, body(): call(functools.partial(local_kernel, steps, members, blocks), 'local', (s...  2.31 us
    pallas_call x1, Pallas kernels, body(): call(functools.partial(weight_kernel, steps, members, blocks), 'weight',...  1.95 us
    pallas_call x1, Pallas kernels, body(): call(functools.partial(leaving_kernel, steps, members, blocks), 'leaving'...  0.84 us
  transfers between devices with their start and end apart: 8, of which 3 were waited for; matrix products, arithmetic and copies ran while one was open for 0% of the time, Pallas kernels for 10%

profile of v2, /device:TPU:0, one launch (start us, length us, event | category | flops | bytes accessed | tf_op | source)
XLA Modules:
  0.0 32.1 jit_solution(2405146059140731440)
XLA Ops:
  0.7 1.7 %copy-done.1 = f32[32,128,128]{2,1,0:T(8,128)S(1)} copy-done((f32[32,128,128]{2,1,0:T(8,128)S(1)}, f32[32,128,128]{2,1,0:T(8,128)}, u32[]{:S(2)}) %copy-start.1) | copy-done | bytes 2097176
  2.3 1.2 %copy-done.3 = bf16[4,32,4096]{2,1,0:T(8,128)(2,1)S(1)} copy-done((bf16[4,32,4096]{2,1,0:T(8,128)(2,1)S(1)}, bf16[4,32,4096]{2,1,0:T(8,128)(2,1)}, u32[]{:S(2)}) %copy-start.3) | copy-done | bytes 1048600
  3.6 0.7 %copy-done.4 = f32[4096]{0:T(1024)S(1)} copy-done((f32[4096]{0:T(1024)S(1)}, f32[4096]{0:T(1024)}, u32[]{:S(2)}) %copy-start.4) | copy-done | bytes 16408
  4.3 0.7 %copy-done.6 = f32[4096]{0:T(1024)S(1)} copy-done((f32[4096]{0:T(1024)S(1)}, f32[4096]{0:T(1024)}, u32[]{:S(2)}) %copy-start.6) | copy-done | bytes 16408
  5.0 0.7 %copy-done.8 = s32[4096]{0:T(1024)S(1)} copy-done((s32[4096]{0:T(1024)S(1)}, s32[4096]{0:T(1024)}, u32[]{:S(2)}) %copy-start.8) | copy-done | bytes 16408
  5.7 0.7 %copy-done.9 = s32[4096]{0:T(1024)S(1)} copy-done((s32[4096]{0:T(1024)S(1)}, s32[4096]{0:T(1024)}, u32[]{:S(2)}) %copy-start.9) | copy-done | bytes 16408
  6.4 0.7 %copy-done.11 = s32[1,128]{1,0:T(1,128)S(1)} copy-done((s32[1,128]{1,0:T(1,128)S(1)}, s32[1,128]{1,0:T(1,128)}, u32[]{:S(2)}) %copy-start.11) | copy-done | bytes 536
  7.1 2.3 %local.1 = (f32[4,32,4096]{2,1,0:T(8,128)S(1)}, f32[136,128]{1,0:T(8,128)S(1)}, f32[4,32,128]{2,1,0:T(8,128)S(1)}, s32[32,128]{1,0:T(8,128)S(1)}, f32[128,128]{1,0:T(8,128)S(1)}, /*index=5*/f32[8,128]{1,0:T(8,128)S(1)}) custom-call(bf16[4,32,4096]{2,1,0:T(8,128)(2,1)S(1)} %copy-done.3, f32[32,128,128]{2,1,0:T(8,128)S(1)} %copy-done.1, ...), custom_call_target="tpu_custom_call" | custom-call | flops 536870912 | bytes 3145728 | tf_op jit(solution)/shard_map/local/pallas_call | solution.py:457
  9.4 4.0 %collective-permute-start.2 = (f32[136,128]{1,0:T(8,128)S(1)}, f32[136,128]{1,0:T(8,128)S(1)}, u32[]{:S(2)}, u32[]{:S(2)}) collective-permute-start(f32[136,128]{1,0:T(8,128)S(1)} %get-tuple-element.15.refs_0_), channel_id=1, source_target_pairs={{12,0},{8,4},{4,8},{0,12},{28,16},{24,20},{20,24},{16,28},{13,1},{... | collective-permute-start | bytes 208904 | tf_op jit(solution)/shard_map/ppermute | solution.py:299
  13.5 0.4 %collective-permute-start.1 = (f32[136,128]{1,0:T(8,128)S(1)}, f32[136,128]{1,0:T(8,128)S(1)}, u32[]{:S(2)}, u32[]{:S(2)}) collective-permute-start(f32[136,128]{1,0:T(8,128)S(1)} %get-tuple-element.15.refs_0_), channel_id=1, source_target_pairs={{8,0},{12,4},{0,8},{4,12},{24,16},{28,20},{16,24},{20,28},{9,1},{1... | collective-permute-start | bytes 208904 | tf_op jit(solution)/shard_map/ppermute | solution.py:299
  13.9 0.2 collective-permute-start
  14.1 0.8 %leaving.1 = f32[160,128]{1,0:T(8,128)S(1)} custom-call(bf16[5,32,4096]{2,1,0:T(8,128)(2,1)S(1)} %copy-done, s32[32,128]{1,0:T(8,128)S(1)} %bitcast.13), custom_call_target="tpu_custom_call" | custom-call | flops 134217728 | bytes 1048576 | tf_op jit(solution)/shard_map/leaving/pallas_call | solution.py:473
  15.0 3.7 %collective-permute-start.4 = (f32[160,128]{1,0:T(8,128)S(1)}, f32[160,128]{1,0:T(8,128)S(1)}, u32[]{:S(2)}, u32[]{:S(2)}) collective-permute-start(f32[160,128]{1,0:T(8,128)S(1)} %leaving.1), channel_id=1, source_target_pairs={{0,4},{4,8},{8,12},{12,16},{16,20},{20,24},{24,28},{1,5},{5,9},{9,... | collective-permute-start | bytes 245768 | tf_op jit(solution)/shard_map/ppermute | solution.py:488
  18.7 0.0 collective-permute-done.2.refs_3_
  18.7 0.0 collective-permute-done.1.refs_2_
  18.7 0.0 collective-permute-done.refs_1_
  18.7 0.3 compose.1
  19.0 0.0 copy-start.12
  19.0 2.7 %collective-permute-start.3 = (f32[136,128]{1,0:T(8,128)S(1)}, f32[136,128]{1,0:T(8,128)S(1)}, u32[]{:S(2)}, u32[]{:S(2)}) collective-permute-start(f32[136,128]{1,0:T(8,128)S(1)} %get-tuple-element.16.refs_0_), channel_id=1, source_target_pairs={{16,0},{20,4},{24,8},{28,12},{0,16},{4,20},{8,24},{12,28},{17,1},{... | collective-permute-start | bytes 208904 | tf_op jit(solution)/shard_map/ppermute | solution.py:299
  21.7 0.0 copy-done.5
  21.7 0.0 copy-done.10
  21.7 2.0 %weight.1.refs_6_ = f32[4,32,4096]{2,1,0:T(8,128)S(1)} custom-call(bf16[5,32,4096]{2,1,0:T(8,128)(2,1)S(1)} %copy-done, bf16[4,32,4096]{2,1,0:T(8,128)(2,1)S(1)} %copy-done.2, f32[32,128]{1,0:T(8,128)S(1)} %bitcast.7, f32[32,128]{1,0:T(8,128)S(1)} %bitcast.10, s32[32,128]{1,0:T(8,128)S(1)} %bitcast.15), custom_call_target="tpu_custom_call" | custom-call | flops 134217728 | bytes 4194304 | tf_op jit(solution)/shard_map/weight/pallas_call | solution.py:480
  23.7 0.0 collective-permute-done.4.refs_11_
  23.7 0.6 %collective-permute-done.3.refs_1_ = f32[136,128]{1,0:T(8,128)S(1)} collective-permute-done((f32[136,128]{1,0:T(8,128)S(1)}, f32[136,128]{1,0:T(8,128)S(1)}, u32[]{:S(2)}, u32[]{:S(2)}) %collective-permute-start.3) | collective-permute-done | bytes 69664 | tf_op jit(solution)/shard_map/ppermute | solution.py:299
  24.3 2.6 %finish.1 = (bf16[4,32,4096]{2,1,0:T(8,128)(2,1)}, f32[8,128]{1,0:T(8,128)S(1)}, f32[8,128]{1,0:T(8,128)S(1)}, f32[8,128]{1,0:T(8,128)S(1)}, f32[8,128]{1,0:T(8,128)S(1)}) custom-call(f32[136,128]{1,0:T(8,128)S(1)} %get-tuple-element.16.refs_0_, f32[136,128]{1,0:T(8,128)S(1)} %collective-permute-done.3.refs_1_, f32[136,128]{1,0:T(8,128)S(1)} %get-tuple-element.17.refs_2_, ...), custom_call_target="tpu_custom_call" | custom-call | flops 15728640 | bytes 5242880 | tf_op jit(solution)/shard_map/finish/pallas_call | solution.py:512
  26.9 0.0 collective-permute-start.5
  26.9 1.5 %collective-permute-start.6 = (f32[8,128]{1,0:T(8,128)S(1)}, f32[8,128]{1,0:T(8,128)S(1)}, u32[]{:S(2)}, u32[]{:S(2)}) collective-permute-start(f32[8,128]{1,0:T(8,128)S(1)} %get-tuple-element.26), channel_id=1, source_target_pairs={{2,0},{3,1},{0,2},{1,3},{6,4},{7,5},{4,6},{5,7},{10,8},{11,9},{8,1... | collective-permute-start | bytes 12296 | tf_op jit(solution)/shard_map/ppermute | solution.py:299
  28.5 0.3 %collective-permute-start.7 = (f32[8,128]{1,0:T(8,128)S(1)}, f32[8,128]{1,0:T(8,128)S(1)}, u32[]{:S(2)}, u32[]{:S(2)}) collective-permute-start(f32[8,128]{1,0:T(8,128)S(1)} %get-tuple-element.27), channel_id=1, source_target_pairs={{3,0},{2,1},{1,2},{0,3},{7,4},{6,5},{5,6},{4,7},{11,8},{10,9},{9,1... | collective-permute-start | bytes 12296 | tf_op jit(solution)/shard_map/ppermute | solution.py:299
  28.8 0.0 collective-permute-done.5
  28.8 1.7 %collective-permute-done.6 = f32[8,128]{1,0:T(8,128)S(1)} collective-permute-done((f32[8,128]{1,0:T(8,128)S(1)}, f32[8,128]{1,0:T(8,128)S(1)}, u32[]{:S(2)}, u32[]{:S(2)}) %collective-permute-start.6) | collective-permute-done | bytes 4128 | tf_op jit(solution)/shard_map/ppermute | solution.py:299
  30.5 0.9 %collective-permute-done.7 = f32[8,128]{1,0:T(8,128)S(1)} collective-permute-done((f32[8,128]{1,0:T(8,128)S(1)}, f32[8,128]{1,0:T(8,128)S(1)}, u32[]{:S(2)}, u32[]{:S(2)}) %collective-permute-start.7) | collective-permute-done | bytes 4128 | tf_op jit(solution)/shard_map/ppermute | solution.py:299
  31.5 0.6 %add_bitcast_fusion = f32[1024]{0:T(1024)} fusion(f32[8,128]{1,0:T(8,128)S(1)} %collective-permute-done.7, f32[8,128]{1,0:T(8,128)S(1)} %collective-permute-done.6, f32[8,128]{1,0:T(8,128)S(1)} %get-tuple-element.24, f32[8,128]{1,0:T(8,128)S(1)} %collective-permute-done.5), kind=kLoop, calls=%fused_computation | loop fusion | flops 3072 | bytes 20480 | tf_op jit(solution)/shard_map/reshape | solution.py:533
  (16 shorter events, 0.0 us)
Async XLA Ops:
  0.6 13.5 %copy-start = (bf16[5,32,4096]{2,1,0:T(8,128)(2,1)S(1)}, bf16[5,32,4096]{2,1,0:T(8,128)(2,1)}, u32[]{:S(2)}) copy-start(bf16[5,32,4096]{2,1,0:T(8,128)(2,1)} %flow_ref.3) | copy-start | bytes 3932164
  0.6 1.7 %copy-start.1 = (f32[32,128,128]{2,1,0:T(8,128)S(1)}, f32[32,128,128]{2,1,0:T(8,128)}, u32[]{:S(2)}) copy-start(f32[32,128,128]{2,1,0:T(8,128)} %matrix_ref.1) | copy-start | bytes 6291460
  2.3 1.2 %copy-start.3 = (bf16[4,32,4096]{2,1,0:T(8,128)(2,1)S(1)}, bf16[4,32,4096]{2,1,0:T(8,128)(2,1)}, u32[]{:S(2)}) copy-start(bf16[4,32,4096]{2,1,0:T(8,128)(2,1)} %cot_ref.1) | copy-start | bytes 3145732
  3.6 0.7 %copy-start.4 = (f32[4096]{0:T(1024)S(1)}, f32[4096]{0:T(1024)}, u32[]{:S(2)}) copy-start(f32[4096]{0:T(1024)} %param.12) | copy-start | bytes 49156
  4.3 0.7 %copy-start.6 = (f32[4096]{0:T(1024)S(1)}, f32[4096]{0:T(1024)}, u32[]{:S(2)}) copy-start(f32[4096]{0:T(1024)} %param.13) | copy-start | bytes 49156
  5.0 0.7 %copy-start.8 = (s32[4096]{0:T(1024)S(1)}, s32[4096]{0:T(1024)}, u32[]{:S(2)}) copy-start(s32[4096]{0:T(1024)} %param.16) | copy-start | bytes 49156
  5.7 0.7 %copy-start.9 = (s32[4096]{0:T(1024)S(1)}, s32[4096]{0:T(1024)}, u32[]{:S(2)}) copy-start(s32[4096]{0:T(1024)} %param.15) | copy-start | bytes 49156
  6.4 0.7 %copy-start.11 = (s32[1,128]{1,0:T(1,128)S(1)}, s32[1,128]{1,0:T(1,128)}, u32[]{:S(2)}) copy-start(s32[1,128]{1,0:T(1,128)} %refs_12_.1) | copy-start | bytes 1540
  7.1 14.6 %copy-start.2 = (bf16[4,32,4096]{2,1,0:T(8,128)(2,1)S(1)}, bf16[4,32,4096]{2,1,0:T(8,128)(2,1)}, u32[]{:S(2)}) copy-start(bf16[4,32,4096]{2,1,0:T(8,128)(2,1)} %lateral_ref.1) | copy-start | bytes 3145732
  7.1 14.6 %copy-start.5 = (f32[4096]{0:T(1024)S(1)}, f32[4096]{0:T(1024)}, u32[]{:S(2)}) copy-start(f32[4096]{0:T(1024)} %param.12) | copy-start | bytes 49156
  7.1 14.6 %copy-start.7 = (f32[4096]{0:T(1024)S(1)}, f32[4096]{0:T(1024)}, u32[]{:S(2)}) copy-start(f32[4096]{0:T(1024)} %param.13) | copy-start | bytes 49156
  7.1 14.6 %copy-start.10 = (s32[4096]{0:T(1024)S(1)}, s32[4096]{0:T(1024)}, u32[]{:S(2)}) copy-start(s32[4096]{0:T(1024)} %param.15) | copy-start | bytes 49156
  9.4 9.3 %collective-permute-start.2 = (f32[136,128]{1,0:T(8,128)S(1)}, f32[136,128]{1,0:T(8,128)S(1)}, u32[]{:S(2)}, u32[]{:S(2)}) collective-permute-start(f32[136,128]{1,0:T(8,128)S(1)} %get-tuple-element.15.refs_0_), channel_id=1, source_target_pairs={{12,0},{8,4},{4,8},{0,12},{28,16},{24,20},{20,24},{16,28},{13,1},{... | collective-permute-start | bytes 208904 | tf_op jit(solution)/shard_map/ppermute | solution.py:299
  13.5 5.2 %collective-permute-start.1 = (f32[136,128]{1,0:T(8,128)S(1)}, f32[136,128]{1,0:T(8,128)S(1)}, u32[]{:S(2)}, u32[]{:S(2)}) collective-permute-start(f32[136,128]{1,0:T(8,128)S(1)} %get-tuple-element.15.refs_0_), channel_id=1, source_target_pairs={{8,0},{12,4},{0,8},{4,12},{24,16},{28,20},{16,24},{20,28},{9,1},{1... | collective-permute-start | bytes 208904 | tf_op jit(solution)/shard_map/ppermute | solution.py:299
  13.9 4.8 %collective-permute-start = (f32[136,128]{1,0:T(8,128)S(1)}, f32[136,128]{1,0:T(8,128)S(1)}, u32[]{:S(2)}, u32[]{:S(2)}) collective-permute-start(f32[136,128]{1,0:T(8,128)S(1)} %get-tuple-element.15.refs_0_), channel_id=1, source_target_pairs={{4,0},{0,4},{12,8},{8,12},{20,16},{16,20},{28,24},{24,28},{5,1},{1... | collective-permute-start | bytes 208904 | tf_op jit(solution)/shard_map/ppermute | solution.py:299
  15.0 8.7 %collective-permute-start.4 = (f32[160,128]{1,0:T(8,128)S(1)}, f32[160,128]{1,0:T(8,128)S(1)}, u32[]{:S(2)}, u32[]{:S(2)}) collective-permute-start(f32[160,128]{1,0:T(8,128)S(1)} %leaving.1), channel_id=1, source_target_pairs={{0,4},{4,8},{8,12},{12,16},{16,20},{20,24},{24,28},{1,5},{5,9},{9,... | collective-permute-start | bytes 245768 | tf_op jit(solution)/shard_map/ppermute | solution.py:488
  19.0 5.3 %copy-start.12 = (s32[1,128]{1,0:T(1,128)S(1)}, s32[1,128]{1,0:T(1,128)}, u32[]{:S(2)}) copy-start(s32[1,128]{1,0:T(1,128)} %refs_12_.1) | copy-start | bytes 1540
  19.0 5.3 %collective-permute-start.3 = (f32[136,128]{1,0:T(8,128)S(1)}, f32[136,128]{1,0:T(8,128)S(1)}, u32[]{:S(2)}, u32[]{:S(2)}) collective-permute-start(f32[136,128]{1,0:T(8,128)S(1)} %get-tuple-element.16.refs_0_), channel_id=1, source_target_pairs={{16,0},{20,4},{24,8},{28,12},{0,16},{4,20},{8,24},{12,28},{17,1},{... | collective-permute-start | bytes 208904 | tf_op jit(solution)/shard_map/ppermute | solution.py:299
  26.9 1.9 %collective-permute-start.5 = (f32[8,128]{1,0:T(8,128)S(1)}, f32[8,128]{1,0:T(8,128)S(1)}, u32[]{:S(2)}, u32[]{:S(2)}) collective-permute-start(f32[8,128]{1,0:T(8,128)S(1)} %get-tuple-element.25), channel_id=1, source_target_pairs={{1,0},{0,1},{3,2},{2,3},{5,4},{4,5},{7,6},{6,7},{9,8},{8,9},{11,10... | collective-permute-start | bytes 12296 | tf_op jit(solution)/shard_map/ppermute | solution.py:299
  26.9 3.6 %collective-permute-start.6 = (f32[8,128]{1,0:T(8,128)S(1)}, f32[8,128]{1,0:T(8,128)S(1)}, u32[]{:S(2)}, u32[]{:S(2)}) collective-permute-start(f32[8,128]{1,0:T(8,128)S(1)} %get-tuple-element.26), channel_id=1, source_target_pairs={{2,0},{3,1},{0,2},{1,3},{6,4},{7,5},{4,6},{5,7},{10,8},{11,9},{8,1... | collective-permute-start | bytes 12296 | tf_op jit(solution)/shard_map/ppermute | solution.py:299
  28.5 3.0 %collective-permute-start.7 = (f32[8,128]{1,0:T(8,128)S(1)}, f32[8,128]{1,0:T(8,128)S(1)}, u32[]{:S(2)}, u32[]{:S(2)}) collective-permute-start(f32[8,128]{1,0:T(8,128)S(1)} %get-tuple-element.27), channel_id=1, source_target_pairs={{3,0},{2,1},{1,2},{0,3},{7,4},{6,5},{5,6},{4,7},{11,8},{10,9},{9,1... | collective-permute-start | bytes 12296 | tf_op jit(solution)/shard_map/ppermute | solution.py:299

commit v3 on v2

--- a/solution.py
+++ b/solution.py
@@ -6,6 +6,7 @@
 from jax.experimental import pallas as pl
 from jax.experimental.pallas import tpu as pltpu
 from jax.sharding import PartitionSpec as P
+
 
 skew_weight = 0.2
 LANES = 128
@@ -71,10 +72,40 @@
 
 def local_kernel(
     steps, members, blocks,
-    cot_ref, matrix_ref, rough_ref, factor_ref, down_ref, exit_ref, inlet_ref,
+    cot_hbm, matrix_hbm, rough_hbm, factor_hbm, down_hbm, exit_hbm, inlet_hbm,
     own_ref, message_ref, response_ref, slot_ref, inlet_values_ref, inlet_rows_ref,
     stay_ref, ratio_ref,
+    cot_ref, matrix_ref, rough_ref, factor_ref, down_ref, exit_ref, inlet_ref,
+    small_sem, cot_sem, matrix_sem,
 ):
+    groups = list(range(0, blocks, GROUP))
+    small = [
+        pltpu.make_async_copy(source, target, small_sem.at[i])
+        for i, (source, target) in enumerate((
+            (rough_hbm, rough_ref), (factor_hbm, factor_ref), (down_hbm, down_ref),
+            (exit_hbm, exit_ref), (inlet_hbm, inlet_ref),
+        ))
+    ]
+    large = []
+    for i, first in enumerate(groups):
+        size = min(GROUP, blocks - first)
+        lanes = pl.ds(first * LANES, size * LANES)
+        large.append((
+            pltpu.make_async_copy(
+                matrix_hbm.at[pl.ds(first, size)], matrix_ref.at[pl.ds(first, size)], matrix_sem.at[i]
+            ),
+            pltpu.make_async_copy(
+                cot_hbm.at[:, :, lanes], cot_ref.at[:, :, lanes], cot_sem.at[i]
+            ),
+        ))
+    for copy in small:
+        copy.start()
+    for pair in large:
+        for copy in pair:
+            copy.start()
+    for copy in small:
+        copy.wait()
+
     travel = rough_ref[...] * factor_ref[...]
     weight_new, weight_old, weight_stay = weights_of(travel)
     down = down_ref[...]
@@ -128,15 +159,11 @@
                 )
         return at_inlet
 
-    groups = list(range(0, blocks, GROUP))
-    for first in groups[:1]:
-        at_inlet = solve_group(first, list(at_inlet))
-
     unit = jnp.where(exit_ref[...] >= 0, 1.0, 0.0).astype(F32)
     response = [unit]
     gain = [jnp.where(interior, next_new, 0.0)]
     base = jnp.where(interior, next_new * weight_stay + next_old, 0.0)
-    for lag in range(1, steps):
+    for _ in range(1, steps):
         response.append(response[-1] * weight_stay)
         gain.append(base)
         base = base * weight_stay
@@ -165,7 +192,9 @@
     response_in = [at_inlets(value) for value in response]
     new_in, old_in, _ = weights_of(travel_in)
 
-    for first in groups[1:]:
+    for first, pair in zip(groups, large):
+        for copy in pair:
+            copy.wait()
         at_inlet = solve_group(first, list(at_inlet))
 
     for step in range(steps):
@@ -324,7 +353,8 @@
 
 def weight_kernel(
     steps, members, blocks,
-    flow_ref, lateral_ref, rough_ref, factor_ref, down_ref, weight_ref, slopes_ref,
+    flow_ref, lateral_ref, own_ref, rough_ref, factor_ref, down_ref,
+    weight_ref, part_ref, slopes_ref,
 ):
     slopes = slopes_of(rough_ref[...] * factor_ref[...])
     for i in range(4):
@@ -340,52 +370,53 @@
             flows, table, (((1,), (1,)), ((), ())), preferred_element_type=F32
         )
         new, old, stay, side = (slopes_ref[i, row, :] for i in range(4))
+        total = jnp.zeros((members, LANES), F32)
         for step in range(steps):
             now = inflow[(step + 1) * members:(step + 2) * members]
             prior = inflow[step * members:(step + 1) * members]
-            weight_ref[step, :, lanes] = (
+            weight = (
                 new * now
                 + old * prior
                 + stay * flow_ref[step, :, lanes].astype(F32)
                 + side * lateral_ref[step, :, lanes].astype(F32)
             )
+            weight_ref[step, :, lanes] = weight
+            total = total + weight * own_ref[step, :, lanes]
+        part_ref[row, :] = jnp.sum(total, axis=0, keepdims=True)
         return carry
 
     lax.fori_loop(0, blocks, one_block, 0, unroll=4)
 
 
-def final_kernel(steps, members, blocks, ranks, stride, radix, has_inner, *refs):
+def sums_kernel(steps, members, blocks, ranks, stride, radix, has_inner, *refs):
     messages, refs = refs[:radix], refs[radix:]
     inner, refs = (refs[0], refs[1:]) if has_inner else (None, refs)
     (
-        own_ref, response_ref, slot_ref, weight_ref, rough_ref, factor_ref,
+        response_ref, slot_ref, weight_ref, own_part_ref, factor_ref,
         inlet_values_ref, inlet_rows_ref, arriving_ref, inlet_ref,
-    ) = refs[:10]
-    grad_ref = refs[10]
-    pieces = refs[11:11 + ranks]
-    part_ref, side_ref, incoming_ref = refs[11 + ranks:]
+    ) = refs[:9]
+    incoming_ref = refs[9]
+    pieces = refs[10:10 + ranks]
+    (part_ref,) = refs[10 + ranks:]
     last_round(steps, members, "net", stride, radix, messages, inner, incoming_ref)
-    travel = rough_ref[...] * factor_ref[...]
-    side_ref[...] = 1.0 / (travel * (1.0 - skew_weight) + 0.5)
     shape = (members, LANES)
 
     def one_block(block, carry):
-        place = pl.ds(pl.multiple_of(block * LANES, LANES), LANES)
+        lanes = pl.ds(pl.multiple_of(block * LANES, LANES), LANES)
         row = pl.ds(block, 1)
         index = jnp.broadcast_to(slot_ref[row, :], shape)
-        response = [response_ref[lag, row, :] for lag in range(steps)]
-        side = side_ref[row, :]
         pulled = [
             take(incoming_ref[pl.ds(step * members, members), :], index) for step in range(steps)
         ]
-        total = jnp.zeros(shape, F32)
-        for step in range(steps):
-            value = own_ref[step, :, place]
-            for lag in range(steps - step):
-                value = value + response[lag] * pulled[step + lag]
-            grad_ref[step, :, place] = (side * value).astype(jnp.bfloat16)
-            total = total + value * weight_ref[step, :, place]
-        part_ref[row, :] = jnp.sum(total, axis=0, keepdims=True)
+        weight = [weight_ref[step, :, lanes] for step in range(steps)]
+        total = None
+        for lag in range(steps):
+            inside = pulled[lag] * weight[0]
+            for step in range(1, steps - lag):
+                inside = inside + pulled[step + lag] * weight[step]
+            inside = response_ref[lag, row, :] * inside
+            total = inside if total is None else total + inside
+        part_ref[row, :] = own_part_ref[row, :] + jnp.sum(total, axis=0, keepdims=True)
         return carry
 
     lax.fori_loop(0, blocks, one_block, 0, unroll=4)
@@ -427,18 +458,42 @@
         pieces[offset][...] = part_ref[pl.ds(pl.multiple_of(target * piece, piece), piece), :]
 
 
-def call(kernel, name, out_shape, scratch=(), flops=0, size=0):
+def grad_kernel(
+    steps, members, blocks,
+    incoming_ref, own_ref, response_ref, slot_ref, rough_ref, factor_ref, grad_ref, side_ref,
+):
+    side_ref[...] = 1.0 / (rough_ref[...] * factor_ref[...] * (1.0 - skew_weight) + 0.5)
+    shape = (members, LANES)
+
+    def one_block(block, carry):
+        lanes = pl.ds(pl.multiple_of(block * LANES, LANES), LANES)
+        row = pl.ds(block, 1)
+        index = jnp.broadcast_to(slot_ref[row, :], shape)
+        pulled = [
+            take(incoming_ref[pl.ds(step * members, members), :], index) for step in range(steps)
+        ]
+        for step in range(steps):
+            value = own_ref[step, :, lanes]
+            for lag in range(steps - step):
+                value = value + response_ref[lag, row, :] * pulled[step + lag]
+            grad_ref[step, :, lanes] = (side_ref[row, :] * value).astype(jnp.bfloat16)
+        return carry
+
+    lax.fori_loop(0, blocks, one_block, 0, unroll=4)
+
+
+def call(kernel, out_shape, scratch=(), flops=0, size=0, **specs):
     return pl.pallas_call(
         kernel,
         out_shape=out_shape,
+        **specs,
         scratch_shapes=scratch,
         compiler_params=pltpu.CompilerParams(vmem_limit_bytes=VMEM_BYTES),
         cost_estimate=pl.CostEstimate(flops=flops, bytes_accessed=size, transcendentals=0),
-        name=name,
-    )
-
-
-def body(
+    )
+
+
+def gradients(
     stored_reach_flows, lateral, cotangent, roughness, travel_factor,
     inverse_block_matrix, down_in_block, exit_slot, inlet_reach,
 ):
@@ -454,9 +509,15 @@
     shape = jax.ShapeDtypeStruct
     work = steps * members * reaches
 
+    inputs = [
+        pltpu.with_memory_space_constraint(array, pltpu.HBM)
+        for array in (
+            cotangent, inverse_block_matrix, rough, factor, down, leave, inlet_reach
+        )
+    ]
+    turns = -(-blocks // GROUP)
     own, message, response, slot, inlet_values, inlet_rows = call(
         functools.partial(local_kernel, steps, members, blocks),
-        "local",
         (
             shape((steps, members, reaches), F32),
             shape((rows, LANES), F32),
@@ -465,38 +526,47 @@
             shape((steps * members, LANES), F32),
             shape((EXTRA, LANES), F32),
         ),
-        scratch=[pltpu.VMEM((blocks, LANES), F32)] * 2,
+        scratch=[pltpu.VMEM((blocks, LANES), F32)] * 2 + [
+            pltpu.VMEM(array.shape, array.dtype) for array in inputs
+        ] + [
+            pltpu.SemaphoreType.DMA((5,)),
+            pltpu.SemaphoreType.DMA((turns,)),
+            pltpu.SemaphoreType.DMA((turns,)),
+        ],
         flops=8 * LANES * work,
         size=6 * work,
-    )(cotangent, inverse_block_matrix, rough, factor, down, leave, inlet_reach)
+        in_specs=[pl.BlockSpec(memory_space=pltpu.HBM)] * len(inputs),
+    )(*inputs)
+    stored_reach_flows, lateral, message = lax.optimization_barrier(
+        (stored_reach_flows, lateral, message)
+    )
 
     leaving = call(
         functools.partial(leaving_kernel, steps, members, blocks),
-        "leaving",
         shape(((steps + 1) * members, LANES), F32),
         flops=2 * LANES * work,
         size=2 * work,
     )(stored_reach_flows, leave)
-    weight = call(
+    weight, own_part = call(
         functools.partial(weight_kernel, steps, members, blocks),
-        "weight",
-        shape((steps, members, reaches), F32),
+        (shape((steps, members, reaches), F32), shape((blocks, LANES), F32)),
         scratch=[pltpu.VMEM((4, blocks, LANES), F32)],
         flops=2 * LANES * work,
         size=8 * work,
-    )(stored_reach_flows, lateral, rough, factor, down)
-    arriving = lax.ppermute(leaving, "net", [(i, i + 1) for i in range(count - 1)])
+    )(stored_reach_flows, lateral, own, rough, factor, down)
 
     stride = 1
     inner = ()
     radices = radices_of(count)
-    for radix in radices[:-1]:
-        received = [message] + [
+    for turn, radix in enumerate(radices[:-1]):
+        received = [
             exchange(message, "net", stride, radix, offset) for offset in range(1, radix)
         ]
+        if turn == 0:
+            message, leaving, weight = lax.optimization_barrier((message, leaving, weight))
+        received = [message] + received
         later, message = call(
             functools.partial(group_kernel, steps, members, "net", stride, radix, len(inner)),
-            "compose",
             (shape((rows, LANES), F32),) * 2,
             flops=20 * radix * rows * LANES,
             size=4 * radix * rows * LANES,
@@ -504,28 +574,32 @@
         inner = (later,)
         stride *= radix
     radix = radices[-1]
+    message, leaving = lax.optimization_barrier((message, leaving))
     received = [message] + [
         exchange(message, "net", stride, radix, offset) for offset in range(1, radix)
     ]
+    arriving = lax.ppermute(leaving, "net", [(i, i + 1) for i in range(count - 1)])
 
     piece = shape((blocks // ranks, LANES), F32)
-    grad_lateral, *pieces = call(
+    incoming, *pieces = call(
         functools.partial(
-            final_kernel, steps, members, blocks, ranks, stride, radix, len(inner)
+            sums_kernel, steps, members, blocks, ranks, stride, radix, len(inner)
         ),
-        "finish",
-        (shape((steps, members, reaches), jnp.bfloat16),) + (piece,) * ranks,
-        scratch=[
-            pltpu.VMEM((blocks, LANES), F32),
-            pltpu.VMEM((blocks, LANES), F32),
-            pltpu.VMEM((steps * members, LANES), F32),
-        ],
+        (shape((steps * members, LANES), F32),) + (piece,) * ranks,
+        scratch=[pltpu.VMEM((blocks, LANES), F32)],
+        flops=20 * work,
+        size=4 * work,
+    )(
+        *received, *inner, response, slot, weight, own_part, factor,
+        inlet_values, inlet_rows, arriving, inlet_reach,
+    )
+    grad_lateral = call(
+        functools.partial(grad_kernel, steps, members, blocks),
+        shape((steps, members, reaches), jnp.bfloat16),
+        scratch=[pltpu.VMEM((blocks, LANES), F32)],
         flops=30 * work,
-        size=10 * work,
-    )(
-        *received, *inner, own, response, slot, weight, rough, factor,
-        inlet_values, inlet_rows, arriving, inlet_reach,
-    )
+        size=6 * work,
+    )(incoming, own, response, slot, rough, factor)
     total = pieces[0]
     for offset in range(1, ranks):
         back = offset if is_power(ranks) else ranks - offset
@@ -546,4 +620,4 @@
         P("net", None),
     )
     out_specs = (P(None, "mem", "net"), P(("net", "mem")))
-    return jax.shard_map(body, mesh=mesh, in_specs=in_specs, out_specs=out_specs, check_vma=False)
+    return jax.shard_map(gradients, mesh=mesh, in_specs=in_specs, out_specs=out_specs, check_vma=False)

time: 32.6 us -> 30.6 us (0.939)
  local copies, waits for them, and re-layouts: 6.46 us -> 0.03 us
  Pallas kernels: 8.01 us -> 12.8 us
  starting transfers between devices: 12.9 us -> 11.9 us
  waiting for transfers between devices: 3.33 us -> 4.28 us
    unnamed x26 -> x14, local copies, waits for them, and re-layouts: 6.46 us -> 0.03 us
    pallas_call x5 -> x6, Pallas kernels: 8.01 us -> 12.8 us  [the longest x1 5.58 us: gradients(): call(functools.partial(local_kernel, steps, members, blocks), (shape((ste...]
    ppermute x1, starting transfers between devices: 3.74 us -> 2.64 us  [gradients(): lax.ppermute(leaving, 'net', [(i, i + 1) for i in range(count - 1)])]
    ppermute x7, waiting for transfers between devices: 3.33 us -> 4.27 us  [exchange(): return lax.ppermute(value, axis, pairs)]
  transfers between devices with their start and end apart: 8 -> 8, of which waited for: 3 -> 4; matrix products, arithmetic and copies ran while one was open for 0% -> 0% of each run, Pallas kernels for 10% -> 17%
where the time goes in v3:
time: 30.6 us; the launch traced here: 30.4 us
  Pallas kernels  12.8 us (42%)
  starting transfers between devices  11.9 us (39%)
  waiting for transfers between devices  4.28 us (14%)
  between operations  0.78 us (3%)
  other arithmetic  0.6 us (2%)
    ppermute x7, starting transfers between devices, exchange(): return lax.ppermute(value, axis, pairs)  9.25 us
    pallas_call x1, Pallas kernels, gradients(): call(functools.partial(local_kernel, steps, members, blocks), (shape((ste...  5.58 us
    ppermute x7, waiting for transfers between devices, exchange(): return lax.ppermute(value, axis, pairs)  4.27 us
    ppermute x1, starting transfers between devices, gradients(): lax.ppermute(leaving, 'net', [(i, i + 1) for i in range(count - 1)])  2.64 us
    pallas_call x1, Pallas kernels, gradients(): call(functools.partial(grad_kernel, steps, members, blocks), shape((steps...  2.27 us
    pallas_call x1, Pallas kernels, gradients(): call(functools.partial(weight_kernel, steps, members, blocks), (shape((st...  2.06 us
    pallas_call x1, Pallas kernels, gradients(): call(functools.partial(sums_kernel, steps, members, blocks, ranks, stride...  1.81 us
    pallas_call x1, Pallas kernels, gradients(): call(functools.partial(leaving_kernel, steps, members, blocks), shape(((s...  0.84 us
  transfers between devices with their start and end apart: 8, of which 4 were waited for; matrix products, arithmetic and copies ran while one was open for 0% of the time, Pallas kernels for 17%

profile of v3, /device:TPU:0, one launch (start us, length us, event | category | flops | bytes accessed | tf_op | source)
XLA Modules:
  0.0 30.4 jit_solution(5301530038968917799)
XLA Ops:
  0.6 0.0 copy-start.4
  0.6 0.0 copy-start
  0.7 0.0 copy-start.1
  0.7 0.0 copy-start.2
  0.7 0.0 copy-start.3
  0.7 0.0 copy-start.5
  0.7 5.6 %shard_map.104 = (f32[4,32,4096]{2,1,0:T(8,128)S(1)}, f32[136,128]{1,0:T(8,128)S(1)}, f32[4,32,128]{2,1,0:T(8,128)S(1)}, s32[32,128]{1,0:T(8,128)S(1)}, f32[128,128]{1,0:T(8,128)S(1)}, /*index=5*/f32[8,128]{1,0:T(8,128)S(1)}) custom-call(bf16[4,32,4096]{2,1,0:T(8,128)(2,1)} %cot_hbm.1, f32[32,128,128]{2,1,0:T(8,128)} %matrix_hbm.1, f32[32,128]{1,0:T(8,128)} %bitcast.10, ...), custom_call_target="tpu_custom_call" | custom-call | flops 536870912 | bytes 3145728 | tf_op jit(solution)/shard_map/pallas_call | solution.py:519
  6.3 4.0 %collective-permute-start.2 = (f32[136,128]{1,0:T(8,128)S(1)}, f32[136,128]{1,0:T(8,128)S(1)}, u32[]{:S(2)}, u32[]{:S(2)}) collective-permute-start(f32[136,128]{1,0:T(8,128)S(1)} %get-tuple-element.31.refs_0_), channel_id=1, source_target_pairs={{12,0},{8,4},{4,8},{0,12},{28,16},{24,20},{20,24},{16,28},{13,1},{... | collective-permute-start | bytes 208904 | tf_op jit(solution)/shard_map/ppermute | solution.py:328
  10.3 0.5 %collective-permute-start.1 = (f32[136,128]{1,0:T(8,128)S(1)}, f32[136,128]{1,0:T(8,128)S(1)}, u32[]{:S(2)}, u32[]{:S(2)}) collective-permute-start(f32[136,128]{1,0:T(8,128)S(1)} %get-tuple-element.31.refs_0_), channel_id=1, source_target_pairs={{8,0},{12,4},{0,8},{4,12},{24,16},{28,20},{16,24},{20,28},{9,1},{1... | collective-permute-start | bytes 208904 | tf_op jit(solution)/shard_map/ppermute | solution.py:328
  10.8 0.2 collective-permute-start
  11.0 0.0 copy-done.4
  11.0 0.0 copy-done
  11.0 0.8 %shard_map.105 = f32[160,128]{1,0:T(8,128)S(1)} custom-call(bf16[5,32,4096]{2,1,0:T(8,128)(2,1)S(1)} %copy-done, s32[32,128]{1,0:T(8,128)S(1)} %bitcast.14), custom_call_target="tpu_custom_call" | custom-call | flops 134217728 | bytes 1048576 | tf_op jit(solution)/shard_map/pallas_call | solution.py:544
  11.8 0.0 copy-start.6
  11.9 2.1 %shard_map.106 = (f32[4,32,4096]{2,1,0:T(8,128)S(1)}, f32[32,128]{1,0:T(8,128)S(1)}) custom-call(bf16[5,32,4096]{2,1,0:T(8,128)(2,1)S(1)} %copy-done, bf16[4,32,4096]{2,1,0:T(8,128)(2,1)S(1)} %copy-done.1, f32[4,32,4096]{2,1,0:T(8,128)S(1)} %get-tuple-element.29.own_ref, f32[32,128]{1,0:T(8,128)S(1)} %bitcast.11, f32[32,128]{1,0:T(8,128)S(1)} %bitcast.7, ...), custom_call_target="tpu_custom_call" | custom-call | flops 134217728 | bytes 4194304 | tf_op jit(solution)/shard_map/pallas_call | solution.py:550
  13.9 0.0 collective-permute-done.2.refs_3_
  13.9 0.7 %collective-permute-done.1.refs_2_ = f32[136,128]{1,0:T(8,128)S(1)} collective-permute-done((f32[136,128]{1,0:T(8,128)S(1)}, f32[136,128]{1,0:T(8,128)S(1)}, u32[]{:S(2)}, u32[]{:S(2)}) %collective-permute-start.1) | collective-permute-done | bytes 69664 | tf_op jit(solution)/shard_map/ppermute | solution.py:328
  14.6 0.5 %collective-permute-done.refs_1_ = f32[136,128]{1,0:T(8,128)S(1)} collective-permute-done((f32[136,128]{1,0:T(8,128)S(1)}, f32[136,128]{1,0:T(8,128)S(1)}, u32[]{:S(2)}, u32[]{:S(2)}) %collective-permute-start) | collective-permute-done | bytes 69664 | tf_op jit(solution)/shard_map/ppermute | solution.py:328
  15.1 0.3 shard_map.107
  15.4 2.6 %collective-permute-start.4 = (f32[160,128]{1,0:T(8,128)S(1)}, f32[160,128]{1,0:T(8,128)S(1)}, u32[]{:S(2)}, u32[]{:S(2)}) collective-permute-start(f32[160,128]{1,0:T(8,128)S(1)} %shard_map.105), channel_id=1, source_target_pairs={{0,4},{4,8},{8,12},{12,16},{16,20},{20,24},{24,28},{1,5},{5,9},{9,... | collective-permute-start | bytes 245768 | tf_op jit(solution)/shard_map/ppermute | solution.py:581
  18.0 2.6 %collective-permute-start.3 = (f32[136,128]{1,0:T(8,128)S(1)}, f32[136,128]{1,0:T(8,128)S(1)}, u32[]{:S(2)}, u32[]{:S(2)}) collective-permute-start(f32[136,128]{1,0:T(8,128)S(1)} %get-tuple-element.34.refs_0_), channel_id=1, source_target_pairs={{16,0},{20,4},{24,8},{28,12},{0,16},{4,20},{8,24},{12,28},{17,1},{... | collective-permute-start | bytes 208904 | tf_op jit(solution)/shard_map/ppermute | solution.py:328
  20.7 2.6 %collective-permute-done.3.refs_1_ = f32[136,128]{1,0:T(8,128)S(1)} collective-permute-done((f32[136,128]{1,0:T(8,128)S(1)}, f32[136,128]{1,0:T(8,128)S(1)}, u32[]{:S(2)}, u32[]{:S(2)}) %collective-permute-start.3) | collective-permute-done | bytes 69664 | tf_op jit(solution)/shard_map/ppermute | solution.py:328
  23.3 0.0 collective-permute-done.4.refs_10_
  23.3 1.8 %shard_map.108 = (f32[128,128]{1,0:T(8,128)S(1)}, f32[8,128]{1,0:T(8,128)S(1)}, f32[8,128]{1,0:T(8,128)S(1)}, f32[8,128]{1,0:T(8,128)S(1)}, f32[8,128]{1,0:T(8,128)S(1)}) custom-call(f32[136,128]{1,0:T(8,128)S(1)} %get-tuple-element.34.refs_0_, f32[136,128]{1,0:T(8,128)S(1)} %collective-permute-done.3.refs_1_, f32[136,128]{1,0:T(8,128)S(1)} %get-tuple-element.35.refs_2_, ...), custom_call_target="tpu_custom_call" | custom-call | flops 10485760 | bytes 2097152 | tf_op jit(solution)/shard_map/pallas_call | solution.py:584
  25.1 0.1 collective-permute-start.5
  25.2 1.6 %collective-permute-start.6 = (f32[8,128]{1,0:T(8,128)S(1)}, f32[8,128]{1,0:T(8,128)S(1)}, u32[]{:S(2)}, u32[]{:S(2)}) collective-permute-start(f32[8,128]{1,0:T(8,128)S(1)} %get-tuple-element.46), channel_id=1, source_target_pairs={{2,0},{3,1},{0,2},{1,3},{6,4},{7,5},{4,6},{5,7},{10,8},{11,9},{8,1... | collective-permute-start | bytes 12296 | tf_op jit(solution)/shard_map/ppermute | solution.py:328
  26.8 0.3 collective-permute-start.7
  27.0 2.3 %shard_map.109 = bf16[4,32,4096]{2,1,0:T(8,128)(2,1)} custom-call(f32[128,128]{1,0:T(8,128)S(1)} %get-tuple-element.43.incoming_ref, f32[4,32,4096]{2,1,0:T(8,128)S(1)} %get-tuple-element.29.own_ref, f32[4,32,128]{2,1,0:T(8,128)S(1)} %get-tuple-element.36.refs_3_.response_ref, s32[32,128]{1,0:T(8,128)S(1)} %get-tuple-element.37.refs_4_.slot_ref, ...), custom_call_target="tpu_custom_call" | custom-call | flops 15728640 | bytes 3145728 | tf_op jit(solution)/shard_map/pallas_call | solution.py:596
  29.3 0.0 collective-permute-done.5
  29.3 0.0 collective-permute-done.6
  29.3 0.5 %collective-permute-done.7 = f32[8,128]{1,0:T(8,128)S(1)} collective-permute-done((f32[8,128]{1,0:T(8,128)S(1)}, f32[8,128]{1,0:T(8,128)S(1)}, u32[]{:S(2)}, u32[]{:S(2)}) %collective-permute-start.7) | collective-permute-done | bytes 4128 | tf_op jit(solution)/shard_map/ppermute | solution.py:328
  29.8 0.6 %add_bitcast_fusion = f32[1024]{0:T(1024)} fusion(f32[8,128]{1,0:T(8,128)S(1)} %collective-permute-done.7, f32[8,128]{1,0:T(8,128)S(1)} %collective-permute-done.6, f32[8,128]{1,0:T(8,128)S(1)} %get-tuple-element.44, f32[8,128]{1,0:T(8,128)S(1)} %collective-permute-done.5), kind=kLoop, calls=%fused_computation | loop fusion | flops 3072 | bytes 20480 | tf_op jit(solution)/shard_map/reshape | solution.py:607
  (5 shorter events, 0.0 us)
Async XLA Ops:
  0.6 10.3 %copy-start.4 = (s32[4096]{0:T(1024)S(1)}, s32[4096]{0:T(1024)}, u32[]{:S(2)}) copy-start(s32[4096]{0:T(1024)} %param.16) | copy-start | bytes 49156
  0.6 10.3 %copy-start = (bf16[5,32,4096]{2,1,0:T(8,128)(2,1)S(1)}, bf16[5,32,4096]{2,1,0:T(8,128)(2,1)}, u32[]{:S(2)}) copy-start(bf16[5,32,4096]{2,1,0:T(8,128)(2,1)} %flow_ref.1) | copy-start | bytes 3932164
  0.7 11.2 %copy-start.1 = (bf16[4,32,4096]{2,1,0:T(8,128)(2,1)S(1)}, bf16[4,32,4096]{2,1,0:T(8,128)(2,1)}, u32[]{:S(2)}) copy-start(bf16[4,32,4096]{2,1,0:T(8,128)(2,1)} %lateral_ref) | copy-start | bytes 3145732
  0.7 11.2 %copy-start.2 = (f32[4096]{0:T(1024)S(1)}, f32[4096]{0:T(1024)}, u32[]{:S(2)}) copy-start(f32[4096]{0:T(1024)} %param.13) | copy-start | bytes 49156
  0.7 11.2 %copy-start.3 = (f32[4096]{0:T(1024)S(1)}, f32[4096]{0:T(1024)}, u32[]{:S(2)}) copy-start(f32[4096]{0:T(1024)} %param.12) | copy-start | bytes 49156
  0.7 11.2 %copy-start.5 = (s32[4096]{0:T(1024)S(1)}, s32[4096]{0:T(1024)}, u32[]{:S(2)}) copy-start(s32[4096]{0:T(1024)} %param.15) | copy-start | bytes 49156
  6.3 7.7 %collective-permute-start.2 = (f32[136,128]{1,0:T(8,128)S(1)}, f32[136,128]{1,0:T(8,128)S(1)}, u32[]{:S(2)}, u32[]{:S(2)}) collective-permute-start(f32[136,128]{1,0:T(8,128)S(1)} %get-tuple-element.31.refs_0_), channel_id=1, source_target_pairs={{12,0},{8,4},{4,8},{0,12},{28,16},{24,20},{20,24},{16,28},{13,1},{... | collective-permute-start | bytes 208904 | tf_op jit(solution)/shard_map/ppermute | solution.py:328
  10.3 4.3 %collective-permute-start.1 = (f32[136,128]{1,0:T(8,128)S(1)}, f32[136,128]{1,0:T(8,128)S(1)}, u32[]{:S(2)}, u32[]{:S(2)}) collective-permute-start(f32[136,128]{1,0:T(8,128)S(1)} %get-tuple-element.31.refs_0_), channel_id=1, source_target_pairs={{8,0},{12,4},{0,8},{4,12},{24,16},{28,20},{16,24},{20,28},{9,1},{1... | collective-permute-start | bytes 208904 | tf_op jit(solution)/shard_map/ppermute | solution.py:328
  10.8 4.3 %collective-permute-start = (f32[136,128]{1,0:T(8,128)S(1)}, f32[136,128]{1,0:T(8,128)S(1)}, u32[]{:S(2)}, u32[]{:S(2)}) collective-permute-start(f32[136,128]{1,0:T(8,128)S(1)} %get-tuple-element.31.refs_0_), channel_id=1, source_target_pairs={{4,0},{0,4},{12,8},{8,12},{20,16},{16,20},{28,24},{24,28},{5,1},{1... | collective-permute-start | bytes 208904 | tf_op jit(solution)/shard_map/ppermute | solution.py:328
  11.8 11.5 %copy-start.6 = (s32[1,128]{1,0:T(1,128)S(1)}, s32[1,128]{1,0:T(1,128)}, u32[]{:S(2)}) copy-start(s32[1,128]{1,0:T(1,128)} %refs_11_.1) | copy-start | bytes 1540
  15.4 7.9 %collective-permute-start.4 = (f32[160,128]{1,0:T(8,128)S(1)}, f32[160,128]{1,0:T(8,128)S(1)}, u32[]{:S(2)}, u32[]{:S(2)}) collective-permute-start(f32[160,128]{1,0:T(8,128)S(1)} %shard_map.105), channel_id=1, source_target_pairs={{0,4},{4,8},{8,12},{12,16},{16,20},{20,24},{24,28},{1,5},{5,9},{9,... | collective-permute-start | bytes 245768 | tf_op jit(solution)/shard_map/ppermute | solution.py:581
  18.0 5.3 %collective-permute-start.3 = (f32[136,128]{1,0:T(8,128)S(1)}, f32[136,128]{1,0:T(8,128)S(1)}, u32[]{:S(2)}, u32[]{:S(2)}) collective-permute-start(f32[136,128]{1,0:T(8,128)S(1)} %get-tuple-element.34.refs_0_), channel_id=1, source_target_pairs={{16,0},{20,4},{24,8},{28,12},{0,16},{4,20},{8,24},{12,28},{17,1},{... | collective-permute-start | bytes 208904 | tf_op jit(solution)/shard_map/ppermute | solution.py:328
  25.1 4.2 %collective-permute-start.5 = (f32[8,128]{1,0:T(8,128)S(1)}, f32[8,128]{1,0:T(8,128)S(1)}, u32[]{:S(2)}, u32[]{:S(2)}) collective-permute-start(f32[8,128]{1,0:T(8,128)S(1)} %get-tuple-element.45), channel_id=1, source_target_pairs={{1,0},{0,1},{3,2},{2,3},{5,4},{4,5},{7,6},{6,7},{9,8},{8,9},{11,10... | collective-permute-start | bytes 12296 | tf_op jit(solution)/shard_map/ppermute | solution.py:328
  25.2 4.1 %collective-permute-start.6 = (f32[8,128]{1,0:T(8,128)S(1)}, f32[8,128]{1,0:T(8,128)S(1)}, u32[]{:S(2)}, u32[]{:S(2)}) collective-permute-start(f32[8,128]{1,0:T(8,128)S(1)} %get-tuple-element.46), channel_id=1, source_target_pairs={{2,0},{3,1},{0,2},{1,3},{6,4},{7,5},{4,6},{5,7},{10,8},{11,9},{8,1... | collective-permute-start | bytes 12296 | tf_op jit(solution)/shard_map/ppermute | solution.py:328
  26.8 3.0 %collective-permute-start.7 = (f32[8,128]{1,0:T(8,128)S(1)}, f32[8,128]{1,0:T(8,128)S(1)}, u32[]{:S(2)}, u32[]{:S(2)}) collective-permute-start(f32[8,128]{1,0:T(8,128)S(1)} %get-tuple-element.47), channel_id=1, source_target_pairs={{3,0},{2,1},{1,2},{0,3},{7,4},{6,5},{5,6},{4,7},{11,8},{10,9},{9,1... | collective-permute-start | bytes 12296 | tf_op jit(solution)/shard_map/ppermute | solution.py:328

commit v4 on v3

--- a/solution.py
+++ b/solution.py
@@ -72,39 +72,12 @@
 
 def local_kernel(
     steps, members, blocks,
-    cot_hbm, matrix_hbm, rough_hbm, factor_hbm, down_hbm, exit_hbm, inlet_hbm,
-    own_ref, message_ref, response_ref, slot_ref, inlet_values_ref, inlet_rows_ref,
-    stay_ref, ratio_ref,
-    cot_ref, matrix_ref, rough_ref, factor_ref, down_ref, exit_ref, inlet_ref,
-    small_sem, cot_sem, matrix_sem,
+    cot_ref, matrix_ref, rough_ref, factor_ref, down_ref, exit_ref, inlet_ref, lateral_hbm,
+    own_ref, message_ref, response_ref, slot_ref, inlet_values_ref, inlet_rows_ref, lateral_ref,
+    stay_ref, ratio_ref, lateral_sem,
 ):
-    groups = list(range(0, blocks, GROUP))
-    small = [
-        pltpu.make_async_copy(source, target, small_sem.at[i])
-        for i, (source, target) in enumerate((
-            (rough_hbm, rough_ref), (factor_hbm, factor_ref), (down_hbm, down_ref),
-            (exit_hbm, exit_ref), (inlet_hbm, inlet_ref),
-        ))
-    ]
-    large = []
-    for i, first in enumerate(groups):
-        size = min(GROUP, blocks - first)
-        lanes = pl.ds(first * LANES, size * LANES)
-        large.append((
-            pltpu.make_async_copy(
-                matrix_hbm.at[pl.ds(first, size)], matrix_ref.at[pl.ds(first, size)], matrix_sem.at[i]
-            ),
-            pltpu.make_async_copy(
-                cot_hbm.at[:, :, lanes], cot_ref.at[:, :, lanes], cot_sem.at[i]
-            ),
-        ))
-    for copy in small:
-        copy.start()
-    for pair in large:
-        for copy in pair:
-            copy.start()
-    for copy in small:
-        copy.wait()
+    lateral_copy = pltpu.make_async_copy(lateral_hbm, lateral_ref, lateral_sem)
+    lateral_copy.start()
 
     travel = rough_ref[...] * factor_ref[...]
     weight_new, weight_old, weight_stay = weights_of(travel)
@@ -192,9 +165,7 @@
     response_in = [at_inlets(value) for value in response]
     new_in, old_in, _ = weights_of(travel_in)
 
-    for first, pair in zip(groups, large):
-        for copy in pair:
-            copy.wait()
+    for first in range(0, blocks, GROUP):
         at_inlet = solve_group(first, list(at_inlet))
 
     for step in range(steps):
@@ -212,6 +183,7 @@
         tail.append(coefficient)
     message_ref[pl.ds(steps * members, EXTRA), :] = eight_rows(tail + [slot_in])
     inlet_rows_ref[...] = eight_rows(response_in + [travel_in, slot_in])
+    lateral_copy.wait()
 
 
 def eight_rows(rows):
@@ -337,10 +309,31 @@
     return radices or [1]
 
 
-def leaving_kernel(steps, members, blocks, flow_ref, exit_ref, leaving_ref):
+def fetch_kernel(steps, members, blocks, count, *refs):
+    sources, targets = refs[:count], refs[count:2 * count]
+    leaving_ref, flow_sem, sem = refs[2 * count:]
+    flow_hbm, flow_ref = sources[0], targets[0]
+    exit_ref = targets[1]
+    flow_copies = []
+    for turn, first in enumerate(range(0, blocks, GROUP)):
+        lanes = pl.ds(first * LANES, min(GROUP, blocks - first) * LANES)
+        flow_copies.append(pltpu.make_async_copy(
+            flow_hbm.at[:, :, lanes], flow_ref.at[:, :, lanes], flow_sem.at[turn]
+        ))
+    copies = [
+        pltpu.make_async_copy(sources[i], targets[i], sem.at[i]) for i in range(1, count)
+    ]
+    copies[0].start()
+    for copy in flow_copies:
+        copy.start()
+    for copy in copies[1:]:
+        copy.start()
+    copies[0].wait()
     sub = lax.broadcasted_iota(jnp.int32, (LANES, LANES), 0)
     total = None
     for block in range(blocks):
+        if block % GROUP == 0:
+            flow_copies[block // GROUP].wait()
         lanes = pl.ds(block * LANES, LANES)
         table = (sub == exit_ref[pl.ds(block, 1), :]).astype(F32).astype(jnp.bfloat16)
         flows = flow_ref[:, :, lanes].reshape((steps + 1) * members, LANES)
@@ -349,11 +342,13 @@
         )
         total = part if total is None else total + part
     leaving_ref[...] = total
+    for copy in copies[1:]:
+        copy.wait()
 
 
 def weight_kernel(
     steps, members, blocks,
-    flow_ref, lateral_ref, own_ref, rough_ref, factor_ref, down_ref,
+    flow_ref, lateral_ref, own_ref, response_ref, rough_ref, factor_ref, down_ref,
     weight_ref, part_ref, slopes_ref,
 ):
     slopes = slopes_of(rough_ref[...] * factor_ref[...])
@@ -371,6 +366,7 @@
         )
         new, old, stay, side = (slopes_ref[i, row, :] for i in range(4))
         total = jnp.zeros((members, LANES), F32)
+        weights = []
         for step in range(steps):
             now = inflow[(step + 1) * members:(step + 2) * members]
             prior = inflow[step * members:(step + 1) * members]
@@ -380,24 +376,28 @@
                 + stay * flow_ref[step, :, lanes].astype(F32)
                 + side * lateral_ref[step, :, lanes].astype(F32)
             )
-            weight_ref[step, :, lanes] = weight
+            weights.append(weight)
             total = total + weight * own_ref[step, :, lanes]
+            folded = response_ref[0, row, :] * weight
+            for lag in range(1, step + 1):
+                folded = folded + response_ref[lag, row, :] * weights[step - lag]
+            weight_ref[step, :, lanes] = folded
         part_ref[row, :] = jnp.sum(total, axis=0, keepdims=True)
         return carry
 
-    lax.fori_loop(0, blocks, one_block, 0, unroll=4)
+    lax.fori_loop(0, blocks, one_block, 0, unroll=8)
 
 
 def sums_kernel(steps, members, blocks, ranks, stride, radix, has_inner, *refs):
     messages, refs = refs[:radix], refs[radix:]
     inner, refs = (refs[0], refs[1:]) if has_inner else (None, refs)
     (
-        response_ref, slot_ref, weight_ref, own_part_ref, factor_ref,
+        slot_ref, weight_ref, own_part_ref, factor_ref,
         inlet_values_ref, inlet_rows_ref, arriving_ref, inlet_ref,
-    ) = refs[:9]
-    incoming_ref = refs[9]
-    pieces = refs[10:10 + ranks]
-    (part_ref,) = refs[10 + ranks:]
+    ) = refs[:8]
+    incoming_ref = refs[8]
+    pieces = refs[9:9 + ranks]
+    (part_ref,) = refs[9 + ranks:]
     last_round(steps, members, "net", stride, radix, messages, inner, incoming_ref)
     shape = (members, LANES)
 
@@ -408,18 +408,13 @@
         pulled = [
             take(incoming_ref[pl.ds(step * members, members), :], index) for step in range(steps)
         ]
-        weight = [weight_ref[step, :, lanes] for step in range(steps)]
-        total = None
-        for lag in range(steps):
-            inside = pulled[lag] * weight[0]
-            for step in range(1, steps - lag):
-                inside = inside + pulled[step + lag] * weight[step]
-            inside = response_ref[lag, row, :] * inside
-            total = inside if total is None else total + inside
+        total = pulled[0] * weight_ref[0, :, lanes]
+        for step in range(1, steps):
+            total = total + pulled[step] * weight_ref[step, :, lanes]
         part_ref[row, :] = own_part_ref[row, :] + jnp.sum(total, axis=0, keepdims=True)
         return carry
 
-    lax.fori_loop(0, blocks, one_block, 0, unroll=4)
+    lax.fori_loop(0, blocks, one_block, 0, unroll=16)
 
     rows = inlet_rows_ref[...]
     slope_new, slope_old, _, _ = slopes_of(rows[steps:steps + 1])
@@ -459,11 +454,13 @@
 
 
 def grad_kernel(
-    steps, members, blocks,
-    incoming_ref, own_ref, response_ref, slot_ref, rough_ref, factor_ref, grad_ref, side_ref,
+    steps, members, blocks, chunks,
+    incoming_ref, own_ref, response_ref, slot_ref, rough_ref, factor_ref,
+    grad_hbm, grad_ref, side_ref, sem,
 ):
     side_ref[...] = 1.0 / (rough_ref[...] * factor_ref[...] * (1.0 - skew_weight) + 0.5)
     shape = (members, LANES)
+    part = blocks // chunks
 
     def one_block(block, carry):
         lanes = pl.ds(pl.multiple_of(block * LANES, LANES), LANES)
@@ -479,7 +476,16 @@
             grad_ref[step, :, lanes] = (side_ref[row, :] * value).astype(jnp.bfloat16)
         return carry
 
-    lax.fori_loop(0, blocks, one_block, 0, unroll=4)
+    copies = []
+    for chunk in range(chunks):
+        lax.fori_loop(chunk * part, (chunk + 1) * part, one_block, 0, unroll=8)
+        lanes = pl.ds(chunk * part * LANES, part * LANES)
+        copies.append(pltpu.make_async_copy(
+            grad_ref.at[:, :, lanes], grad_hbm.at[:, :, lanes], sem.at[chunk]
+        ))
+        copies[-1].start()
+    for copy in copies:
+        copy.wait()
 
 
 def call(kernel, out_shape, scratch=(), flops=0, size=0, **specs):
@@ -509,14 +515,29 @@
     shape = jax.ShapeDtypeStruct
     work = steps * members * reaches
 
-    inputs = [
-        pltpu.with_memory_space_constraint(array, pltpu.HBM)
-        for array in (
-            cotangent, inverse_block_matrix, rough, factor, down, leave, inlet_reach
-        )
-    ]
-    turns = -(-blocks // GROUP)
-    own, message, response, slot, inlet_values, inlet_rows = call(
+    hbm = pl.BlockSpec(memory_space=pltpu.HBM)
+
+    def stay_out(array):
+        return pltpu.with_memory_space_constraint(array, pltpu.HBM)
+
+    inputs = (
+        stored_reach_flows, leave, rough, factor, down, inlet_reach, inverse_block_matrix, cotangent
+    )
+    flows, leave, rough, factor, down, inlets, matrix, cotangent, leaving = call(
+        functools.partial(fetch_kernel, steps, members, blocks, len(inputs)),
+        tuple(shape(array.shape, array.dtype) for array in inputs)
+        + (shape(((steps + 1) * members, LANES), F32),),
+        scratch=[
+            pltpu.SemaphoreType.DMA((-(-blocks // GROUP),)),
+            pltpu.SemaphoreType.DMA((len(inputs),)),
+        ],
+        flops=2 * LANES * work,
+        size=9 * work,
+        in_specs=[hbm] * len(inputs),
+    )(*(stay_out(array) for array in inputs))
+    arriving = lax.ppermute(leaving, "net", [(i, i + 1) for i in range(count - 1)])
+
+    own, message, response, slot, inlet_values, inlet_rows, lateral = call(
         functools.partial(local_kernel, steps, members, blocks),
         (
             shape((steps, members, reaches), F32),
@@ -525,35 +546,21 @@
             shape((blocks, LANES), jnp.int32),
             shape((steps * members, LANES), F32),
             shape((EXTRA, LANES), F32),
+            shape(lateral.shape, lateral.dtype),
         ),
-        scratch=[pltpu.VMEM((blocks, LANES), F32)] * 2 + [
-            pltpu.VMEM(array.shape, array.dtype) for array in inputs
-        ] + [
-            pltpu.SemaphoreType.DMA((5,)),
-            pltpu.SemaphoreType.DMA((turns,)),
-            pltpu.SemaphoreType.DMA((turns,)),
-        ],
+        scratch=[pltpu.VMEM((blocks, LANES), F32)] * 2 + [pltpu.SemaphoreType.DMA],
         flops=8 * LANES * work,
         size=6 * work,
-        in_specs=[pl.BlockSpec(memory_space=pltpu.HBM)] * len(inputs),
-    )(*inputs)
-    stored_reach_flows, lateral, message = lax.optimization_barrier(
-        (stored_reach_flows, lateral, message)
-    )
-
-    leaving = call(
-        functools.partial(leaving_kernel, steps, members, blocks),
-        shape(((steps + 1) * members, LANES), F32),
-        flops=2 * LANES * work,
-        size=2 * work,
-    )(stored_reach_flows, leave)
+        in_specs=[pl.BlockSpec()] * 7 + [hbm],
+    )(cotangent, matrix, rough, factor, down, leave, inlets, stay_out(lateral))
+
     weight, own_part = call(
         functools.partial(weight_kernel, steps, members, blocks),
         (shape((steps, members, reaches), F32), shape((blocks, LANES), F32)),
         scratch=[pltpu.VMEM((4, blocks, LANES), F32)],
         flops=2 * LANES * work,
         size=8 * work,
-    )(stored_reach_flows, lateral, own, rough, factor, down)
+    )(flows, lateral, own, response, rough, factor, down)
 
     stride = 1
     inner = ()
@@ -563,7 +570,7 @@
             exchange(message, "net", stride, radix, offset) for offset in range(1, radix)
         ]
         if turn == 0:
-            message, leaving, weight = lax.optimization_barrier((message, leaving, weight))
+            message, weight = lax.optimization_barrier((message, weight))
         received = [message] + received
         later, message = call(
             functools.partial(group_kernel, steps, members, "net", stride, radix, len(inner)),
@@ -574,11 +581,9 @@
         inner = (later,)
         stride *= radix
     radix = radices[-1]
-    message, leaving = lax.optimization_barrier((message, leaving))
     received = [message] + [
         exchange(message, "net", stride, radix, offset) for offset in range(1, radix)
     ]
-    arriving = lax.ppermute(leaving, "net", [(i, i + 1) for i in range(count - 1)])
 
     piece = shape((blocks // ranks, LANES), F32)
     incoming, *pieces = call(
@@ -590,15 +595,21 @@
         flops=20 * work,
         size=4 * work,
     )(
-        *received, *inner, response, slot, weight, own_part, factor,
-        inlet_values, inlet_rows, arriving, inlet_reach,
-    )
+        *received, *inner, slot, weight, own_part, factor,
+        inlet_values, inlet_rows, arriving, inlets,
+    )
+    chunks = next(n for n in (4, 2, 1) if blocks % n == 0)
     grad_lateral = call(
-        functools.partial(grad_kernel, steps, members, blocks),
+        functools.partial(grad_kernel, steps, members, blocks, chunks),
         shape((steps, members, reaches), jnp.bfloat16),
-        scratch=[pltpu.VMEM((blocks, LANES), F32)],
+        scratch=[
+            pltpu.VMEM((steps, members, reaches), jnp.bfloat16),
+            pltpu.VMEM((blocks, LANES), F32),
+            pltpu.SemaphoreType.DMA((chunks,)),
+        ],
         flops=30 * work,
         size=6 * work,
+        out_specs=pl.BlockSpec(memory_space=pl.ANY),
     )(incoming, own, response, slot, rough, factor)
     total = pieces[0]
     for offset in range(1, ranks):

time: 30.6 us -> 28.3 us (0.925)
  Pallas kernels: 12.8 us -> 9.83 us
  starting transfers between devices: 11.9 us -> 13 us
  waiting for transfers between devices: 4.28 us -> 3.87 us
    pallas_call x1, Pallas kernels: 5.58 us -> 2.32 us  [gradients(): call(functools.partial(local_kernel, steps, members, blocks), (shape((ste...]
    ppermute x1, starting transfers between devices: 2.64 us -> 3.73 us  [gradients(): lax.ppermute(leaving, 'net', [(i, i + 1) for i in range(count - 1)])]
    pallas_call x2, Pallas kernels: 3.11 us -> 4.06 us  [the longest x1 2.55 us: gradients(): call(functools.partial(fetch_kernel, steps, members, blocks, len(inputs))...]
    pallas_call x1, Pallas kernels: 1.81 us -> 1.2 us  [gradients(): call(functools.partial(sums_kernel, steps, members, blocks, ranks, stride...]
    ppermute x7, waiting for transfers between devices: 4.27 us -> 3.87 us  [exchange(): return lax.ppermute(value, axis, pairs)]
  transfers between devices with their start and end apart: 8 -> 8, of which waited for: 4 -> 3; matrix products, arithmetic and copies ran while one was open for 0% -> 0% of each run, Pallas kernels for 17% -> 13%
where the time goes in v4:
time: 28.3 us; the launch traced here: 28 us
  starting transfers between devices  13 us (46%)
  Pallas kernels  9.83 us (35%)
  waiting for transfers between devices  3.87 us (14%)
  between operations  0.73 us (3%)
  other arithmetic  0.6 us (2%)
    ppermute x7, starting transfers between devices, exchange(): return lax.ppermute(value, axis, pairs)  9.26 us
    ppermute x7, waiting for transfers between devices, exchange(): return lax.ppermute(value, axis, pairs)  3.87 us
    ppermute x1, starting transfers between devices, gradients(): lax.ppermute(leaving, 'net', [(i, i + 1) for i in range(count - 1)])  3.73 us
    pallas_call x1, Pallas kernels, gradients(): call(functools.partial(fetch_kernel, steps, members, blocks, len(inputs))...  2.55 us
    pallas_call x1, Pallas kernels, gradients(): call(functools.partial(local_kernel, steps, members, blocks), (shape((ste...  2.32 us
    pallas_call x1, Pallas kernels, gradients(): call(functools.partial(weight_kernel, steps, members, blocks), (shape((st...  1.96 us
    pallas_call x1, Pallas kernels, gradients(): call(functools.partial(grad_kernel, steps, members, blocks, chunks), shap...  1.5 us
    pallas_call x1, Pallas kernels, gradients(): call(functools.partial(sums_kernel, steps, members, blocks, ranks, stride...  1.2 us
  transfers between devices with their start and end apart: 8, of which 3 were waited for; matrix products, arithmetic and copies ran while one was open for 0% of the time, Pallas kernels for 13%

profile of v4, /device:TPU:0, one launch (start us, length us, event | category | flops | bytes accessed | tf_op | source)
XLA Modules:
  0.0 28.0 jit_solution(819944969981448770)
XLA Ops:
  0.6 2.6 %shard_map.104 = (bf16[5,32,4096]{2,1,0:T(8,128)(2,1)S(1)}, s32[32,128]{1,0:T(8,128)S(1)}, f32[32,128]{1,0:T(8,128)S(1)}, f32[32,128]{1,0:T(8,128)S(1)}, s32[32,...) custom-call(bf16[5,32,4096]{2,1,0:T(8,128)(2,1)} %refs_0_.1, ...), custom_call_target="tpu_custom_call" | custom-call | flops 134217728 | bytes 4718592 | tf_op jit(solution)/shard_map/pallas_call | solution.py:526
  3.2 2.3 %shard_map.105 = (f32[4,32,4096]{2,1,0:T(8,128)S(1)}, f32[136,128]{1,0:T(8,128)S(1)}, f32[4,32,128]{2,1,0:T(8,128)S(1)}, s32[32,128]{1,0:T(8,128)S(1)}, f32[128,...) custom-call(bf16[4,32,4096]{2,1,0:T(8,128)(2,1)S(1)} %get-tuple-element.29.cot_ref, ...), custom_call_target="tpu_custom_call" | custom-call | flops 536870912 | bytes 3145728 | tf_op jit(solution)/shard_map/pallas_call | solution.py:540
  5.5 4.0 %collective-permute-start.2 = (f32[136,128]{1,0:T(8,128)S(1)}, f32[136,128]{1,0:T(8,128)S(1)}, u32[]{:S(2)}, u32[]{:S(2)}) collective-permute-start(f32[136,128]{1,0:T(8,128)S(1)} %get-tuple-element.42.refs_0_), channel_id=1, source_target_pairs={{12,0},{8,4},{4,8},{0,12},{28,16},{24,20},{20,24},{16,28},{13,1},{... | collective-permute-start | bytes 208904 | tf_op jit(solution)/shard_map/ppermute | solution.py:300
  9.6 0.4 %collective-permute-start.1 = (f32[136,128]{1,0:T(8,128)S(1)}, f32[136,128]{1,0:T(8,128)S(1)}, u32[]{:S(2)}, u32[]{:S(2)}) collective-permute-start(f32[136,128]{1,0:T(8,128)S(1)} %get-tuple-element.42.refs_0_), channel_id=1, source_target_pairs={{8,0},{12,4},{0,8},{4,12},{24,16},{28,20},{16,24},{20,28},{9,1},{1... | collective-permute-start | bytes 208904 | tf_op jit(solution)/shard_map/ppermute | solution.py:300
  10.0 0.2 collective-permute-start
  10.2 3.7 %collective-permute-start.4 = (f32[160,128]{1,0:T(8,128)S(1)}, f32[160,128]{1,0:T(8,128)S(1)}, u32[]{:S(2)}, u32[]{:S(2)}) collective-permute-start(f32[160,128]{1,0:T(8,128)S(1)} %get-tuple-element.50), channel_id=1, source_target_pairs={{0,4},{4,8},{8,12},{12,16},{16,20},{20,24},{24,28},{1,5},{5,9},{9,... | collective-permute-start | bytes 245768 | tf_op jit(solution)/shard_map/ppermute | solution.py:538
  13.9 2.0 %shard_map.106 = (f32[4,32,4096]{2,1,0:T(8,128)S(1)}, f32[32,128]{1,0:T(8,128)S(1)}) custom-call(bf16[5,32,4096]{2,1,0:T(8,128)(2,1)S(1)} %get-tuple-element.37.flow_ref, bf16[4,32,4096]{2,1,0:T(8,128)(2,1)S(1)} %get-tuple-element.38.lateral_ref, f32[4,32,4096]{2,1,0:T(8,128)S(1)} %get-tuple-element.39.own_ref, ...), custom_call_target="tpu_custom_call" | custom-call | flops 134217728 | bytes 4194304 | tf_op jit(solution)/shard_map/pallas_call | solution.py:557
  15.9 0.0 collective-permute-done.2.refs_3_
  15.9 0.0 collective-permute-done.1.refs_2_
  15.9 0.0 collective-permute-done.refs_1_
  15.9 0.3 %shard_map.107 = (f32[136,128]{1,0:T(8,128)S(1)}, f32[136,128]{1,0:T(8,128)S(1)}) custom-call(f32[136,128]{1,0:T(8,128)S(1)} %get-tuple-element.42.refs_0_, f32[136,128]{1,0:T(8,128)S(1)} %collective-permute-done.refs_1_, f32[136,128]{1,0:T(8,128)S(1)} %collective-permute-done.1.refs_2_, f32[136,128]{1,0:T(8,128)S(1)} %collective-permute-done.2.refs_3_), custom_call_target="tpu_custom_call" | custom-call | flops 1392640 | bytes 278528 | tf_op jit(solution)/shard_map/pallas_call | solution.py:575
  16.2 2.7 %collective-permute-start.3 = (f32[136,128]{1,0:T(8,128)S(1)}, f32[136,128]{1,0:T(8,128)S(1)}, u32[]{:S(2)}, u32[]{:S(2)}) collective-permute-start(f32[136,128]{1,0:T(8,128)S(1)} %get-tuple-element.43.refs_0_), channel_id=1, source_target_pairs={{16,0},{20,4},{24,8},{28,12},{0,16},{4,20},{8,24},{12,28},{17,1},{... | collective-permute-start | bytes 208904 | tf_op jit(solution)/shard_map/ppermute | solution.py:300
  18.9 0.0 collective-permute-done.4.refs_9_
  18.9 2.6 %collective-permute-done.3.refs_1_ = f32[136,128]{1,0:T(8,128)S(1)} collective-permute-done((f32[136,128]{1,0:T(8,128)S(1)}, f32[136,128]{1,0:T(8,128)S(1)}, u32[]{:S(2)}, u32[]{:S(2)}) %collective-permute-start.3) | collective-permute-done | bytes 69664 | tf_op jit(solution)/shard_map/ppermute | solution.py:300
  21.5 1.2 %shard_map.108 = (f32[128,128]{1,0:T(8,128)S(1)}, f32[8,128]{1,0:T(8,128)S(1)}, f32[8,128]{1,0:T(8,128)S(1)}, f32[8,128]{1,0:T(8,128)S(1)}, f32[8,128]{1,0:T(8,128)S(1)}) custom-call(f32[136,128]{1,0:T(8,128)S(1)} %get-tuple-element.43.refs_0_, f32[136,128]{1,0:T(8,128)S(1)} %collective-permute-done.3.refs_1_, f32[136,128]{1,0:T(8,128)S(1)} %get-tuple-element.44.refs_2_, ...), custom_call_target="tpu_custom_call" | custom-call | flops 10485760 | bytes 2097152 | tf_op jit(solution)/shard_map/pallas_call | solution.py:589
  22.7 0.1 collective-permute-start.5
  22.8 1.6 %collective-permute-start.6 = (f32[8,128]{1,0:T(8,128)S(1)}, f32[8,128]{1,0:T(8,128)S(1)}, u32[]{:S(2)}, u32[]{:S(2)}) collective-permute-start(f32[8,128]{1,0:T(8,128)S(1)} %get-tuple-element.54), channel_id=1, source_target_pairs={{2,0},{3,1},{0,2},{1,3},{6,4},{7,5},{4,6},{5,7},{10,8},{11,9},{8,1... | collective-permute-start | bytes 12296 | tf_op jit(solution)/shard_map/ppermute | solution.py:300
  24.4 0.3 collective-permute-start.7
  24.7 1.5 %shard_map.109 = bf16[4,32,4096]{2,1,0:T(8,128)(2,1)} custom-call(f32[128,128]{1,0:T(8,128)S(1)} %get-tuple-element.51.incoming_ref, f32[4,32,4096]{2,1,0:T(8,128)S(1)} %get-tuple-element.39.own_ref, f32[4,32,128]{2,1,0:T(8,128)S(1)} %get-tuple-element.40.response_ref, s32[32,128]{1,0:T(8,128)S(1)} %get-tuple-element.45.refs_3_.slot_ref, ...), custom_call_target="tpu_custom_call" | custom-call | flops 15728640 | bytes 3145728 | tf_op jit(solution)/shard_map/pallas_call | solution.py:602
  26.2 0.0 collective-permute-done.5
  26.2 0.3 %collective-permute-done.6 = f32[8,128]{1,0:T(8,128)S(1)} collective-permute-done((f32[8,128]{1,0:T(8,128)S(1)}, f32[8,128]{1,0:T(8,128)S(1)}, u32[]{:S(2)}, u32[]{:S(2)}) %collective-permute-start.6) | collective-permute-done | bytes 4128 | tf_op jit(solution)/shard_map/ppermute | solution.py:300
  26.5 0.9 %collective-permute-done.7 = f32[8,128]{1,0:T(8,128)S(1)} collective-permute-done((f32[8,128]{1,0:T(8,128)S(1)}, f32[8,128]{1,0:T(8,128)S(1)}, u32[]{:S(2)}, u32[]{:S(2)}) %collective-permute-start.7) | collective-permute-done | bytes 4128 | tf_op jit(solution)/shard_map/ppermute | solution.py:300
  27.4 0.6 %add_bitcast_fusion = f32[1024]{0:T(1024)} fusion(f32[8,128]{1,0:T(8,128)S(1)} %collective-permute-done.7, f32[8,128]{1,0:T(8,128)S(1)} %collective-permute-done.6, f32[8,128]{1,0:T(8,128)S(1)} %get-tuple-element.52, f32[8,128]{1,0:T(8,128)S(1)} %collective-permute-done.5), kind=kLoop, calls=%fused_computation | loop fusion | flops 3072 | bytes 20480 | tf_op jit(solution)/shard_map/reshape | solution.py:618
Async XLA Ops:
  5.5 10.4 %collective-permute-start.2 = (f32[136,128]{1,0:T(8,128)S(1)}, f32[136,128]{1,0:T(8,128)S(1)}, u32[]{:S(2)}, u32[]{:S(2)}) collective-permute-start(f32[136,128]{1,0:T(8,128)S(1)} %get-tuple-element.42.refs_0_), channel_id=1, source_target_pairs={{12,0},{8,4},{4,8},{0,12},{28,16},{24,20},{20,24},{16,28},{13,1},{... | collective-permute-start | bytes 208904 | tf_op jit(solution)/shard_map/ppermute | solution.py:300
  9.6 6.4 %collective-permute-start.1 = (f32[136,128]{1,0:T(8,128)S(1)}, f32[136,128]{1,0:T(8,128)S(1)}, u32[]{:S(2)}, u32[]{:S(2)}) collective-permute-start(f32[136,128]{1,0:T(8,128)S(1)} %get-tuple-element.42.refs_0_), channel_id=1, source_target_pairs={{8,0},{12,4},{0,8},{4,12},{24,16},{28,20},{16,24},{20,28},{9,1},{1... | collective-permute-start | bytes 208904 | tf_op jit(solution)/shard_map/ppermute | solution.py:300
  10.0 5.9 %collective-permute-start = (f32[136,128]{1,0:T(8,128)S(1)}, f32[136,128]{1,0:T(8,128)S(1)}, u32[]{:S(2)}, u32[]{:S(2)}) collective-permute-start(f32[136,128]{1,0:T(8,128)S(1)} %get-tuple-element.42.refs_0_), channel_id=1, source_target_pairs={{4,0},{0,4},{12,8},{8,12},{20,16},{16,20},{28,24},{24,28},{5,1},{1... | collective-permute-start | bytes 208904 | tf_op jit(solution)/shard_map/ppermute | solution.py:300
  10.2 8.7 %collective-permute-start.4 = (f32[160,128]{1,0:T(8,128)S(1)}, f32[160,128]{1,0:T(8,128)S(1)}, u32[]{:S(2)}, u32[]{:S(2)}) collective-permute-start(f32[160,128]{1,0:T(8,128)S(1)} %get-tuple-element.50), channel_id=1, source_target_pairs={{0,4},{4,8},{8,12},{12,16},{16,20},{20,24},{24,28},{1,5},{5,9},{9,... | collective-permute-start | bytes 245768 | tf_op jit(solution)/shard_map/ppermute | solution.py:538
  16.2 5.3 %collective-permute-start.3 = (f32[136,128]{1,0:T(8,128)S(1)}, f32[136,128]{1,0:T(8,128)S(1)}, u32[]{:S(2)}, u32[]{:S(2)}) collective-permute-start(f32[136,128]{1,0:T(8,128)S(1)} %get-tuple-element.43.refs_0_), channel_id=1, source_target_pairs={{16,0},{20,4},{24,8},{28,12},{0,16},{4,20},{8,24},{12,28},{17,1},{... | collective-permute-start | bytes 208904 | tf_op jit(solution)/shard_map/ppermute | solution.py:300
  22.7 3.4 %collective-permute-start.5 = (f32[8,128]{1,0:T(8,128)S(1)}, f32[8,128]{1,0:T(8,128)S(1)}, u32[]{:S(2)}, u32[]{:S(2)}) collective-permute-start(f32[8,128]{1,0:T(8,128)S(1)} %get-tuple-element.53), channel_id=1, source_target_pairs={{1,0},{0,1},{3,2},{2,3},{5,4},{4,5},{7,6},{6,7},{9,8},{8,9},{11,10... | collective-permute-start | bytes 12296 | tf_op jit(solution)/shard_map/ppermute | solution.py:300
  22.8 3.7 %collective-permute-start.6 = (f32[8,128]{1,0:T(8,128)S(1)}, f32[8,128]{1,0:T(8,128)S(1)}, u32[]{:S(2)}, u32[]{:S(2)}) collective-permute-start(f32[8,128]{1,0:T(8,128)S(1)} %get-tuple-element.54), channel_id=1, source_target_pairs={{2,0},{3,1},{0,2},{1,3},{6,4},{7,5},{4,6},{5,7},{10,8},{11,9},{8,1... | collective-permute-start | bytes 12296 | tf_op jit(solution)/shard_map/ppermute | solution.py:300
  24.4 3.0 %collective-permute-start.7 = (f32[8,128]{1,0:T(8,128)S(1)}, f32[8,128]{1,0:T(8,128)S(1)}, u32[]{:S(2)}, u32[]{:S(2)}) collective-permute-start(f32[8,128]{1,0:T(8,128)S(1)} %get-tuple-element.55), channel_id=1, source_target_pairs={{3,0},{2,1},{1,2},{0,3},{7,4},{6,5},{5,6},{4,7},{11,8},{10,9},{9,1... | collective-permute-start | bytes 12296 | tf_op jit(solution)/shard_map/ppermute | solution.py:300

commit v5 on v4

--- a/solution.py
+++ b/solution.py
@@ -72,12 +72,41 @@
 
 def local_kernel(
     steps, members, blocks,
-    cot_ref, matrix_ref, rough_ref, factor_ref, down_ref, exit_ref, inlet_ref, lateral_hbm,
-    own_ref, message_ref, response_ref, slot_ref, inlet_values_ref, inlet_rows_ref, lateral_ref,
-    stay_ref, ratio_ref, lateral_sem,
+    flow_hbm, lateral_hbm, cot_hbm, matrix_hbm,
+    rough_hbm, factor_hbm, down_hbm, exit_hbm, inlet_hbm,
+    own_ref, message_ref, leaving_ref, response_ref, slot_ref, inlet_values_ref, inlet_rows_ref,
+    flow_ref, lateral_ref, rough_ref, factor_ref, down_ref, inlet_ref,
+    exit_ref, cot_ref, matrix_ref, stay_ref, ratio_ref,
+    small_sem, cot_sem, matrix_sem, flow_sem, lateral_sem,
 ):
+    small = [
+        pltpu.make_async_copy(source, target, small_sem.at[i])
+        for i, (source, target) in enumerate((
+            (rough_hbm, rough_ref), (factor_hbm, factor_ref), (down_hbm, down_ref),
+            (exit_hbm, exit_ref), (inlet_hbm, inlet_ref),
+        ))
+    ]
+    large = []
+    for i, first in enumerate(range(0, blocks, GROUP)):
+        size = min(GROUP, blocks - first)
+        lanes = pl.ds(first * LANES, size * LANES)
+        part = pl.ds(first, size)
+        large.append((
+            pltpu.make_async_copy(matrix_hbm.at[part], matrix_ref.at[part], matrix_sem.at[i]),
+            pltpu.make_async_copy(cot_hbm.at[:, :, lanes], cot_ref.at[:, :, lanes], cot_sem.at[i]),
+            pltpu.make_async_copy(
+                flow_hbm.at[:, :, lanes], flow_ref.at[:, :, lanes], flow_sem.at[i]
+            ),
+        ))
     lateral_copy = pltpu.make_async_copy(lateral_hbm, lateral_ref, lateral_sem)
+    for copy in small:
+        copy.start()
+    for copies in large:
+        for copy in copies:
+            copy.start()
     lateral_copy.start()
+    for copy in small:
+        copy.wait()
 
     travel = rough_ref[...] * factor_ref[...]
     weight_new, weight_old, weight_stay = weights_of(travel)
@@ -165,8 +194,21 @@
     response_in = [at_inlets(value) for value in response]
     new_in, old_in, _ = weights_of(travel_in)
 
-    for first in range(0, blocks, GROUP):
+    sub = lax.broadcasted_iota(jnp.int32, (LANES, LANES), 0)
+    leaving = None
+    for turn, first in enumerate(range(0, blocks, GROUP)):
+        for copy in large[turn]:
+            copy.wait()
         at_inlet = solve_group(first, list(at_inlet))
+        for block in range(first, min(first + GROUP, blocks)):
+            lanes = pl.ds(block * LANES, LANES)
+            table = (sub == exit_ref[pl.ds(block, 1), :]).astype(F32).astype(jnp.bfloat16)
+            part = lax.dot_general(
+                flow_ref[:, :, lanes].reshape((steps + 1) * members, LANES), table,
+                (((1,), (1,)), ((), ())), preferred_element_type=F32,
+            )
+            leaving = part if leaving is None else leaving + part
+    leaving_ref[...] = leaving
 
     for step in range(steps):
         rows = pl.ds(step * members, members)
@@ -307,43 +349,6 @@
         radices.append(radix)
         count //= radix
     return radices or [1]
-
-
-def fetch_kernel(steps, members, blocks, count, *refs):
-    sources, targets = refs[:count], refs[count:2 * count]
-    leaving_ref, flow_sem, sem = refs[2 * count:]
-    flow_hbm, flow_ref = sources[0], targets[0]
-    exit_ref = targets[1]
-    flow_copies = []
-    for turn, first in enumerate(range(0, blocks, GROUP)):
-        lanes = pl.ds(first * LANES, min(GROUP, blocks - first) * LANES)
-        flow_copies.append(pltpu.make_async_copy(
-            flow_hbm.at[:, :, lanes], flow_ref.at[:, :, lanes], flow_sem.at[turn]
-        ))
-    copies = [
-        pltpu.make_async_copy(sources[i], targets[i], sem.at[i]) for i in range(1, count)
-    ]
-    copies[0].start()
-    for copy in flow_copies:
-        copy.start()
-    for copy in copies[1:]:
-        copy.start()
-    copies[0].wait()
-    sub = lax.broadcasted_iota(jnp.int32, (LANES, LANES), 0)
-    total = None
-    for block in range(blocks):
-        if block % GROUP == 0:
-            flow_copies[block // GROUP].wait()
-        lanes = pl.ds(block * LANES, LANES)
-        table = (sub == exit_ref[pl.ds(block, 1), :]).astype(F32).astype(jnp.bfloat16)
-        flows = flow_ref[:, :, lanes].reshape((steps + 1) * members, LANES)
-        part = lax.dot_general(
-            flows, table, (((1,), (1,)), ((), ())), preferred_element_type=F32
-        )
-        total = part if total is None else total + part
-    leaving_ref[...] = total
-    for copy in copies[1:]:
-        copy.wait()
 
 
 def weight_kernel(
@@ -520,39 +525,44 @@
     def stay_out(array):
         return pltpu.with_memory_space_constraint(array, pltpu.HBM)
 
-    inputs = (
-        stored_reach_flows, leave, rough, factor, down, inlet_reach, inverse_block_matrix, cotangent
-    )
-    flows, leave, rough, factor, down, inlets, matrix, cotangent, leaving = call(
-        functools.partial(fetch_kernel, steps, members, blocks, len(inputs)),
-        tuple(shape(array.shape, array.dtype) for array in inputs)
-        + (shape(((steps + 1) * members, LANES), F32),),
-        scratch=[
-            pltpu.SemaphoreType.DMA((-(-blocks // GROUP),)),
-            pltpu.SemaphoreType.DMA((len(inputs),)),
-        ],
-        flops=2 * LANES * work,
-        size=9 * work,
-        in_specs=[hbm] * len(inputs),
-    )(*(stay_out(array) for array in inputs))
-    arriving = lax.ppermute(leaving, "net", [(i, i + 1) for i in range(count - 1)])
-
-    own, message, response, slot, inlet_values, inlet_rows, lateral = call(
+    small = (rough, factor, down, leave, inlet_reach)
+    turns = -(-blocks // GROUP)
+    (
+        own, message, leaving, response, slot, inlet_values, inlet_rows,
+        flows, lateral, rough, factor, down, inlets,
+    ) = call(
         functools.partial(local_kernel, steps, members, blocks),
         (
             shape((steps, members, reaches), F32),
             shape((rows, LANES), F32),
+            shape(((steps + 1) * members, LANES), F32),
             shape((steps, blocks, LANES), F32),
             shape((blocks, LANES), jnp.int32),
             shape((steps * members, LANES), F32),
             shape((EXTRA, LANES), F32),
-            shape(lateral.shape, lateral.dtype),
+        ) + tuple(
+            shape(array.shape, array.dtype)
+            for array in (stored_reach_flows, lateral, rough, factor, down, inlet_reach)
         ),
-        scratch=[pltpu.VMEM((blocks, LANES), F32)] * 2 + [pltpu.SemaphoreType.DMA],
-        flops=8 * LANES * work,
-        size=6 * work,
-        in_specs=[pl.BlockSpec()] * 7 + [hbm],
-    )(cotangent, matrix, rough, factor, down, leave, inlets, stay_out(lateral))
+        scratch=[
+            pltpu.VMEM(leave.shape, leave.dtype),
+            pltpu.VMEM(cotangent.shape, cotangent.dtype),
+            pltpu.VMEM(inverse_block_matrix.shape, inverse_block_matrix.dtype),
+            pltpu.VMEM((blocks, LANES), F32),
+            pltpu.VMEM((blocks, LANES), F32),
+            pltpu.SemaphoreType.DMA((len(small),)),
+            pltpu.SemaphoreType.DMA((turns,)),
+            pltpu.SemaphoreType.DMA((turns,)),
+            pltpu.SemaphoreType.DMA((turns,)),
+            pltpu.SemaphoreType.DMA,
+        ],
+        flops=10 * LANES * work,
+        size=10 * work,
+        in_specs=[hbm] * (4 + len(small)),
+    )(*(
+        stay_out(array)
+        for array in (stored_reach_flows, lateral, cotangent, inverse_block_matrix) + small
+    ))
 
     weight, own_part = call(
         functools.partial(weight_kernel, steps, members, blocks),
@@ -566,12 +576,11 @@
     inner = ()
     radices = radices_of(count)
     for turn, radix in enumerate(radices[:-1]):
-        received = [
+        received = [message] + [
             exchange(message, "net", stride, radix, offset) for offset in range(1, radix)
         ]
         if turn == 0:
-            message, weight = lax.optimization_barrier((message, weight))
-        received = [message] + received
+            arriving = lax.ppermute(leaving, "net", [(i, i + 1) for i in range(count - 1)])
         later, message = call(
             functools.partial(group_kernel, steps, members, "net", stride, radix, len(inner)),
             (shape((rows, LANES), F32),) * 2,
@@ -581,6 +590,8 @@
         inner = (later,)
         stride *= radix
     radix = radices[-1]
+    if len(radices) == 1:
+        arriving = lax.ppermute(leaving, "net", [(i, i + 1) for i in range(count - 1)])
     received = [message] + [
         exchange(message, "net", stride, radix, offset) for offset in range(1, radix)
     ]

time: 28.3 us -> 27.9 us (0.986)
  waiting for transfers between devices: 3.87 us -> 2.28 us
  Pallas kernels: 9.83 us -> 11.2 us
    pallas_call x1, Pallas kernels: 2.32 us -> 6.27 us  [gradients(): call(functools.partial(local_kernel, steps, members, blocks), (shape((ste...]
    pallas_call x1 -> x0, Pallas kernels: 2.55 us -> none  [gradients(): call(functools.partial(fetch_kernel, steps, members, blocks, len(inputs))...]
    ppermute x7, waiting for transfers between devices: 3.87 us -> 2.27 us  [exchange(): return lax.ppermute(value, axis, pairs)]
  transfers between devices with their start and end apart: 8 -> 8, of which waited for: 3 -> 4; matrix products, arithmetic and copies ran while one was open for 0% -> 0% of each run, Pallas kernels for 13% -> 13%
where the time goes in v5:
time: 27.9 us; the launch traced here: 27.8 us
  starting transfers between devices  13 us (47%)
  Pallas kernels  11.2 us (40%)
  waiting for transfers between devices  2.28 us (8%)
  between operations  0.73 us (3%)
  other arithmetic  0.6 us (2%)
    ppermute x7, starting transfers between devices, exchange(): return lax.ppermute(value, axis, pairs)  9.27 us
    pallas_call x1, Pallas kernels, gradients(): call(functools.partial(local_kernel, steps, members, blocks), (shape((ste...  6.27 us
    ppermute x1, starting transfers between devices, gradients(): lax.ppermute(leaving, 'net', [(i, i + 1) for i in range(count - 1)])  3.72 us
    ppermute x7, waiting for transfers between devices, exchange(): return lax.ppermute(value, axis, pairs)  2.27 us
    pallas_call x1, Pallas kernels, gradients(): call(functools.partial(weight_kernel, steps, members, blocks), (shape((st...  1.95 us
    pallas_call x1, Pallas kernels, gradients(): call(functools.partial(grad_kernel, steps, members, blocks, chunks), shap...  1.48 us
    pallas_call x1, Pallas kernels, gradients(): call(functools.partial(sums_kernel, steps, members, blocks, ranks, stride...  1.2 us
    reshape x1, other arithmetic, gradients(): return (grad_lateral, total.reshape(-1))  0.6 us
  transfers between devices with their start and end apart: 8, of which 4 were waited for; matrix products, arithmetic and copies ran while one was open for 0% of the time, Pallas kernels for 13%

profile of v5, /device:TPU:0, one launch (start us, length us, event | category | flops | bytes accessed | tf_op | source)
XLA Modules:
  0.0 27.8 jit_solution(4313734209593424979)
XLA Ops:
  0.6 6.3 %shard_map.104 = (f32[4,32,4096]{2,1,0:T(8,128)S(1)}, f32[136,128]{1,0:T(8,128)S(1)}, f32[160,128]{1,0:T(8,128)S(1)}, f32[4,32,128]{2,1,0:T(8,128)S(1)}, s32[32,...) custom-call(bf16[5,32,4096]{2,1,0:T(8,128)(2,1)} %flow_hbm.1, ...), custom_call_target="tpu_custom_call" | custom-call | flops 671088640 | bytes 5242880 | tf_op jit(solution)/shard_map/pallas_call | solution.py:533
  6.9 4.0 %collective-permute-start.2 = (f32[136,128]{1,0:T(8,128)S(1)}, f32[136,128]{1,0:T(8,128)S(1)}, u32[]{:S(2)}, u32[]{:S(2)}) collective-permute-start(f32[136,128]{1,0:T(8,128)S(1)} %get-tuple-element.24.refs_0_), channel_id=1, source_target_pairs={{12,0},{8,4},{4,8},{0,12},{28,16},{24,20},{20,24},{16,28},{13,1},{... | collective-permute-start | bytes 208904 | tf_op jit(solution)/shard_map/ppermute | solution.py:342
  11.0 0.4 %collective-permute-start.1 = (f32[136,128]{1,0:T(8,128)S(1)}, f32[136,128]{1,0:T(8,128)S(1)}, u32[]{:S(2)}, u32[]{:S(2)}) collective-permute-start(f32[136,128]{1,0:T(8,128)S(1)} %get-tuple-element.24.refs_0_), channel_id=1, source_target_pairs={{8,0},{12,4},{0,8},{4,12},{24,16},{28,20},{16,24},{20,28},{9,1},{1... | collective-permute-start | bytes 208904 | tf_op jit(solution)/shard_map/ppermute | solution.py:342
  11.4 0.2 collective-permute-start
  11.6 3.7 %collective-permute-start.4 = (f32[160,128]{1,0:T(8,128)S(1)}, f32[160,128]{1,0:T(8,128)S(1)}, u32[]{:S(2)}, u32[]{:S(2)}) collective-permute-start(f32[160,128]{1,0:T(8,128)S(1)} %get-tuple-element.39), channel_id=1, source_target_pairs={{0,4},{4,8},{8,12},{12,16},{16,20},{20,24},{24,28},{1,5},{5,9},{9,... | collective-permute-start | bytes 245768 | tf_op jit(solution)/shard_map/ppermute | solution.py:583
  15.3 0.0 collective-permute-done.2.refs_3_
  15.3 0.0 collective-permute-done.1.refs_2_
  15.4 0.4 %collective-permute-done.refs_1_ = f32[136,128]{1,0:T(8,128)S(1)} collective-permute-done((f32[136,128]{1,0:T(8,128)S(1)}, f32[136,128]{1,0:T(8,128)S(1)}, u32[]{:S(2)}, u32[]{:S(2)}) %collective-permute-start) | collective-permute-done | bytes 69664 | tf_op jit(solution)/shard_map/ppermute | solution.py:342
  15.7 0.3 shard_map.105
  16.0 2.7 %collective-permute-start.3 = (f32[136,128]{1,0:T(8,128)S(1)}, f32[136,128]{1,0:T(8,128)S(1)}, u32[]{:S(2)}, u32[]{:S(2)}) collective-permute-start(f32[136,128]{1,0:T(8,128)S(1)} %get-tuple-element.25.refs_0_), channel_id=1, source_target_pairs={{16,0},{20,4},{24,8},{28,12},{0,16},{4,20},{8,24},{12,28},{17,1},{... | collective-permute-start | bytes 208904 | tf_op jit(solution)/shard_map/ppermute | solution.py:342
  18.7 2.0 %shard_map.106 = (f32[4,32,4096]{2,1,0:T(8,128)S(1)}, f32[32,128]{1,0:T(8,128)S(1)}) custom-call(bf16[5,32,4096]{2,1,0:T(8,128)(2,1)S(1)} %get-tuple-element.28.flow_ref, bf16[4,32,4096]{2,1,0:T(8,128)(2,1)S(1)} %get-tuple-element.29.lateral_ref, f32[4,32,4096]{2,1,0:T(8,128)S(1)} %get-tuple-element.30.own_ref, ...), custom_call_target="tpu_custom_call" | custom-call | flops 134217728 | bytes 4194304 | tf_op jit(solution)/shard_map/pallas_call | solution.py:567
  20.6 0.0 collective-permute-done.4.refs_9_
  20.6 0.6 %collective-permute-done.3.refs_1_ = f32[136,128]{1,0:T(8,128)S(1)} collective-permute-done((f32[136,128]{1,0:T(8,128)S(1)}, f32[136,128]{1,0:T(8,128)S(1)}, u32[]{:S(2)}, u32[]{:S(2)}) %collective-permute-start.3) | collective-permute-done | bytes 69664 | tf_op jit(solution)/shard_map/ppermute | solution.py:342
  21.3 1.2 %shard_map.107 = (f32[128,128]{1,0:T(8,128)S(1)}, f32[8,128]{1,0:T(8,128)S(1)}, f32[8,128]{1,0:T(8,128)S(1)}, f32[8,128]{1,0:T(8,128)S(1)}, f32[8,128]{1,0:T(8,128)S(1)}) custom-call(f32[136,128]{1,0:T(8,128)S(1)} %get-tuple-element.25.refs_0_, f32[136,128]{1,0:T(8,128)S(1)} %collective-permute-done.3.refs_1_, f32[136,128]{1,0:T(8,128)S(1)} %get-tuple-element.26.refs_2_, ...), custom_call_target="tpu_custom_call" | custom-call | flops 10485760 | bytes 2097152 | tf_op jit(solution)/shard_map/pallas_call | solution.py:600
  22.5 0.1 collective-permute-start.5
  22.6 1.6 %collective-permute-start.6 = (f32[8,128]{1,0:T(8,128)S(1)}, f32[8,128]{1,0:T(8,128)S(1)}, u32[]{:S(2)}, u32[]{:S(2)}) collective-permute-start(f32[8,128]{1,0:T(8,128)S(1)} %get-tuple-element.44), channel_id=1, source_target_pairs={{2,0},{3,1},{0,2},{1,3},{6,4},{7,5},{4,6},{5,7},{10,8},{11,9},{8,1... | collective-permute-start | bytes 12296 | tf_op jit(solution)/shard_map/ppermute | solution.py:342
  24.1 0.3 collective-permute-start.7
  24.4 1.5 %shard_map.108 = bf16[4,32,4096]{2,1,0:T(8,128)(2,1)} custom-call(f32[128,128]{1,0:T(8,128)S(1)} %get-tuple-element.41.incoming_ref, f32[4,32,4096]{2,1,0:T(8,128)S(1)} %get-tuple-element.30.own_ref, f32[4,32,128]{2,1,0:T(8,128)S(1)} %get-tuple-element.31.response_ref, s32[32,128]{1,0:T(8,128)S(1)} %get-tuple-element.27.refs_3_.slot_ref, ...), custom_call_target="tpu_custom_call" | custom-call | flops 15728640 | bytes 3145728 | tf_op jit(solution)/shard_map/pallas_call | solution.py:613
  25.9 0.0 collective-permute-done.5
  25.9 0.3 %collective-permute-done.6 = f32[8,128]{1,0:T(8,128)S(1)} collective-permute-done((f32[8,128]{1,0:T(8,128)S(1)}, f32[8,128]{1,0:T(8,128)S(1)}, u32[]{:S(2)}, u32[]{:S(2)}) %collective-permute-start.6) | collective-permute-done | bytes 4128 | tf_op jit(solution)/shard_map/ppermute | solution.py:342
  26.2 0.9 %collective-permute-done.7 = f32[8,128]{1,0:T(8,128)S(1)} collective-permute-done((f32[8,128]{1,0:T(8,128)S(1)}, f32[8,128]{1,0:T(8,128)S(1)}, u32[]{:S(2)}, u32[]{:S(2)}) %collective-permute-start.7) | collective-permute-done | bytes 4128 | tf_op jit(solution)/shard_map/ppermute | solution.py:342
  27.2 0.6 %add_bitcast_fusion = f32[1024]{0:T(1024)} fusion(f32[8,128]{1,0:T(8,128)S(1)} %collective-permute-done.7, f32[8,128]{1,0:T(8,128)S(1)} %collective-permute-done.6, f32[8,128]{1,0:T(8,128)S(1)} %get-tuple-element.42, f32[8,128]{1,0:T(8,128)S(1)} %collective-permute-done.5), kind=kLoop, calls=%fused_computation | loop fusion | flops 3072 | bytes 20480 | tf_op jit(solution)/shard_map/reshape | solution.py:629
Async XLA Ops:
  6.9 8.4 %collective-permute-start.2 = (f32[136,128]{1,0:T(8,128)S(1)}, f32[136,128]{1,0:T(8,128)S(1)}, u32[]{:S(2)}, u32[]{:S(2)}) collective-permute-start(f32[136,128]{1,0:T(8,128)S(1)} %get-tuple-element.24.refs_0_), channel_id=1, source_target_pairs={{12,0},{8,4},{4,8},{0,12},{28,16},{24,20},{20,24},{16,28},{13,1},{... | collective-permute-start | bytes 208904 | tf_op jit(solution)/shard_map/ppermute | solution.py:342
  11.0 4.4 %collective-permute-start.1 = (f32[136,128]{1,0:T(8,128)S(1)}, f32[136,128]{1,0:T(8,128)S(1)}, u32[]{:S(2)}, u32[]{:S(2)}) collective-permute-start(f32[136,128]{1,0:T(8,128)S(1)} %get-tuple-element.24.refs_0_), channel_id=1, source_target_pairs={{8,0},{12,4},{0,8},{4,12},{24,16},{28,20},{16,24},{20,28},{9,1},{1... | collective-permute-start | bytes 208904 | tf_op jit(solution)/shard_map/ppermute | solution.py:342
  11.4 4.3 %collective-permute-start = (f32[136,128]{1,0:T(8,128)S(1)}, f32[136,128]{1,0:T(8,128)S(1)}, u32[]{:S(2)}, u32[]{:S(2)}) collective-permute-start(f32[136,128]{1,0:T(8,128)S(1)} %get-tuple-element.24.refs_0_), channel_id=1, source_target_pairs={{4,0},{0,4},{12,8},{8,12},{20,16},{16,20},{28,24},{24,28},{5,1},{1... | collective-permute-start | bytes 208904 | tf_op jit(solution)/shard_map/ppermute | solution.py:342
  11.6 9.0 %collective-permute-start.4 = (f32[160,128]{1,0:T(8,128)S(1)}, f32[160,128]{1,0:T(8,128)S(1)}, u32[]{:S(2)}, u32[]{:S(2)}) collective-permute-start(f32[160,128]{1,0:T(8,128)S(1)} %get-tuple-element.39), channel_id=1, source_target_pairs={{0,4},{4,8},{8,12},{12,16},{16,20},{20,24},{24,28},{1,5},{5,9},{9,... | collective-permute-start | bytes 245768 | tf_op jit(solution)/shard_map/ppermute | solution.py:583
  16.0 5.3 %collective-permute-start.3 = (f32[136,128]{1,0:T(8,128)S(1)}, f32[136,128]{1,0:T(8,128)S(1)}, u32[]{:S(2)}, u32[]{:S(2)}) collective-permute-start(f32[136,128]{1,0:T(8,128)S(1)} %get-tuple-element.25.refs_0_), channel_id=1, source_target_pairs={{16,0},{20,4},{24,8},{28,12},{0,16},{4,20},{8,24},{12,28},{17,1},{... | collective-permute-start | bytes 208904 | tf_op jit(solution)/shard_map/ppermute | solution.py:342
  22.5 3.4 %collective-permute-start.5 = (f32[8,128]{1,0:T(8,128)S(1)}, f32[8,128]{1,0:T(8,128)S(1)}, u32[]{:S(2)}, u32[]{:S(2)}) collective-permute-start(f32[8,128]{1,0:T(8,128)S(1)} %get-tuple-element.43), channel_id=1, source_target_pairs={{1,0},{0,1},{3,2},{2,3},{5,4},{4,5},{7,6},{6,7},{9,8},{8,9},{11,10... | collective-permute-start | bytes 12296 | tf_op jit(solution)/shard_map/ppermute | solution.py:342
  22.6 3.7 %collective-permute-start.6 = (f32[8,128]{1,0:T(8,128)S(1)}, f32[8,128]{1,0:T(8,128)S(1)}, u32[]{:S(2)}, u32[]{:S(2)}) collective-permute-start(f32[8,128]{1,0:T(8,128)S(1)} %get-tuple-element.44), channel_id=1, source_target_pairs={{2,0},{3,1},{0,2},{1,3},{6,4},{7,5},{4,6},{5,7},{10,8},{11,9},{8,1... | collective-permute-start | bytes 12296 | tf_op jit(solution)/shard_map/ppermute | solution.py:342
  24.1 3.0 %collective-permute-start.7 = (f32[8,128]{1,0:T(8,128)S(1)}, f32[8,128]{1,0:T(8,128)S(1)}, u32[]{:S(2)}, u32[]{:S(2)}) collective-permute-start(f32[8,128]{1,0:T(8,128)S(1)} %get-tuple-element.45), channel_id=1, source_target_pairs={{3,0},{2,1},{1,2},{0,3},{7,4},{6,5},{5,6},{4,7},{11,8},{10,9},{9,1... | collective-permute-start | bytes 12296 | tf_op jit(solution)/shard_map/ppermute | solution.py:342

commit v6 on v4

--- a/solution.py
+++ b/solution.py
@@ -19,7 +19,8 @@
     operand_batching_dims=(0,), start_indices_batching_dims=(0,),
 )
 VMEM_BYTES = 20 << 20
-GROUP = 8
+GROUP = 16
+CHUNK = 8
 
 
 def take(values, index):
@@ -186,6 +187,43 @@
     lateral_copy.wait()
 
 
+def fetch_kernel(steps, members, blocks, count, *refs):
+    sources, targets = refs[:count], refs[count:2 * count]
+    leaving_ref, flow_sem, sem = refs[2 * count:]
+    flow_hbm, flow_ref = sources[0], targets[0]
+    exit_ref = targets[1]
+    flow_copies = []
+    for turn, first in enumerate(range(0, blocks, CHUNK)):
+        lanes = pl.ds(first * LANES, min(CHUNK, blocks - first) * LANES)
+        flow_copies.append(pltpu.make_async_copy(
+            flow_hbm.at[:, :, lanes], flow_ref.at[:, :, lanes], flow_sem.at[turn]
+        ))
+    copies = [
+        pltpu.make_async_copy(sources[i], targets[i], sem.at[i]) for i in range(1, count)
+    ]
+    copies[0].start()
+    for copy in flow_copies:
+        copy.start()
+    for copy in copies[1:]:
+        copy.start()
+    copies[0].wait()
+    sub = lax.broadcasted_iota(jnp.int32, (LANES, LANES), 0)
+    total = None
+    for block in range(blocks):
+        if block % CHUNK == 0:
+            flow_copies[block // CHUNK].wait()
+        lanes = pl.ds(block * LANES, LANES)
+        table = (sub == exit_ref[pl.ds(block, 1), :]).astype(F32).astype(jnp.bfloat16)
+        flows = flow_ref[:, :, lanes].reshape((steps + 1) * members, LANES)
+        part = lax.dot_general(
+            flows, table, (((1,), (1,)), ((), ())), preferred_element_type=F32
+        )
+        total = part if total is None else total + part
+    leaving_ref[...] = total
+    for copy in copies[1:]:
+        copy.wait()
+
+
 def eight_rows(rows):
     rows = list(rows)
     while len(rows) % EXTRA:
@@ -307,43 +345,6 @@
         radices.append(radix)
         count //= radix
     return radices or [1]
-
-
-def fetch_kernel(steps, members, blocks, count, *refs):
-    sources, targets = refs[:count], refs[count:2 * count]
-    leaving_ref, flow_sem, sem = refs[2 * count:]
-    flow_hbm, flow_ref = sources[0], targets[0]
-    exit_ref = targets[1]
-    flow_copies = []
-    for turn, first in enumerate(range(0, blocks, GROUP)):
-        lanes = pl.ds(first * LANES, min(GROUP, blocks - first) * LANES)
-        flow_copies.append(pltpu.make_async_copy(
-            flow_hbm.at[:, :, lanes], flow_ref.at[:, :, lanes], flow_sem.at[turn]
-        ))
-    copies = [
-        pltpu.make_async_copy(sources[i], targets[i], sem.at[i]) for i in range(1, count)
-    ]
-    copies[0].start()
-    for copy in flow_copies:
-        copy.start()
-    for copy in copies[1:]:
-        copy.start()
-    copies[0].wait()
-    sub = lax.broadcasted_iota(jnp.int32, (LANES, LANES), 0)
-    total = None
-    for block in range(blocks):
-        if block % GROUP == 0:
-            flow_copies[block // GROUP].wait()
-        lanes = pl.ds(block * LANES, LANES)
-        table = (sub == exit_ref[pl.ds(block, 1), :]).astype(F32).astype(jnp.bfloat16)
-        flows = flow_ref[:, :, lanes].reshape((steps + 1) * members, LANES)
-        part = lax.dot_general(
-            flows, table, (((1,), (1,)), ((), ())), preferred_element_type=F32
-        )
-        total = part if total is None else total + part
-    leaving_ref[...] = total
-    for copy in copies[1:]:
-        copy.wait()
 
 
 def weight_kernel(
@@ -528,15 +529,13 @@
         tuple(shape(array.shape, array.dtype) for array in inputs)
         + (shape(((steps + 1) * members, LANES), F32),),
         scratch=[
-            pltpu.SemaphoreType.DMA((-(-blocks // GROUP),)),
+            pltpu.SemaphoreType.DMA((-(-blocks // CHUNK),)),
             pltpu.SemaphoreType.DMA((len(inputs),)),
         ],
         flops=2 * LANES * work,
         size=9 * work,
         in_specs=[hbm] * len(inputs),
     )(*(stay_out(array) for array in inputs))
-    arriving = lax.ppermute(leaving, "net", [(i, i + 1) for i in range(count - 1)])
-
     own, message, response, slot, inlet_values, inlet_rows, lateral = call(
         functools.partial(local_kernel, steps, members, blocks),
         (
@@ -566,12 +565,11 @@
     inner = ()
     radices = radices_of(count)
     for turn, radix in enumerate(radices[:-1]):
-        received = [
+        received = [message] + [
             exchange(message, "net", stride, radix, offset) for offset in range(1, radix)
         ]
         if turn == 0:
-            message, weight = lax.optimization_barrier((message, weight))
-        received = [message] + received
+            arriving = lax.ppermute(leaving, "net", [(i, i + 1) for i in range(count - 1)])
         later, message = call(
             functools.partial(group_kernel, steps, members, "net", stride, radix, len(inner)),
             (shape((rows, LANES), F32),) * 2,
@@ -581,6 +579,8 @@
         inner = (later,)
         stride *= radix
     radix = radices[-1]
+    if len(radices) == 1:
+        arriving = lax.ppermute(leaving, "net", [(i, i + 1) for i in range(count - 1)])
     received = [message] + [
         exchange(message, "net", stride, radix, offset) for offset in range(1, radix)
     ]

time: 28.3 us -> 26 us (0.919)
  waiting for transfers between devices: 3.87 us -> 2.25 us
  Pallas kernels: 9.83 us -> 9.2 us
    ppermute x7, waiting for transfers between devices: 3.87 us -> 2.25 us  [exchange(): return lax.ppermute(value, axis, pairs)]
    pallas_call x1, Pallas kernels: 2.32 us -> 1.71 us  [gradients(): call(functools.partial(local_kernel, steps, members, blocks), (shape((ste...]
  transfers between devices with their start and end apart: 8 -> 8, of which waited for: 3 -> 4; matrix products, arithmetic and copies ran while one was open for 0% -> 0% of each run, Pallas kernels for 13% -> 14%
where the time goes in v6:
time: 26 us; the launch traced here: 25.8 us
  starting transfers between devices  13 us (50%)
  Pallas kernels  9.2 us (35%)
  waiting for transfers between devices  2.25 us (9%)
  between operations  0.73 us (3%)
  other arithmetic  0.6 us (2%)
    ppermute x7, starting transfers between devices, exchange(): return lax.ppermute(value, axis, pairs)  9.26 us
    ppermute x1, starting transfers between devices, gradients(): lax.ppermute(leaving, 'net', [(i, i + 1) for i in range(count - 1)])  3.73 us
    pallas_call x1, Pallas kernels, gradients(): call(functools.partial(fetch_kernel, steps, members, blocks, len(inputs))...  2.55 us
    ppermute x7, waiting for transfers between devices, exchange(): return lax.ppermute(value, axis, pairs)  2.25 us
    pallas_call x1, Pallas kernels, gradients(): call(functools.partial(weight_kernel, steps, members, blocks), (shape((st...  1.96 us
    pallas_call x1, Pallas kernels, gradients(): call(functools.partial(local_kernel, steps, members, blocks), (shape((ste...  1.71 us
    pallas_call x1, Pallas kernels, gradients(): call(functools.partial(grad_kernel, steps, members, blocks, chunks), shap...  1.5 us
    pallas_call x1, Pallas kernels, gradients(): call(functools.partial(sums_kernel, steps, members, blocks, ranks, stride...  1.2 us
  transfers between devices with their start and end apart: 8, of which 4 were waited for; matrix products, arithmetic and copies ran while one was open for 0% of the time, Pallas kernels for 14%

profile of v6, /device:TPU:0, one launch (start us, length us, event | category | flops | bytes accessed | tf_op | source)
XLA Modules:
  0.0 25.8 jit_solution(2106118060428398589)
XLA Ops:
  0.6 2.6 %shard_map.104 = (bf16[5,32,4096]{2,1,0:T(8,128)(2,1)S(1)}, s32[32,128]{1,0:T(8,128)S(1)}, f32[32,128]{1,0:T(8,128)S(1)}, f32[32,128]{1,0:T(8,128)S(1)}, s32[32,...) custom-call(bf16[5,32,4096]{2,1,0:T(8,128)(2,1)} %refs_0_.1, ...), custom_call_target="tpu_custom_call" | custom-call | flops 134217728 | bytes 4718592 | tf_op jit(solution)/shard_map/pallas_call | solution.py:527
  3.2 1.7 %shard_map.105 = (f32[4,32,4096]{2,1,0:T(8,128)S(1)}, f32[136,128]{1,0:T(8,128)S(1)}, f32[4,32,128]{2,1,0:T(8,128)S(1)}, s32[32,128]{1,0:T(8,128)S(1)}, f32[128,...) custom-call(bf16[4,32,4096]{2,1,0:T(8,128)(2,1)S(1)} %get-tuple-element.27.cot_ref, ...), custom_call_target="tpu_custom_call" | custom-call | flops 536870912 | bytes 3145728 | tf_op jit(solution)/shard_map/pallas_call | solution.py:539
  4.9 4.0 %collective-permute-start.2 = (f32[136,128]{1,0:T(8,128)S(1)}, f32[136,128]{1,0:T(8,128)S(1)}, u32[]{:S(2)}, u32[]{:S(2)}) collective-permute-start(f32[136,128]{1,0:T(8,128)S(1)} %get-tuple-element.34.refs_0_), channel_id=1, source_target_pairs={{12,0},{8,4},{4,8},{0,12},{28,16},{24,20},{20,24},{16,28},{13,1},{... | collective-permute-start | bytes 208904 | tf_op jit(solution)/shard_map/ppermute | solution.py:338
  9.0 0.4 %collective-permute-start.1 = (f32[136,128]{1,0:T(8,128)S(1)}, f32[136,128]{1,0:T(8,128)S(1)}, u32[]{:S(2)}, u32[]{:S(2)}) collective-permute-start(f32[136,128]{1,0:T(8,128)S(1)} %get-tuple-element.34.refs_0_), channel_id=1, source_target_pairs={{8,0},{12,4},{0,8},{4,12},{24,16},{28,20},{16,24},{20,28},{9,1},{1... | collective-permute-start | bytes 208904 | tf_op jit(solution)/shard_map/ppermute | solution.py:338
  9.4 0.2 collective-permute-start
  9.6 3.7 %collective-permute-start.4 = (f32[160,128]{1,0:T(8,128)S(1)}, f32[160,128]{1,0:T(8,128)S(1)}, u32[]{:S(2)}, u32[]{:S(2)}) collective-permute-start(f32[160,128]{1,0:T(8,128)S(1)} %get-tuple-element.46), channel_id=1, source_target_pairs={{0,4},{4,8},{8,12},{12,16},{16,20},{20,24},{24,28},{1,5},{5,9},{9,... | collective-permute-start | bytes 245768 | tf_op jit(solution)/shard_map/ppermute | solution.py:572
  13.3 0.0 collective-permute-done.2.refs_3_
  13.3 0.0 collective-permute-done.1.refs_2_
  13.4 0.4 %collective-permute-done.refs_1_ = f32[136,128]{1,0:T(8,128)S(1)} collective-permute-done((f32[136,128]{1,0:T(8,128)S(1)}, f32[136,128]{1,0:T(8,128)S(1)}, u32[]{:S(2)}, u32[]{:S(2)}) %collective-permute-start) | collective-permute-done | bytes 69664 | tf_op jit(solution)/shard_map/ppermute | solution.py:338
  13.7 0.3 %shard_map.106 = (f32[136,128]{1,0:T(8,128)S(1)}, f32[136,128]{1,0:T(8,128)S(1)}) custom-call(f32[136,128]{1,0:T(8,128)S(1)} %get-tuple-element.34.refs_0_, f32[136,128]{1,0:T(8,128)S(1)} %collective-permute-done.refs_1_, f32[136,128]{1,0:T(8,128)S(1)} %collective-permute-done.1.refs_2_, f32[136,128]{1,0:T(8,128)S(1)} %collective-permute-done.2.refs_3_), custom_call_target="tpu_custom_call" | custom-call | flops 1392640 | bytes 278528 | tf_op jit(solution)/shard_map/pallas_call | solution.py:573
  14.0 2.7 %collective-permute-start.3 = (f32[136,128]{1,0:T(8,128)S(1)}, f32[136,128]{1,0:T(8,128)S(1)}, u32[]{:S(2)}, u32[]{:S(2)}) collective-permute-start(f32[136,128]{1,0:T(8,128)S(1)} %get-tuple-element.35.refs_0_), channel_id=1, source_target_pairs={{16,0},{20,4},{24,8},{28,12},{0,16},{4,20},{8,24},{12,28},{17,1},{... | collective-permute-start | bytes 208904 | tf_op jit(solution)/shard_map/ppermute | solution.py:338
  16.7 2.0 %shard_map.107 = (f32[4,32,4096]{2,1,0:T(8,128)S(1)}, f32[32,128]{1,0:T(8,128)S(1)}) custom-call(bf16[5,32,4096]{2,1,0:T(8,128)(2,1)S(1)} %get-tuple-element.38.flow_ref, bf16[4,32,4096]{2,1,0:T(8,128)(2,1)S(1)} %get-tuple-element.39.lateral_ref, f32[4,32,4096]{2,1,0:T(8,128)S(1)} %get-tuple-element.40.own_ref, ...), custom_call_target="tpu_custom_call" | custom-call | flops 134217728 | bytes 4194304 | tf_op jit(solution)/shard_map/pallas_call | solution.py:556
  18.6 0.0 collective-permute-done.4.refs_9_
  18.6 0.6 %collective-permute-done.3.refs_1_ = f32[136,128]{1,0:T(8,128)S(1)} collective-permute-done((f32[136,128]{1,0:T(8,128)S(1)}, f32[136,128]{1,0:T(8,128)S(1)}, u32[]{:S(2)}, u32[]{:S(2)}) %collective-permute-start.3) | collective-permute-done | bytes 69664 | tf_op jit(solution)/shard_map/ppermute | solution.py:338
  19.3 1.2 %shard_map.108 = (f32[128,128]{1,0:T(8,128)S(1)}, f32[8,128]{1,0:T(8,128)S(1)}, f32[8,128]{1,0:T(8,128)S(1)}, f32[8,128]{1,0:T(8,128)S(1)}, f32[8,128]{1,0:T(8,128)S(1)}) custom-call(f32[136,128]{1,0:T(8,128)S(1)} %get-tuple-element.35.refs_0_, f32[136,128]{1,0:T(8,128)S(1)} %collective-permute-done.3.refs_1_, f32[136,128]{1,0:T(8,128)S(1)} %get-tuple-element.36.refs_2_, ...), custom_call_target="tpu_custom_call" | custom-call | flops 10485760 | bytes 2097152 | tf_op jit(solution)/shard_map/pallas_call | solution.py:589
  20.5 0.1 collective-permute-start.5
  20.6 1.6 %collective-permute-start.6 = (f32[8,128]{1,0:T(8,128)S(1)}, f32[8,128]{1,0:T(8,128)S(1)}, u32[]{:S(2)}, u32[]{:S(2)}) collective-permute-start(f32[8,128]{1,0:T(8,128)S(1)} %get-tuple-element.50), channel_id=1, source_target_pairs={{2,0},{3,1},{0,2},{1,3},{6,4},{7,5},{4,6},{5,7},{10,8},{11,9},{8,1... | collective-permute-start | bytes 12296 | tf_op jit(solution)/shard_map/ppermute | solution.py:338
  22.1 0.3 %collective-permute-start.7 = (f32[8,128]{1,0:T(8,128)S(1)}, f32[8,128]{1,0:T(8,128)S(1)}, u32[]{:S(2)}, u32[]{:S(2)}) collective-permute-start(f32[8,128]{1,0:T(8,128)S(1)} %get-tuple-element.51), channel_id=1, source_target_pairs={{3,0},{2,1},{1,2},{0,3},{7,4},{6,5},{5,6},{4,7},{11,8},{10,9},{9,1... | collective-permute-start | bytes 12296 | tf_op jit(solution)/shard_map/ppermute | solution.py:338
  22.4 1.5 %shard_map.109 = bf16[4,32,4096]{2,1,0:T(8,128)(2,1)} custom-call(f32[128,128]{1,0:T(8,128)S(1)} %get-tuple-element.47.incoming_ref, f32[4,32,4096]{2,1,0:T(8,128)S(1)} %get-tuple-element.40.own_ref, f32[4,32,128]{2,1,0:T(8,128)S(1)} %get-tuple-element.41.response_ref, s32[32,128]{1,0:T(8,128)S(1)} %get-tuple-element.37.refs_3_.slot_ref, ...), custom_call_target="tpu_custom_call" | custom-call | flops 15728640 | bytes 3145728 | tf_op jit(solution)/shard_map/pallas_call | solution.py:602
  23.9 0.0 collective-permute-done.5
  23.9 0.3 %collective-permute-done.6 = f32[8,128]{1,0:T(8,128)S(1)} collective-permute-done((f32[8,128]{1,0:T(8,128)S(1)}, f32[8,128]{1,0:T(8,128)S(1)}, u32[]{:S(2)}, u32[]{:S(2)}) %collective-permute-start.6) | collective-permute-done | bytes 4128 | tf_op jit(solution)/shard_map/ppermute | solution.py:338
  24.2 0.9 %collective-permute-done.7 = f32[8,128]{1,0:T(8,128)S(1)} collective-permute-done((f32[8,128]{1,0:T(8,128)S(1)}, f32[8,128]{1,0:T(8,128)S(1)}, u32[]{:S(2)}, u32[]{:S(2)}) %collective-permute-start.7) | collective-permute-done | bytes 4128 | tf_op jit(solution)/shard_map/ppermute | solution.py:338
  25.2 0.6 %add_bitcast_fusion = f32[1024]{0:T(1024)} fusion(f32[8,128]{1,0:T(8,128)S(1)} %collective-permute-done.7, f32[8,128]{1,0:T(8,128)S(1)} %collective-permute-done.6, f32[8,128]{1,0:T(8,128)S(1)} %get-tuple-element.48, f32[8,128]{1,0:T(8,128)S(1)} %collective-permute-done.5), kind=kLoop, calls=%fused_computation | loop fusion | flops 3072 | bytes 20480 | tf_op jit(solution)/shard_map/reshape | solution.py:618
Async XLA Ops:
  4.9 8.4 %collective-permute-start.2 = (f32[136,128]{1,0:T(8,128)S(1)}, f32[136,128]{1,0:T(8,128)S(1)}, u32[]{:S(2)}, u32[]{:S(2)}) collective-permute-start(f32[136,128]{1,0:T(8,128)S(1)} %get-tuple-element.34.refs_0_), channel_id=1, source_target_pairs={{12,0},{8,4},{4,8},{0,12},{28,16},{24,20},{20,24},{16,28},{13,1},{... | collective-permute-start | bytes 208904 | tf_op jit(solution)/shard_map/ppermute | solution.py:338
  9.0 4.4 %collective-permute-start.1 = (f32[136,128]{1,0:T(8,128)S(1)}, f32[136,128]{1,0:T(8,128)S(1)}, u32[]{:S(2)}, u32[]{:S(2)}) collective-permute-start(f32[136,128]{1,0:T(8,128)S(1)} %get-tuple-element.34.refs_0_), channel_id=1, source_target_pairs={{8,0},{12,4},{0,8},{4,12},{24,16},{28,20},{16,24},{20,28},{9,1},{1... | collective-permute-start | bytes 208904 | tf_op jit(solution)/shard_map/ppermute | solution.py:338
  9.4 4.3 %collective-permute-start = (f32[136,128]{1,0:T(8,128)S(1)}, f32[136,128]{1,0:T(8,128)S(1)}, u32[]{:S(2)}, u32[]{:S(2)}) collective-permute-start(f32[136,128]{1,0:T(8,128)S(1)} %get-tuple-element.34.refs_0_), channel_id=1, source_target_pairs={{4,0},{0,4},{12,8},{8,12},{20,16},{16,20},{28,24},{24,28},{5,1},{1... | collective-permute-start | bytes 208904 | tf_op jit(solution)/shard_map/ppermute | solution.py:338
  9.6 9.0 %collective-permute-start.4 = (f32[160,128]{1,0:T(8,128)S(1)}, f32[160,128]{1,0:T(8,128)S(1)}, u32[]{:S(2)}, u32[]{:S(2)}) collective-permute-start(f32[160,128]{1,0:T(8,128)S(1)} %get-tuple-element.46), channel_id=1, source_target_pairs={{0,4},{4,8},{8,12},{12,16},{16,20},{20,24},{24,28},{1,5},{5,9},{9,... | collective-permute-start | bytes 245768 | tf_op jit(solution)/shard_map/ppermute | solution.py:572
  14.0 5.3 %collective-permute-start.3 = (f32[136,128]{1,0:T(8,128)S(1)}, f32[136,128]{1,0:T(8,128)S(1)}, u32[]{:S(2)}, u32[]{:S(2)}) collective-permute-start(f32[136,128]{1,0:T(8,128)S(1)} %get-tuple-element.35.refs_0_), channel_id=1, source_target_pairs={{16,0},{20,4},{24,8},{28,12},{0,16},{4,20},{8,24},{12,28},{17,1},{... | collective-permute-start | bytes 208904 | tf_op jit(solution)/shard_map/ppermute | solution.py:338
  20.5 3.4 %collective-permute-start.5 = (f32[8,128]{1,0:T(8,128)S(1)}, f32[8,128]{1,0:T(8,128)S(1)}, u32[]{:S(2)}, u32[]{:S(2)}) collective-permute-start(f32[8,128]{1,0:T(8,128)S(1)} %get-tuple-element.49), channel_id=1, source_target_pairs={{1,0},{0,1},{3,2},{2,3},{5,4},{4,5},{7,6},{6,7},{9,8},{8,9},{11,10... | collective-permute-start | bytes 12296 | tf_op jit(solution)/shard_map/ppermute | solution.py:338
  20.6 3.7 %collective-permute-start.6 = (f32[8,128]{1,0:T(8,128)S(1)}, f32[8,128]{1,0:T(8,128)S(1)}, u32[]{:S(2)}, u32[]{:S(2)}) collective-permute-start(f32[8,128]{1,0:T(8,128)S(1)} %get-tuple-element.50), channel_id=1, source_target_pairs={{2,0},{3,1},{0,2},{1,3},{6,4},{7,5},{4,6},{5,7},{10,8},{11,9},{8,1... | collective-permute-start | bytes 12296 | tf_op jit(solution)/shard_map/ppermute | solution.py:338
  22.1 3.0 %collective-permute-start.7 = (f32[8,128]{1,0:T(8,128)S(1)}, f32[8,128]{1,0:T(8,128)S(1)}, u32[]{:S(2)}, u32[]{:S(2)}) collective-permute-start(f32[8,128]{1,0:T(8,128)S(1)} %get-tuple-element.51), channel_id=1, source_target_pairs={{3,0},{2,1},{1,2},{0,3},{7,4},{6,5},{5,6},{4,7},{11,8},{10,9},{9,1... | collective-permute-start | bytes 12296 | tf_op jit(solution)/shard_map/ppermute | solution.py:338

commit v7 on v6

--- a/solution.py
+++ b/solution.py
@@ -20,7 +20,7 @@
 )
 VMEM_BYTES = 20 << 20
 GROUP = 16
-CHUNK = 8
+CHUNK = 32
 
 
 def take(values, index):
@@ -415,7 +415,7 @@
         part_ref[row, :] = own_part_ref[row, :] + jnp.sum(total, axis=0, keepdims=True)
         return carry
 
-    lax.fori_loop(0, blocks, one_block, 0, unroll=16)
+    lax.fori_loop(0, blocks, one_block, 0, unroll=32)
 
     rows = inlet_rows_ref[...]
     slope_new, slope_old, _, _ = slopes_of(rows[steps:steps + 1])
@@ -565,9 +565,9 @@
     inner = ()
     radices = radices_of(count)
     for turn, radix in enumerate(radices[:-1]):
-        received = [message] + [
-            exchange(message, "net", stride, radix, offset) for offset in range(1, radix)
-        ]
+        received = [message]
+        for offset in range(1, radix):
+            received.append(exchange(message, "net", stride, radix, offset))
         if turn == 0:
             arriving = lax.ppermute(leaving, "net", [(i, i + 1) for i in range(count - 1)])
         later, message = call(
@@ -614,7 +614,8 @@
     total = pieces[0]
     for offset in range(1, ranks):
         back = offset if is_power(ranks) else ranks - offset
-        total = total + exchange(pieces[offset], "mem", 1, ranks, back)
+        arrived = exchange(pieces[offset], "mem", 1, ranks, back)
+        total = total + arrived
     return grad_lateral, total.reshape(-1)
 
 

time: 26 us -> 25.5 us (0.981)
  Pallas kernels: 9.2 us -> 8.78 us
    pallas_call x1, Pallas kernels: 1.2 us -> 0.92 us  [gradients(): call(functools.partial(sums_kernel, steps, members, blocks, ranks, stride...]
  transfers between devices with their start and end apart: 8 -> 8, of which waited for: 4 -> 4; matrix products, arithmetic and copies ran while one was open for 0% -> 0% of each run, Pallas kernels for 14% -> 15%
where the time goes in v7:
time: 25.5 us; the launch traced here: 25.3 us
  starting transfers between devices  13 us (51%)
  Pallas kernels  8.78 us (34%)
  waiting for transfers between devices  2.25 us (9%)
  between operations  0.73 us (3%)
  other arithmetic  0.6 us (2%)
    ppermute x7, starting transfers between devices, exchange(): return lax.ppermute(value, axis, pairs)  9.26 us
    ppermute x1, starting transfers between devices, gradients(): lax.ppermute(leaving, 'net', [(i, i + 1) for i in range(count - 1)])  3.73 us
    pallas_call x1, Pallas kernels, gradients(): call(functools.partial(fetch_kernel, steps, members, blocks, len(inputs))...  2.41 us
    ppermute x7, waiting for transfers between devices, exchange(): return lax.ppermute(value, axis, pairs)  2.25 us
    pallas_call x1, Pallas kernels, gradients(): call(functools.partial(weight_kernel, steps, members, blocks), (shape((st...  1.96 us
    pallas_call x1, Pallas kernels, gradients(): call(functools.partial(local_kernel, steps, members, blocks), (shape((ste...  1.71 us
    pallas_call x1, Pallas kernels, gradients(): call(functools.partial(grad_kernel, steps, members, blocks, chunks), shap...  1.5 us
    pallas_call x1, Pallas kernels, gradients(): call(functools.partial(sums_kernel, steps, members, blocks, ranks, stride...  0.92 us
  transfers between devices with their start and end apart: 8, of which 4 were waited for; matrix products, arithmetic and copies ran while one was open for 0% of the time, Pallas kernels for 15%

profile of v7, /device:TPU:0, one launch (start us, length us, event | category | flops | bytes accessed | tf_op | source)
XLA Modules:
  0.0 25.3 jit_solution(16934469472239825998)
XLA Ops:
  0.6 2.4 %shard_map.104 = (bf16[5,32,4096]{2,1,0:T(8,128)(2,1)S(1)}, s32[32,128]{1,0:T(8,128)S(1)}, f32[32,128]{1,0:T(8,128)S(1)}, f32[32,128]{1,0:T(8,128)S(1)}, s32[32,...) custom-call(bf16[5,32,4096]{2,1,0:T(8,128)(2,1)} %refs_0_.1, ...), custom_call_target="tpu_custom_call" | custom-call | flops 134217728 | bytes 4718592 | tf_op jit(solution)/shard_map/pallas_call | solution.py:527
  3.1 1.7 %shard_map.105 = (f32[4,32,4096]{2,1,0:T(8,128)S(1)}, f32[136,128]{1,0:T(8,128)S(1)}, f32[4,32,128]{2,1,0:T(8,128)S(1)}, s32[32,128]{1,0:T(8,128)S(1)}, f32[128,...) custom-call(bf16[4,32,4096]{2,1,0:T(8,128)(2,1)S(1)} %get-tuple-element.27.cot_ref, ...), custom_call_target="tpu_custom_call" | custom-call | flops 536870912 | bytes 3145728 | tf_op jit(solution)/shard_map/pallas_call | solution.py:539
  4.8 4.0 %collective-permute-start.2 = (f32[136,128]{1,0:T(8,128)S(1)}, f32[136,128]{1,0:T(8,128)S(1)}, u32[]{:S(2)}, u32[]{:S(2)}) collective-permute-start(f32[136,128]{1,0:T(8,128)S(1)} %get-tuple-element.34.refs_0_), channel_id=1, source_target_pairs={{12,0},{8,4},{4,8},{0,12},{28,16},{24,20},{20,24},{16,28},{13,1},{... | collective-permute-start | bytes 208904 | tf_op jit(solution)/shard_map/ppermute | solution.py:338
  8.8 0.5 %collective-permute-start.1 = (f32[136,128]{1,0:T(8,128)S(1)}, f32[136,128]{1,0:T(8,128)S(1)}, u32[]{:S(2)}, u32[]{:S(2)}) collective-permute-start(f32[136,128]{1,0:T(8,128)S(1)} %get-tuple-element.34.refs_0_), channel_id=1, source_target_pairs={{8,0},{12,4},{0,8},{4,12},{24,16},{28,20},{16,24},{20,28},{9,1},{1... | collective-permute-start | bytes 208904 | tf_op jit(solution)/shard_map/ppermute | solution.py:338
  9.3 0.2 collective-permute-start
  9.5 3.7 %collective-permute-start.4 = (f32[160,128]{1,0:T(8,128)S(1)}, f32[160,128]{1,0:T(8,128)S(1)}, u32[]{:S(2)}, u32[]{:S(2)}) collective-permute-start(f32[160,128]{1,0:T(8,128)S(1)} %get-tuple-element.46), channel_id=1, source_target_pairs={{0,4},{4,8},{8,12},{12,16},{16,20},{20,24},{24,28},{1,5},{5,9},{9,... | collective-permute-start | bytes 245768 | tf_op jit(solution)/shard_map/ppermute | solution.py:572
  13.2 0.0 collective-permute-done.2.refs_3_
  13.2 0.0 collective-permute-done.1.refs_2_
  13.2 0.4 %collective-permute-done.refs_1_ = f32[136,128]{1,0:T(8,128)S(1)} collective-permute-done((f32[136,128]{1,0:T(8,128)S(1)}, f32[136,128]{1,0:T(8,128)S(1)}, u32[]{:S(2)}, u32[]{:S(2)}) %collective-permute-start) | collective-permute-done | bytes 69664 | tf_op jit(solution)/shard_map/ppermute | solution.py:338
  13.6 0.3 %shard_map.106 = (f32[136,128]{1,0:T(8,128)S(1)}, f32[136,128]{1,0:T(8,128)S(1)}) custom-call(f32[136,128]{1,0:T(8,128)S(1)} %get-tuple-element.34.refs_0_, f32[136,128]{1,0:T(8,128)S(1)} %collective-permute-done.refs_1_, f32[136,128]{1,0:T(8,128)S(1)} %collective-permute-done.1.refs_2_, f32[136,128]{1,0:T(8,128)S(1)} %collective-permute-done.2.refs_3_), custom_call_target="tpu_custom_call" | custom-call | flops 1392640 | bytes 278528 | tf_op jit(solution)/shard_map/pallas_call | solution.py:573
  13.9 2.7 %collective-permute-start.3 = (f32[136,128]{1,0:T(8,128)S(1)}, f32[136,128]{1,0:T(8,128)S(1)}, u32[]{:S(2)}, u32[]{:S(2)}) collective-permute-start(f32[136,128]{1,0:T(8,128)S(1)} %get-tuple-element.35.refs_0_), channel_id=1, source_target_pairs={{16,0},{20,4},{24,8},{28,12},{0,16},{4,20},{8,24},{12,28},{17,1},{... | collective-permute-start | bytes 208904 | tf_op jit(solution)/shard_map/ppermute | solution.py:338
  16.5 2.0 %shard_map.107 = (f32[4,32,4096]{2,1,0:T(8,128)S(1)}, f32[32,128]{1,0:T(8,128)S(1)}) custom-call(bf16[5,32,4096]{2,1,0:T(8,128)(2,1)S(1)} %get-tuple-element.38.flow_ref, bf16[4,32,4096]{2,1,0:T(8,128)(2,1)S(1)} %get-tuple-element.39.lateral_ref, f32[4,32,4096]{2,1,0:T(8,128)S(1)} %get-tuple-element.40.own_ref, ...), custom_call_target="tpu_custom_call" | custom-call | flops 134217728 | bytes 4194304 | tf_op jit(solution)/shard_map/pallas_call | solution.py:556
  18.5 0.0 collective-permute-done.4.refs_9_
  18.5 0.6 %collective-permute-done.3.refs_1_ = f32[136,128]{1,0:T(8,128)S(1)} collective-permute-done((f32[136,128]{1,0:T(8,128)S(1)}, f32[136,128]{1,0:T(8,128)S(1)}, u32[]{:S(2)}, u32[]{:S(2)}) %collective-permute-start.3) | collective-permute-done | bytes 69664 | tf_op jit(solution)/shard_map/ppermute | solution.py:338
  19.1 0.9 %shard_map.108 = (f32[128,128]{1,0:T(8,128)S(1)}, f32[8,128]{1,0:T(8,128)S(1)}, f32[8,128]{1,0:T(8,128)S(1)}, f32[8,128]{1,0:T(8,128)S(1)}, f32[8,128]{1,0:T(8,128)S(1)}) custom-call(f32[136,128]{1,0:T(8,128)S(1)} %get-tuple-element.35.refs_0_, f32[136,128]{1,0:T(8,128)S(1)} %collective-permute-done.3.refs_1_, f32[136,128]{1,0:T(8,128)S(1)} %get-tuple-element.36.refs_2_, ...), custom_call_target="tpu_custom_call" | custom-call | flops 10485760 | bytes 2097152 | tf_op jit(solution)/shard_map/pallas_call | solution.py:589
  20.1 0.1 collective-permute-start.5
  20.1 1.6 %collective-permute-start.6 = (f32[8,128]{1,0:T(8,128)S(1)}, f32[8,128]{1,0:T(8,128)S(1)}, u32[]{:S(2)}, u32[]{:S(2)}) collective-permute-start(f32[8,128]{1,0:T(8,128)S(1)} %get-tuple-element.50), channel_id=1, source_target_pairs={{2,0},{3,1},{0,2},{1,3},{6,4},{7,5},{4,6},{5,7},{10,8},{11,9},{8,1... | collective-permute-start | bytes 12296 | tf_op jit(solution)/shard_map/ppermute | solution.py:338
  21.7 0.3 %collective-permute-start.7 = (f32[8,128]{1,0:T(8,128)S(1)}, f32[8,128]{1,0:T(8,128)S(1)}, u32[]{:S(2)}, u32[]{:S(2)}) collective-permute-start(f32[8,128]{1,0:T(8,128)S(1)} %get-tuple-element.51), channel_id=1, source_target_pairs={{3,0},{2,1},{1,2},{0,3},{7,4},{6,5},{5,6},{4,7},{11,8},{10,9},{9,1... | collective-permute-start | bytes 12296 | tf_op jit(solution)/shard_map/ppermute | solution.py:338
  22.0 1.5 %shard_map.109 = bf16[4,32,4096]{2,1,0:T(8,128)(2,1)} custom-call(f32[128,128]{1,0:T(8,128)S(1)} %get-tuple-element.47.incoming_ref, f32[4,32,4096]{2,1,0:T(8,128)S(1)} %get-tuple-element.40.own_ref, f32[4,32,128]{2,1,0:T(8,128)S(1)} %get-tuple-element.41.response_ref, s32[32,128]{1,0:T(8,128)S(1)} %get-tuple-element.37.refs_3_.slot_ref, ...), custom_call_target="tpu_custom_call" | custom-call | flops 15728640 | bytes 3145728 | tf_op jit(solution)/shard_map/pallas_call | solution.py:602
  23.5 0.0 collective-permute-done.5
  23.5 0.3 %collective-permute-done.6 = f32[8,128]{1,0:T(8,128)S(1)} collective-permute-done((f32[8,128]{1,0:T(8,128)S(1)}, f32[8,128]{1,0:T(8,128)S(1)}, u32[]{:S(2)}, u32[]{:S(2)}) %collective-permute-start.6) | collective-permute-done | bytes 4128 | tf_op jit(solution)/shard_map/ppermute | solution.py:338
  23.8 0.9 %collective-permute-done.7 = f32[8,128]{1,0:T(8,128)S(1)} collective-permute-done((f32[8,128]{1,0:T(8,128)S(1)}, f32[8,128]{1,0:T(8,128)S(1)}, u32[]{:S(2)}, u32[]{:S(2)}) %collective-permute-start.7) | collective-permute-done | bytes 4128 | tf_op jit(solution)/shard_map/ppermute | solution.py:338
  24.8 0.6 %add_bitcast_fusion = f32[1024]{0:T(1024)} fusion(f32[8,128]{1,0:T(8,128)S(1)} %collective-permute-done.7, f32[8,128]{1,0:T(8,128)S(1)} %collective-permute-done.6, f32[8,128]{1,0:T(8,128)S(1)} %get-tuple-element.48, f32[8,128]{1,0:T(8,128)S(1)} %collective-permute-done.5), kind=kLoop, calls=%fused_computation | loop fusion | flops 3072 | bytes 20480 | tf_op jit(solution)/shard_map/reshape | solution.py:619
Async XLA Ops:
  4.8 8.4 %collective-permute-start.2 = (f32[136,128]{1,0:T(8,128)S(1)}, f32[136,128]{1,0:T(8,128)S(1)}, u32[]{:S(2)}, u32[]{:S(2)}) collective-permute-start(f32[136,128]{1,0:T(8,128)S(1)} %get-tuple-element.34.refs_0_), channel_id=1, source_target_pairs={{12,0},{8,4},{4,8},{0,12},{28,16},{24,20},{20,24},{16,28},{13,1},{... | collective-permute-start | bytes 208904 | tf_op jit(solution)/shard_map/ppermute | solution.py:338
  8.8 4.4 %collective-permute-start.1 = (f32[136,128]{1,0:T(8,128)S(1)}, f32[136,128]{1,0:T(8,128)S(1)}, u32[]{:S(2)}, u32[]{:S(2)}) collective-permute-start(f32[136,128]{1,0:T(8,128)S(1)} %get-tuple-element.34.refs_0_), channel_id=1, source_target_pairs={{8,0},{12,4},{0,8},{4,12},{24,16},{28,20},{16,24},{20,28},{9,1},{1... | collective-permute-start | bytes 208904 | tf_op jit(solution)/shard_map/ppermute | solution.py:338
  9.3 4.3 %collective-permute-start = (f32[136,128]{1,0:T(8,128)S(1)}, f32[136,128]{1,0:T(8,128)S(1)}, u32[]{:S(2)}, u32[]{:S(2)}) collective-permute-start(f32[136,128]{1,0:T(8,128)S(1)} %get-tuple-element.34.refs_0_), channel_id=1, source_target_pairs={{4,0},{0,4},{12,8},{8,12},{20,16},{16,20},{28,24},{24,28},{5,1},{1... | collective-permute-start | bytes 208904 | tf_op jit(solution)/shard_map/ppermute | solution.py:338
  9.5 9.0 %collective-permute-start.4 = (f32[160,128]{1,0:T(8,128)S(1)}, f32[160,128]{1,0:T(8,128)S(1)}, u32[]{:S(2)}, u32[]{:S(2)}) collective-permute-start(f32[160,128]{1,0:T(8,128)S(1)} %get-tuple-element.46), channel_id=1, source_target_pairs={{0,4},{4,8},{8,12},{12,16},{16,20},{20,24},{24,28},{1,5},{5,9},{9,... | collective-permute-start | bytes 245768 | tf_op jit(solution)/shard_map/ppermute | solution.py:572
  13.9 5.3 %collective-permute-start.3 = (f32[136,128]{1,0:T(8,128)S(1)}, f32[136,128]{1,0:T(8,128)S(1)}, u32[]{:S(2)}, u32[]{:S(2)}) collective-permute-start(f32[136,128]{1,0:T(8,128)S(1)} %get-tuple-element.35.refs_0_), channel_id=1, source_target_pairs={{16,0},{20,4},{24,8},{28,12},{0,16},{4,20},{8,24},{12,28},{17,1},{... | collective-permute-start | bytes 208904 | tf_op jit(solution)/shard_map/ppermute | solution.py:338
  20.1 3.4 %collective-permute-start.5 = (f32[8,128]{1,0:T(8,128)S(1)}, f32[8,128]{1,0:T(8,128)S(1)}, u32[]{:S(2)}, u32[]{:S(2)}) collective-permute-start(f32[8,128]{1,0:T(8,128)S(1)} %get-tuple-element.49), channel_id=1, source_target_pairs={{1,0},{0,1},{3,2},{2,3},{5,4},{4,5},{7,6},{6,7},{9,8},{8,9},{11,10... | collective-permute-start | bytes 12296 | tf_op jit(solution)/shard_map/ppermute | solution.py:338
  20.1 3.7 %collective-permute-start.6 = (f32[8,128]{1,0:T(8,128)S(1)}, f32[8,128]{1,0:T(8,128)S(1)}, u32[]{:S(2)}, u32[]{:S(2)}) collective-permute-start(f32[8,128]{1,0:T(8,128)S(1)} %get-tuple-element.50), channel_id=1, source_target_pairs={{2,0},{3,1},{0,2},{1,3},{6,4},{7,5},{4,6},{5,7},{10,8},{11,9},{8,1... | collective-permute-start | bytes 12296 | tf_op jit(solution)/shard_map/ppermute | solution.py:338
  21.7 3.0 %collective-permute-start.7 = (f32[8,128]{1,0:T(8,128)S(1)}, f32[8,128]{1,0:T(8,128)S(1)}, u32[]{:S(2)}, u32[]{:S(2)}) collective-permute-start(f32[8,128]{1,0:T(8,128)S(1)} %get-tuple-element.51), channel_id=1, source_target_pairs={{3,0},{2,1},{1,2},{0,3},{7,4},{6,5},{5,6},{4,7},{11,8},{10,9},{9,1... | collective-permute-start | bytes 12296 | tf_op jit(solution)/shard_map/ppermute | solution.py:338

commit v8 on v7

--- a/solution.py
+++ b/solution.py
@@ -276,7 +276,7 @@
     return (lax.axis_index(axis) // stride) % radix
 
 
-def group_kernel(steps, members, axis, stride, radix, has_inner, *refs):
+def group_kernel(steps, members, axis, stride, radix, has_inner, values_only, *refs):
     messages = refs[:radix]
     inner = refs[radix] if has_inner else None
     outs = refs[radix + has_inner:]
@@ -296,7 +296,11 @@
             if has_inner:
                 later = compose(steps, members, read_message(steps, members, inner), later)
             write_message(steps, members, outs[0], later)
-            write_message(steps, members, outs[1], total)
+            if values_only:
+                for step in range(steps):
+                    outs[1][pl.ds(step * members, members), :] = total[0][step]
+            else:
+                write_message(steps, members, outs[1], total)
 
 
 def last_round(steps, members, axis, stride, radix, messages, inner, out):
@@ -306,10 +310,11 @@
         def _(mine=mine):
             value = [jnp.zeros((members, LANES), F32)] * steps
             for other in reversed(range(mine + 1, radix)):
-                message = read_message(steps, members, messages[source_of(mine, other, radix)])
+                source = messages[source_of(mine, other, radix)]
                 if other == radix - 1:
-                    value = message[0]
+                    value = [source[pl.ds(step * members, members), :] for step in range(steps)]
                 else:
+                    message = read_message(steps, members, source)
                     value = compose(steps, members, message, (value, None, None))[0]
             if inner is not None:
                 within = read_message(steps, members, inner)
@@ -570,9 +575,15 @@
             received.append(exchange(message, "net", stride, radix, offset))
         if turn == 0:
             arriving = lax.ppermute(leaving, "net", [(i, i + 1) for i in range(count - 1)])
+        values_only = turn == len(radices) - 2 and radices[-1] == 2
         later, message = call(
-            functools.partial(group_kernel, steps, members, "net", stride, radix, len(inner)),
-            (shape((rows, LANES), F32),) * 2,
+            functools.partial(
+                group_kernel, steps, members, "net", stride, radix, len(inner), values_only
+            ),
+            (
+                shape((rows, LANES), F32),
+                shape((steps * members if values_only else rows, LANES), F32),
+            ),
             flops=20 * radix * rows * LANES,
             size=4 * radix * rows * LANES,
         )(*received, *inner)

time: 25.5 us -> 25.5 us (level)
  no operation moved by 1% of the time
where the time goes in v8:
time: 25.5 us; the launch traced here: 25.3 us
  starting transfers between devices  13 us (51%)
  Pallas kernels  8.75 us (34%)
  waiting for transfers between devices  2.23 us (9%)
  between operations  0.73 us (3%)
  other arithmetic  0.6 us (2%)
    ppermute x7, starting transfers between devices, exchange(): return lax.ppermute(value, axis, pairs)  9.26 us
    ppermute x1, starting transfers between devices, gradients(): lax.ppermute(leaving, 'net', [(i, i + 1) for i in range(count - 1)])  3.73 us
    pallas_call x1, Pallas kernels, gradients(): call(functools.partial(fetch_kernel, steps, members, blocks, len(inputs))...  2.41 us
    ppermute x7, waiting for transfers between devices, exchange(): return lax.ppermute(value, axis, pairs)  2.23 us
    pallas_call x1, Pallas kernels, gradients(): call(functools.partial(weight_kernel, steps, members, blocks), (shape((st...  1.96 us
    pallas_call x1, Pallas kernels, gradients(): call(functools.partial(local_kernel, steps, members, blocks), (shape((ste...  1.71 us
    pallas_call x1, Pallas kernels, gradients(): call(functools.partial(grad_kernel, steps, members, blocks, chunks), shap...  1.49 us
    pallas_call x1, Pallas kernels, gradients(): call(functools.partial(sums_kernel, steps, members, blocks, ranks, stride...  0.91 us
  transfers between devices with their start and end apart: 8, of which 4 were waited for; matrix products, arithmetic and copies ran while one was open for 0% of the time, Pallas kernels for 15%

profile of v8, /device:TPU:0, one launch (start us, length us, event | category | flops | bytes accessed | tf_op | source)
XLA Modules:
  0.0 25.3 jit_solution(8220538901233800987)
XLA Ops:
  0.6 2.4 %shard_map.104 = (bf16[5,32,4096]{2,1,0:T(8,128)(2,1)S(1)}, s32[32,128]{1,0:T(8,128)S(1)}, f32[32,128]{1,0:T(8,128)S(1)}, f32[32,128]{1,0:T(8,128)S(1)}, s32[32,...) custom-call(bf16[5,32,4096]{2,1,0:T(8,128)(2,1)} %refs_0_.1, ...), custom_call_target="tpu_custom_call" | custom-call | flops 134217728 | bytes 4718592 | tf_op jit(solution)/shard_map/pallas_call | solution.py:532
  3.1 1.7 %shard_map.105 = (f32[4,32,4096]{2,1,0:T(8,128)S(1)}, f32[136,128]{1,0:T(8,128)S(1)}, f32[4,32,128]{2,1,0:T(8,128)S(1)}, s32[32,128]{1,0:T(8,128)S(1)}, f32[128,...) custom-call(bf16[4,32,4096]{2,1,0:T(8,128)(2,1)S(1)} %get-tuple-element.27.cot_ref, ...), custom_call_target="tpu_custom_call" | custom-call | flops 536870912 | bytes 3145728 | tf_op jit(solution)/shard_map/pallas_call | solution.py:544
  4.8 4.0 %collective-permute-start.2 = (f32[136,128]{1,0:T(8,128)S(1)}, f32[136,128]{1,0:T(8,128)S(1)}, u32[]{:S(2)}, u32[]{:S(2)}) collective-permute-start(f32[136,128]{1,0:T(8,128)S(1)} %get-tuple-element.34.refs_0_), channel_id=1, source_target_pairs={{12,0},{8,4},{4,8},{0,12},{28,16},{24,20},{20,24},{16,28},{13,1},{... | collective-permute-start | bytes 208904 | tf_op jit(solution)/shard_map/ppermute | solution.py:343
  8.8 0.5 %collective-permute-start.1 = (f32[136,128]{1,0:T(8,128)S(1)}, f32[136,128]{1,0:T(8,128)S(1)}, u32[]{:S(2)}, u32[]{:S(2)}) collective-permute-start(f32[136,128]{1,0:T(8,128)S(1)} %get-tuple-element.34.refs_0_), channel_id=1, source_target_pairs={{8,0},{12,4},{0,8},{4,12},{24,16},{28,20},{16,24},{20,28},{9,1},{1... | collective-permute-start | bytes 208904 | tf_op jit(solution)/shard_map/ppermute | solution.py:343
  9.3 0.2 collective-permute-start
  9.5 3.7 %collective-permute-start.4 = (f32[160,128]{1,0:T(8,128)S(1)}, f32[160,128]{1,0:T(8,128)S(1)}, u32[]{:S(2)}, u32[]{:S(2)}) collective-permute-start(f32[160,128]{1,0:T(8,128)S(1)} %get-tuple-element.46), channel_id=1, source_target_pairs={{0,4},{4,8},{8,12},{12,16},{16,20},{20,24},{24,28},{1,5},{5,9},{9,... | collective-permute-start | bytes 245768 | tf_op jit(solution)/shard_map/ppermute | solution.py:577
  13.2 0.0 collective-permute-done.2.refs_3_
  13.2 0.0 collective-permute-done.1.refs_2_
  13.2 0.4 %collective-permute-done.refs_1_ = f32[136,128]{1,0:T(8,128)S(1)} collective-permute-done((f32[136,128]{1,0:T(8,128)S(1)}, f32[136,128]{1,0:T(8,128)S(1)}, u32[]{:S(2)}, u32[]{:S(2)}) %collective-permute-start) | collective-permute-done | bytes 69664 | tf_op jit(solution)/shard_map/ppermute | solution.py:343
  13.6 0.3 %shard_map.106 = (f32[136,128]{1,0:T(8,128)S(1)}, f32[128,128]{1,0:T(8,128)S(1)}) custom-call(f32[136,128]{1,0:T(8,128)S(1)} %get-tuple-element.34.refs_0_, f32[136,128]{1,0:T(8,128)S(1)} %collective-permute-done.refs_1_, f32[136,128]{1,0:T(8,128)S(1)} %collective-permute-done.1.refs_2_, f32[136,128]{1,0:T(8,128)S(1)} %collective-permute-done.2.refs_3_), custom_call_target="tpu_custom_call" | custom-call | flops 1392640 | bytes 278528 | tf_op jit(solution)/shard_map/pallas_call | solution.py:579
  13.9 2.7 %collective-permute-start.3 = (f32[128,128]{1,0:T(8,128)S(1)}, f32[128,128]{1,0:T(8,128)S(1)}, u32[]{:S(2)}, u32[]{:S(2)}) collective-permute-start(f32[128,128]{1,0:T(8,128)S(1)} %get-tuple-element.35.refs_0_), channel_id=1, source_target_pairs={{16,0},{20,4},{24,8},{28,12},{0,16},{4,20},{8,24},{12,28},{17,1},{... | collective-permute-start | bytes 196616 | tf_op jit(solution)/shard_map/ppermute | solution.py:343
  16.5 2.0 %shard_map.107 = (f32[4,32,4096]{2,1,0:T(8,128)S(1)}, f32[32,128]{1,0:T(8,128)S(1)}) custom-call(bf16[5,32,4096]{2,1,0:T(8,128)(2,1)S(1)} %get-tuple-element.38.flow_ref, bf16[4,32,4096]{2,1,0:T(8,128)(2,1)S(1)} %get-tuple-element.39.lateral_ref, f32[4,32,4096]{2,1,0:T(8,128)S(1)} %get-tuple-element.40.own_ref, ...), custom_call_target="tpu_custom_call" | custom-call | flops 134217728 | bytes 4194304 | tf_op jit(solution)/shard_map/pallas_call | solution.py:561
  18.5 0.0 collective-permute-done.4.refs_9_
  18.5 0.6 %collective-permute-done.3.refs_1_ = f32[128,128]{1,0:T(8,128)S(1)} collective-permute-done((f32[128,128]{1,0:T(8,128)S(1)}, f32[128,128]{1,0:T(8,128)S(1)}, u32[]{:S(2)}, u32[]{:S(2)}) %collective-permute-start.3) | collective-permute-done | bytes 65568 | tf_op jit(solution)/shard_map/ppermute | solution.py:343
  19.1 0.9 %shard_map.108 = (f32[128,128]{1,0:T(8,128)S(1)}, f32[8,128]{1,0:T(8,128)S(1)}, f32[8,128]{1,0:T(8,128)S(1)}, f32[8,128]{1,0:T(8,128)S(1)}, f32[8,128]{1,0:T(8,128)S(1)}) custom-call(f32[128,128]{1,0:T(8,128)S(1)} %get-tuple-element.35.refs_0_, f32[128,128]{1,0:T(8,128)S(1)} %collective-permute-done.3.refs_1_, f32[136,128]{1,0:T(8,128)S(1)} %get-tuple-element.36.refs_2_, ...), custom_call_target="tpu_custom_call" | custom-call | flops 10485760 | bytes 2097152 | tf_op jit(solution)/shard_map/pallas_call | solution.py:600
  20.0 0.1 collective-permute-start.5
  20.1 1.6 %collective-permute-start.6 = (f32[8,128]{1,0:T(8,128)S(1)}, f32[8,128]{1,0:T(8,128)S(1)}, u32[]{:S(2)}, u32[]{:S(2)}) collective-permute-start(f32[8,128]{1,0:T(8,128)S(1)} %get-tuple-element.50), channel_id=1, source_target_pairs={{2,0},{3,1},{0,2},{1,3},{6,4},{7,5},{4,6},{5,7},{10,8},{11,9},{8,1... | collective-permute-start | bytes 12296 | tf_op jit(solution)/shard_map/ppermute | solution.py:343
  21.7 0.3 %collective-permute-start.7 = (f32[8,128]{1,0:T(8,128)S(1)}, f32[8,128]{1,0:T(8,128)S(1)}, u32[]{:S(2)}, u32[]{:S(2)}) collective-permute-start(f32[8,128]{1,0:T(8,128)S(1)} %get-tuple-element.51), channel_id=1, source_target_pairs={{3,0},{2,1},{1,2},{0,3},{7,4},{6,5},{5,6},{4,7},{11,8},{10,9},{9,1... | collective-permute-start | bytes 12296 | tf_op jit(solution)/shard_map/ppermute | solution.py:343
  21.9 1.5 %shard_map.109 = bf16[4,32,4096]{2,1,0:T(8,128)(2,1)} custom-call(f32[128,128]{1,0:T(8,128)S(1)} %get-tuple-element.47.incoming_ref, f32[4,32,4096]{2,1,0:T(8,128)S(1)} %get-tuple-element.40.own_ref, f32[4,32,128]{2,1,0:T(8,128)S(1)} %get-tuple-element.41.response_ref, s32[32,128]{1,0:T(8,128)S(1)} %get-tuple-element.37.refs_3_.slot_ref, ...), custom_call_target="tpu_custom_call" | custom-call | flops 15728640 | bytes 3145728 | tf_op jit(solution)/shard_map/pallas_call | solution.py:613
  23.4 0.0 collective-permute-done.5
  23.4 0.3 %collective-permute-done.6 = f32[8,128]{1,0:T(8,128)S(1)} collective-permute-done((f32[8,128]{1,0:T(8,128)S(1)}, f32[8,128]{1,0:T(8,128)S(1)}, u32[]{:S(2)}, u32[]{:S(2)}) %collective-permute-start.6) | collective-permute-done | bytes 4128 | tf_op jit(solution)/shard_map/ppermute | solution.py:343
  23.8 0.9 %collective-permute-done.7 = f32[8,128]{1,0:T(8,128)S(1)} collective-permute-done((f32[8,128]{1,0:T(8,128)S(1)}, f32[8,128]{1,0:T(8,128)S(1)}, u32[]{:S(2)}, u32[]{:S(2)}) %collective-permute-start.7) | collective-permute-done | bytes 4128 | tf_op jit(solution)/shard_map/ppermute | solution.py:343
  24.7 0.6 %add_bitcast_fusion = f32[1024]{0:T(1024)} fusion(f32[8,128]{1,0:T(8,128)S(1)} %collective-permute-done.7, f32[8,128]{1,0:T(8,128)S(1)} %collective-permute-done.6, f32[8,128]{1,0:T(8,128)S(1)} %get-tuple-element.48, f32[8,128]{1,0:T(8,128)S(1)} %collective-permute-done.5), kind=kLoop, calls=%fused_computation | loop fusion | flops 3072 | bytes 20480 | tf_op jit(solution)/shard_map/reshape | solution.py:630
Async XLA Ops:
  4.8 8.4 %collective-permute-start.2 = (f32[136,128]{1,0:T(8,128)S(1)}, f32[136,128]{1,0:T(8,128)S(1)}, u32[]{:S(2)}, u32[]{:S(2)}) collective-permute-start(f32[136,128]{1,0:T(8,128)S(1)} %get-tuple-element.34.refs_0_), channel_id=1, source_target_pairs={{12,0},{8,4},{4,8},{0,12},{28,16},{24,20},{20,24},{16,28},{13,1},{... | collective-permute-start | bytes 208904 | tf_op jit(solution)/shard_map/ppermute | solution.py:343
  8.8 4.4 %collective-permute-start.1 = (f32[136,128]{1,0:T(8,128)S(1)}, f32[136,128]{1,0:T(8,128)S(1)}, u32[]{:S(2)}, u32[]{:S(2)}) collective-permute-start(f32[136,128]{1,0:T(8,128)S(1)} %get-tuple-element.34.refs_0_), channel_id=1, source_target_pairs={{8,0},{12,4},{0,8},{4,12},{24,16},{28,20},{16,24},{20,28},{9,1},{1... | collective-permute-start | bytes 208904 | tf_op jit(solution)/shard_map/ppermute | solution.py:343
  9.3 4.3 %collective-permute-start = (f32[136,128]{1,0:T(8,128)S(1)}, f32[136,128]{1,0:T(8,128)S(1)}, u32[]{:S(2)}, u32[]{:S(2)}) collective-permute-start(f32[136,128]{1,0:T(8,128)S(1)} %get-tuple-element.34.refs_0_), channel_id=1, source_target_pairs={{4,0},{0,4},{12,8},{8,12},{20,16},{16,20},{28,24},{24,28},{5,1},{1... | collective-permute-start | bytes 208904 | tf_op jit(solution)/shard_map/ppermute | solution.py:343
  9.5 9.0 %collective-permute-start.4 = (f32[160,128]{1,0:T(8,128)S(1)}, f32[160,128]{1,0:T(8,128)S(1)}, u32[]{:S(2)}, u32[]{:S(2)}) collective-permute-start(f32[160,128]{1,0:T(8,128)S(1)} %get-tuple-element.46), channel_id=1, source_target_pairs={{0,4},{4,8},{8,12},{12,16},{16,20},{20,24},{24,28},{1,5},{5,9},{9,... | collective-permute-start | bytes 245768 | tf_op jit(solution)/shard_map/ppermute | solution.py:577
  13.9 5.2 %collective-permute-start.3 = (f32[128,128]{1,0:T(8,128)S(1)}, f32[128,128]{1,0:T(8,128)S(1)}, u32[]{:S(2)}, u32[]{:S(2)}) collective-permute-start(f32[128,128]{1,0:T(8,128)S(1)} %get-tuple-element.35.refs_0_), channel_id=1, source_target_pairs={{16,0},{20,4},{24,8},{28,12},{0,16},{4,20},{8,24},{12,28},{17,1},{... | collective-permute-start | bytes 196616 | tf_op jit(solution)/shard_map/ppermute | solution.py:343
  20.0 3.4 %collective-permute-start.5 = (f32[8,128]{1,0:T(8,128)S(1)}, f32[8,128]{1,0:T(8,128)S(1)}, u32[]{:S(2)}, u32[]{:S(2)}) collective-permute-start(f32[8,128]{1,0:T(8,128)S(1)} %get-tuple-element.49), channel_id=1, source_target_pairs={{1,0},{0,1},{3,2},{2,3},{5,4},{4,5},{7,6},{6,7},{9,8},{8,9},{11,10... | collective-permute-start | bytes 12296 | tf_op jit(solution)/shard_map/ppermute | solution.py:343
  20.1 3.7 %collective-permute-start.6 = (f32[8,128]{1,0:T(8,128)S(1)}, f32[8,128]{1,0:T(8,128)S(1)}, u32[]{:S(2)}, u32[]{:S(2)}) collective-permute-start(f32[8,128]{1,0:T(8,128)S(1)} %get-tuple-element.50), channel_id=1, source_target_pairs={{2,0},{3,1},{0,2},{1,3},{6,4},{7,5},{4,6},{5,7},{10,8},{11,9},{8,1... | collective-permute-start | bytes 12296 | tf_op jit(solution)/shard_map/ppermute | solution.py:343
  21.7 3.0 %collective-permute-start.7 = (f32[8,128]{1,0:T(8,128)S(1)}, f32[8,128]{1,0:T(8,128)S(1)}, u32[]{:S(2)}, u32[]{:S(2)}) collective-permute-start(f32[8,128]{1,0:T(8,128)S(1)} %get-tuple-element.51), channel_id=1, source_target_pairs={{3,0},{2,1},{1,2},{0,3},{7,4},{6,5},{5,6},{4,7},{11,8},{10,9},{9,1... | collective-permute-start | bytes 12296 | tf_op jit(solution)/shard_map/ppermute | solution.py:343
